TPU v7x, 256 devices: a whole 4x4x8 slice. The times are simulated.
256 devices in a mesh: wide: 32 (over z, x), narrow: 8 (over y, core).
Axes of the slice: x: 4, y: 4, z: 8, core: 2. Of those that a mesh axis runs over, the one named last changes fastest.
Arguments:
- walkers: bfloat16 [512, 768, 128], P('wide', 'narrow'), may hold values from -6 to 6
- intersection_inverse: bfloat16 [512, 128, 128], P('wide')
- noise: bfloat16 [512, 1024], P('wide'), may hold values from -6 to 6
- half_cholesky: bfloat16 [128, 768, 1024], P('wide', 'narrow'), may hold values from -0.25 to 0.25
- cholesky: bfloat16 [768, 768, 1024], P('narrow', 'wide'), may hold values from -0.1875 to 0.1875
- comb_source: int32 [512], P('wide'), may hold values from 0 to 511, as said below
Outputs:
- new_walkers: bfloat16 [512, 768, 128], P('wide', 'narrow')
- force_bias: float32 [512, 1024], P(('wide', 'narrow'))
Inputs may be any that keep to these rules, and one draw needn't show every extreme that they name: comb_source[j] lies in the block of 16 slots that holds j or in one of the two blocks beside it; within each block the sources never fall; every block but the first copies some walker of the block before it, and every block but the last some walker of the block after it.
All inputs are finite; a program needn't handle non-finite values.
Results may differ from a plain program's by a relative error of at most 0.0085.
Values may be sent and summed in bfloat16 or wider, within the bound.
No kernel may reach another device: no remote copies, remote signals or barrier semaphores. Data moves between devices by JAX's collectives and lax.ppermute only.
A program may use at most 128 MiB of HBM per device.

v0:
```python
import math

import jax
import jax.numpy as jnp
from jax import lax
from jax.sharding import PartitionSpec as P

time_step = 0.01


def padded_2(array, sides, width):
    for axis, dim in sides:
        count, length = (lax.axis_size(axis), array.shape[dim])
        up = [(i, (i + 1) % count) for i in range(count - 1)]
        down = [(j, i) for i, j in up]
        last = lax.slice_in_dim(array, length - width, length, axis=dim)
        leading = lax.slice_in_dim(array, 0, width, axis=dim)
        before = lax.ppermute(last, axis, up)
        after = lax.ppermute(leading, axis, down)
        array = jnp.concatenate([before, array, after], axis=dim)
    return array


def per_device(walkers, intersection_inverse, noise, half_cholesky, cholesky, comb_source):
    walk_local, row_count, electrons = walkers.shape
    col_count = cholesky.shape[1]
    vectors = cholesky.shape[2]
    wide_count = lax.axis_size("wide")
    narrow_count = lax.axis_size("narrow")
    root_step = math.sqrt(time_step)
    rotated = jnp.einsum(
        "wiq,wqp->wpi", walkers, intersection_inverse, preferred_element_type=jnp.float32
    ).astype(jnp.bfloat16)
    rotated = rotated.reshape(walk_local, electrons * row_count)
    pair_block = lax.all_to_all(rotated, "wide", split_axis=1, concat_axis=0, tiled=True)
    partial_bias = jnp.dot(
        pair_block, half_cholesky.reshape(-1, vectors), preferred_element_type=jnp.float32
    )
    share_rows = walk_local // narrow_count
    summed_bias = lax.psum(partial_bias, ("wide", "narrow"))
    all_noise = lax.all_gather(noise, "wide", axis=0, tiled=True)
    aux_field = (root_step * all_noise.astype(jnp.float32) + time_step * summed_bias).astype(
        jnp.bfloat16
    )
    position = lax.axis_index("wide") * narrow_count + lax.axis_index("narrow")
    force_bias = lax.dynamic_slice_in_dim(summed_bias, position * share_rows, share_rows, 0)
    flat_chol = cholesky.reshape(row_count * col_count, vectors)
    operator_part = lax.dot_general(
        aux_field, flat_chol, (((1,), (1,)), ((), ())), preferred_element_type=jnp.float32
    ).astype(jnp.bfloat16)
    operator = lax.all_to_all(operator_part, "wide", split_axis=0, concat_axis=1, tiled=True)
    operator = operator.reshape(walk_local, wide_count, row_count, col_count)
    summed = walkers.astype(jnp.float32)
    current = walkers
    for degree in range(1, 5):
        rows_in = lax.all_gather(current, "narrow", axis=1, tiled=True)
        blocks = rows_in.shape[1] // col_count
        shaped = rows_in.reshape(walk_local, blocks, col_count, electrons)
        product = jnp.einsum(
            "waij,waje->wie", operator, shaped, preferred_element_type=jnp.float32
        ) / float(degree)
        if degree < 4:
            current = product.astype(jnp.bfloat16)
            summed = summed + current.astype(jnp.float32)
        else:
            summed = summed + product
    propagated = summed.astype(jnp.bfloat16)
    padded = padded_2(propagated, (("wide", 0),), walk_local)
    offset = comb_source - (lax.axis_index("wide") - 1) * walk_local
    new_walkers = jnp.take(padded, offset, axis=0)
    return (new_walkers, force_bias)


def solution(mesh):
    in_specs = (
        P("wide", "narrow", None),
        P("wide", None, None),
        P("wide", None),
        P("wide", "narrow", None),
        P("narrow", "wide", None),
        P("wide"),
    )
    out_specs = (P("wide", "narrow", None), P(("wide", "narrow"), None))
    return jax.shard_map(
        per_device, mesh=mesh, in_specs=in_specs, out_specs=out_specs, check_vma=False
    )
```

profile of v0, /device:TPU:1, one launch (start us, length us, event | category | flops | bytes accessed | tf_op | source)
XLA Modules:
  0.0 535.9 jit_solution(598549826143370649)
XLA Ops:
  8.0 0.0 copy-start
  8.0 0.0 all-reduce.2.cloned.1.call-start
  8.1 1.5 convolution_convert_fusion.1
  9.6 0.3 copy.22
  9.9 0.4 all_to_all.26
  10.2 0.1 copy.23
  10.4 25.5 %all_to_all.35 = bf16[16,32,384]{2,0,1:T(8,128)(2,1)S(1)} all-to-all(bf16[16,32,384]{2,0,1:T(8,128)(2,1)S(1)} %copy.23), channel_id=1, replica_groups=mesh['wide'=32,'narrow'=8] {'wide'}, dimensions={1} | all-to-all | bytes 786432 | tf_op jit(solution)/shard_map/all_to_all | solution.py:35
  35.8 0.0 copy-done
  35.8 2.0 fusion.12
  37.9 0.0 all-reduce.2.cloned.1.call-update
  37.9 0.0 all-gather.6.cloned.1.call-start
  38.0 0.5 all-gather.6.cloned.1.call-update
  38.5 0.0 all-gather.8.cloned.1.call-start
  38.5 0.5 all-gather.8.cloned.1.call-update
  39.1 0.0 all-gather.10.cloned.1.call-start
  39.1 259.4 %all-reduce.2.cloned.1.call-done = f32[512,1024]{1,0:T(8,128)} async-done(((f32[512,1024]{1,0:T(8,128)}), f32[512,1024]{1,0:T(8,128)}) %all-reduce.2.cloned.1.call-update) | async-done | bytes 2097168 | tf_op jit(solution)/shard_map/psum | solution.py:40
  298.6 0.0 all-gather.6.cloned.1.call-done
  298.6 6.0 %convolution_convert_fusion = bf16[512,2304]{1,0:T(8,128)(2,1)S(1)} fusion(bf16[2304,1024]{1,0:T(8,128)(2,1)} %bitcast.56, f32[512,1024]{1,0:T(8,128)} %all-reduce.2.cloned.1.call-done, bf16[512,1024]{1,0:T(8,128)(2,1)} %all-gather.6.cloned.1.call-done), kind=kOutput, calls=%fused_computation.1 | convolution fusion | flops 2419720192 | bytes 10223616 | tf_op jit(solution)/shard_map/dot_general | solution.py:48
  304.6 66.2 %all_to_all.36 = bf16[32,16,2304]{2,1,0:T(8,128)(2,1)S(1)} all-to-all(bf16[32,16,2304]{2,1,0:T(8,128)(2,1)S(1)} %bitcast.54), channel_id=1, replica_groups=mesh['wide'=32,'narrow'=8] {'wide'}, dimensions={0} | all-to-all | bytes 4718592 | tf_op jit(solution)/shard_map/all_to_all | solution.py:51
  370.7 0.7 copy.24
  371.4 21.4 %reshape.41 = bf16[16,32,96,24]{3,2,1,0:T(8,128)(2,1)} reshape(bf16[16,32,2304]{2,1,0:T(8,128)(2,1)S(1)} %copy.24) | data formatting | bytes 4718592 | tf_op jit(solution)/shard_map/reshape | solution.py:52
  392.8 0.0 all-gather.8.cloned.1.call-done
  392.8 8.8 %fusion.5 = bf16[16,96,128]{2,1,0:T(8,128)(2,1)} fusion(bf16[16,32,96,24]{3,2,1,0:T(8,128)(2,1)} %reshape.41, bf16[16,32,24,128]{3,2,1,0:T(8,128)(2,1)} %bitcast.58), kind=kOutput, calls=%fused_computation.13 | convolution fusion | flops 302186496 | bytes 5898240 | tf_op jit(solution)/shard_map/waij,waje->wie/dot_general | solution.py:59
  401.6 0.0 all-gather.10.cloned.1.call-update
  401.6 0.2 all-gather.12.cloned.1.call-start
  401.9 25.1 %all-gather.10.cloned.1.call-done = bf16[16,768,128]{2,1,0:T(8,128)(2,1)} async-done(((bf16[16,96,128]{2,1,0:T(8,128)(2,1)}), bf16[16,768,128]{2,1,0:T(8,128)(2,1)}) %all-gather.10.cloned.1.call-update) | async-done | bytes 3145744 | tf_op jit(solution)/shard_map/all_gather | solution.py:56
  426.9 8.8 %fusion.6 = bf16[16,96,128]{2,1,0:T(8,128)(2,1)} fusion(bf16[16,32,96,24]{3,2,1,0:T(8,128)(2,1)} %reshape.41, bf16[16,32,24,128]{3,2,1,0:T(8,128)(2,1)} %bitcast.59), kind=kOutput, calls=%fused_computation.14 | convolution fusion | flops 302383104 | bytes 5898240 | tf_op jit(solution)/shard_map/waij,waje->wie/dot_general | solution.py:59
  435.7 0.0 all-gather.12.cloned.1.call-update
  435.8 0.0 all-gather.14.cloned.1.call-start
  435.8 30.2 %all-gather.12.cloned.1.call-done = bf16[16,768,128]{2,1,0:T(8,128)(2,1)} async-done(((bf16[16,96,128]{2,1,0:T(8,128)(2,1)}), bf16[16,768,128]{2,1,0:T(8,128)(2,1)}) %all-gather.12.cloned.1.call-update) | async-done | bytes 3145744 | tf_op jit(solution)/shard_map/all_gather | solution.py:56
  466.0 0.0 copy-start.1
  466.0 0.0 copy-start.2
  466.0 0.0 copy-start.3
  466.0 8.9 %fusion.7 = bf16[16,96,128]{2,1,0:T(8,128)(2,1)} fusion(bf16[16,32,96,24]{3,2,1,0:T(8,128)(2,1)} %reshape.41, bf16[16,32,24,128]{3,2,1,0:T(8,128)(2,1)} %bitcast.60), kind=kOutput, calls=%fused_computation.15 | convolution fusion | flops 302383104 | bytes 5898240 | tf_op jit(solution)/shard_map/waij,waje->wie/dot_general | solution.py:59
  474.9 0.0 all-gather.14.cloned.1.call-update
  474.9 30.2 %all-gather.14.cloned.1.call-done = bf16[16,768,128]{2,1,0:T(8,128)(2,1)} async-done(((bf16[16,96,128]{2,1,0:T(8,128)(2,1)}), bf16[16,768,128]{2,1,0:T(8,128)(2,1)}) %all-gather.14.cloned.1.call-update) | async-done | bytes 3145744 | tf_op jit(solution)/shard_map/all_gather | solution.py:56
  505.2 0.0 copy-done.1
  505.2 0.0 copy-done.2
  505.2 0.0 copy-done.3
  505.2 0.0 copy-start.4
  505.2 8.3 %fusion.4 = bf16[16,96,128]{2,1,0:T(8,128)(2,1)S(1)} fusion(bf16[16,32,96,24]{3,2,1,0:T(8,128)(2,1)} %reshape.41, bf16[16,32,24,128]{3,2,1,0:T(8,128)(2,1)} %bitcast.57, bf16[16,96,128]{2,1,0:T(8,128)(2,1)} %fusion.7, bf16[16,96,128]{2,1,0:T(8,128)(2,1)S(1)} %copy-done.3, bf16[16,96,128]{2,1,0:T(8,128)(2,1)S(1)} %copy-done.2, ...), kind=kOutput, calls=%fused_computation.12 | convolution fusion | flops 303955968 | bytes 7471104 | tf_op jit(solution)/shard_map/waij,waje->wie/dot_general | solution.py:59
  513.5 1.3 collective-permute-start.1
  514.8 4.0 collective-permute-start
  518.8 0.0 copy-done.4
  518.9 1.4 constant_dynamic-slice_fusion
  520.2 5.6 %collective-permute-done.1 = bf16[16,96,128]{2,1,0:T(8,128)(2,1)S(1)} collective-permute-done((bf16[16,96,128]{2,1,0:T(8,128)(2,1)S(1)}, bf16[16,96,128]{2,1,0:T(8,128)(2,1)S(1)}, u32[]{:S(2)}, u32[]{:S(2)}) %collective-permute-start.1) | collective-permute-done | bytes 393248 | tf_op jit(solution)/shard_map/ppermute | solution.py:19
  525.8 0.9 collective-permute-done
  526.7 0.1 pad_maximum_fusion
  526.8 0.6 gather_fusion
  527.5 0.9 broadcast_select_fusion
  (2 shorter events, 0.0 us)
Async XLA Ops:
  8.0 27.8 %copy-start = (bf16[4,96,1024]{2,1,0:T(8,128)(2,1)S(1)}, bf16[4,96,1024]{2,1,0:T(8,128)(2,1)}, u32[]{:S(2)}) copy-start(bf16[4,96,1024]{2,1,0:T(8,128)(2,1)} %param.9) | copy-start | bytes 2359300
  8.0 290.5 %all-reduce.2.cloned.1.call-start = ((), (), s32[]{:S(2)}) async-start(), calls=%async_computation.3 | async-start | bytes 4194304 | tf_op jit(solution)/shard_map/psum | solution.py:40
  37.9 260.7 %all-gather.6.cloned.1.call-start = ((), (), s32[]{:S(2)}) async-start(), calls=%async_computation.2 | async-start | bytes 1081344 | tf_op jit(solution)/shard_map/all_gather | solution.py:41
  38.5 354.4 %all-gather.8.cloned.1.call-start = ((), (), s32[]{:S(2)}) async-start(), calls=%async_computation.4 | async-start | bytes 3538944 | tf_op jit(solution)/shard_map/all_gather | solution.py:56
  39.1 387.9 %all-gather.10.cloned.1.call-start = ((), (), s32[]{:S(2)}) async-start(), calls=%async_computation.5 | async-start | bytes 3538944 | tf_op jit(solution)/shard_map/all_gather | solution.py:56
  401.6 64.4 %all-gather.12.cloned.1.call-start = ((), (), s32[]{:S(2)}) async-start(), calls=%async_computation.6 | async-start | bytes 3538944 | tf_op jit(solution)/shard_map/all_gather | solution.py:56
  435.8 69.4 %all-gather.14.cloned.1.call-start = ((), (), s32[]{:S(2)}) async-start(), calls=%async_computation.7 | async-start | bytes 3538944 | tf_op jit(solution)/shard_map/all_gather | solution.py:56
  466.0 39.2 %copy-start.1 = (bf16[16,96,128]{2,1,0:T(8,128)(2,1)S(1)}, bf16[16,96,128]{2,1,0:T(8,128)(2,1)}, u32[]{:S(2)}) copy-start(bf16[16,96,128]{2,1,0:T(8,128)(2,1)} %param.6) | copy-start | bytes 1179652
  466.0 39.2 %copy-start.2 = (bf16[16,96,128]{2,1,0:T(8,128)(2,1)S(1)}, bf16[16,96,128]{2,1,0:T(8,128)(2,1)}, u32[]{:S(2)}) copy-start(bf16[16,96,128]{2,1,0:T(8,128)(2,1)} %fusion.5) | copy-start | bytes 1179652
  466.0 39.2 %copy-start.3 = (bf16[16,96,128]{2,1,0:T(8,128)(2,1)S(1)}, bf16[16,96,128]{2,1,0:T(8,128)(2,1)}, u32[]{:S(2)}) copy-start(bf16[16,96,128]{2,1,0:T(8,128)(2,1)} %fusion.6) | copy-start | bytes 1179652
  505.2 13.7 %copy-start.4 = (s32[16]{0:T(128)S(1)}, s32[16]{0:T(128)}, u32[]{:S(2)}) copy-start(s32[16]{0:T(128)} %param.11) | copy-start | bytes 196
  513.5 12.3 %collective-permute-start.1 = (bf16[16,96,128]{2,1,0:T(8,128)(2,1)S(1)}, bf16[16,96,128]{2,1,0:T(8,128)(2,1)S(1)}, u32[]{:S(2)}, u32[]{:S(2)}) collective-permute-start(bf16[16,96,128]{2,1,0:T(8,128)(2,1)S(1)} %fusion.4), channel_id=1, source_target_pairs={{8,0},{16,8},{24,16},{32,24},{40,32},{48,40},{56,48},{64,56},{72,6... | collective-permute-start | bytes 1179656 | tf_op jit(solution)/shard_map/ppermute | solution.py:19
  514.8 11.9 %collective-permute-start = (bf16[16,96,128]{2,1,0:T(8,128)(2,1)S(1)}, bf16[16,96,128]{2,1,0:T(8,128)(2,1)S(1)}, u32[]{:S(2)}, u32[]{:S(2)}) collective-permute-start(bf16[16,96,128]{2,1,0:T(8,128)(2,1)S(1)} %fusion.4), channel_id=1, source_target_pairs={{0,8},{8,16},{16,24},{24,32},{32,40},{40,48},{48,56},{56,64},{64,7... | collective-permute-start | bytes 1179656 | tf_op jit(solution)/shard_map/ppermute | solution.py:18
Sparse Core Ops, SparseCore 0:
  38.0 260.4 all-reduce.1
Sparse Core Ops, SparseCore 1:
  41.0 69.3 all-gather.5
  112.0 33.1 all-gather.7
  401.7 25.2 all-gather.9
  435.8 30.1 all-gather.11
  475.0 30.1 all-gather.13
where the time goes:
time: 541 us; the launch traced here: 536 us
  waiting for transfers between devices  353 us (65%)
  blocking collectives  91.6 us (17%)
  matrix products  44.3 us (8%)
  local copies, waits for them, and re-layouts  24.9 us (5%)
  between operations  15.8 us (3%)
  starting transfers between devices  5.73 us (1%)
    psum x1, waiting for transfers between devices, per_device(): summed_bias = lax.psum(partial_bias, ('wide', 'narrow'))  259 us
    all_gather x4, waiting for transfers between devices, per_device(): rows_in = lax.all_gather(current, 'narrow', axis=1, tiled=True)  85.5 us
    all_to_all x1, blocking collectives, per_device(): lax.all_to_all(operator_part, 'wide', split_axis=0, concat_axis=1, tiled=...  66.2 us
    dot_general x4, matrix products, per_device(): jnp.einsum('waij,waje->wie', operator, shaped, preferred_element_type=jnp...  34.8 us
    all_to_all x1, blocking collectives, per_device(): lax.all_to_all(rotated, 'wide', split_axis=1, concat_axis=0, tiled=True)  25.5 us
    reshape x1, local copies, waits for them, and re-layouts, per_device(): operator = operator.reshape(walk_local, wide_count, row_count, col_count)  21.4 us
  transfers between devices with their start and end apart: 8, of which 6 were waited for; matrix products, arithmetic and copies ran while one was open for 6% of the time, Pallas kernels for 0%

commit v1 on v0

v1 whole, which is shorter than its diff:
```python
import math

import jax
import jax.numpy as jnp
from jax import lax
from jax.sharding import Mesh, PartitionSpec as P

time_step = 0.01
WIDE = ("z", "x")
NARROW = ("y", "c")
ALL = WIDE + NARROW


def exchange(blocks, axes):
    return lax.all_to_all(blocks, axes, split_axis=0, concat_axis=0, tiled=True)


def slot_walkers(walkers, offset, wide_count):
    up = [(i, (i + 1) % wide_count) for i in range(wide_count - 1)]
    down = [(j, i) for i, j in up]
    before = lax.ppermute(walkers, WIDE, up)
    after = lax.ppermute(walkers, WIDE, down)
    padded = jnp.concatenate([before, walkers, after], axis=0)
    return jnp.take(padded, offset, axis=0)


def per_device(walkers, intersection_inverse, noise, half_cholesky, cholesky, comb_source):
    walk_local, row_count, electrons = walkers.shape
    col_count, vectors = cholesky.shape[1:]
    wide_count = lax.axis_size(WIDE)
    narrow_count = lax.axis_size(NARROW)
    share = walk_local // narrow_count
    wide_at = lax.axis_index(WIDE)
    narrow_at = lax.axis_index(NARROW)
    root_step = math.sqrt(time_step)
    f32, bf16 = jnp.float32, jnp.bfloat16

    offset = comb_source - (wide_at - 1) * walk_local
    chosen = slot_walkers(walkers, offset, wide_count)
    chosen = chosen.reshape(narrow_count, share, row_count, electrons)
    chosen = exchange(chosen, NARROW)
    current = chosen.transpose(1, 0, 2, 3).reshape(share, narrow_count * row_count, electrons)

    rotated = jnp.einsum(
        "wiq,wqp->wpi", walkers, intersection_inverse, preferred_element_type=f32
    ).astype(bf16)
    rotated = rotated.reshape(walk_local, wide_count, -1).transpose(1, 0, 2)
    pairs = exchange(rotated, WIDE).reshape(wide_count * walk_local, -1)
    partial = jnp.dot(pairs, half_cholesky.reshape(-1, vectors), preferred_element_type=f32)
    partial = partial.astype(bf16).reshape(wide_count, narrow_count, share, vectors)
    partial = exchange(partial.transpose(1, 0, 2, 3), NARROW)
    partial = jnp.sum(partial.astype(f32), axis=0).astype(bf16)
    partial = exchange(partial, WIDE)
    force_bias = jnp.sum(partial.astype(f32), axis=0)

    own_noise = lax.dynamic_slice_in_dim(noise, narrow_at * share, share, 0)
    aux = (root_step * own_noise.astype(f32) + time_step * force_bias).astype(bf16)
    own_offset = lax.dynamic_slice_in_dim(offset, narrow_at * share, share, 0).astype(bf16)
    aux = jnp.concatenate([aux, jnp.broadcast_to(own_offset[:, None], (share, 128))], axis=1)
    aux = exchange(jnp.broadcast_to(aux[None], (wide_count,) + aux.shape), WIDE)
    aux = exchange(jnp.broadcast_to(aux[None], (narrow_count,) + aux.shape), NARROW)
    offsets = aux[:, :, :, vectors].transpose(1, 0, 2).astype(jnp.int32)
    source = offsets + (jnp.arange(wide_count, dtype=jnp.int32)[:, None, None] - 1) * walk_local
    source = source.reshape(-1)
    block, inner = source // walk_local, source % walk_local
    row = (inner // share) * (wide_count * share) + block * share + inner % share
    table = aux[..., :vectors].reshape(-1, vectors)
    pick = (row[:, None] == jnp.arange(table.shape[0], dtype=jnp.int32)[None]).astype(bf16)
    fields = jnp.dot(pick, table, preferred_element_type=f32).astype(bf16)

    flat_chol = cholesky.reshape(row_count * col_count, vectors)
    operator = lax.dot_general(
        fields, flat_chol, (((1,), (1,)), ((), ())), preferred_element_type=f32
    ).astype(bf16)
    operator = exchange(operator.reshape(wide_count * narrow_count, share, -1), ALL)
    operator = operator.reshape(wide_count, narrow_count, share, row_count, col_count)
    orbitals = narrow_count * row_count
    operator = operator.transpose(2, 1, 3, 0, 4).reshape(share, orbitals, orbitals)
    summed = current.astype(f32)
    for degree in range(1, 5):
        product = jnp.einsum(
            "wij,wje->wie", operator, current, preferred_element_type=f32
        ) / float(degree)
        if degree < 4:
            current = product.astype(bf16)
            summed = summed + current.astype(f32)
        else:
            summed = summed + product
    propagated = summed.astype(bf16).reshape(share, narrow_count, row_count, electrons)
    new_walkers = exchange(propagated.transpose(1, 0, 2, 3), NARROW)
    return (new_walkers.reshape(walk_local, row_count, electrons), force_bias)


def solution(mesh):
    fine = Mesh(mesh.devices.reshape(8, 4, 4, 2), ALL)
    in_specs = (
        P(WIDE, NARROW, None),
        P(WIDE, None, None),
        P(WIDE, None),
        P(WIDE, NARROW, None),
        P(NARROW, WIDE, None),
        P(WIDE),
    )
    out_specs = (P(WIDE, NARROW, None), P(ALL, None))
    return jax.shard_map(
        per_device, mesh=fine, in_specs=in_specs, out_specs=out_specs, check_vma=False
    )
```

time: 541 us -> 253 us (0.47)
  waiting for transfers between devices: 353 us -> 90.7 us
  blocking collectives: 91.6 us -> 51.4 us
  starting transfers between devices: 5.73 us -> 39.2 us
  matrix products: 44.3 us -> 12.4 us
  local copies, waits for them, and re-layouts: 24.9 us -> 52.4 us
  between operations: 15.8 us -> 0.89 us
    psum x1 -> x0, waiting for transfers between devices: 259 us -> none  [per_device(): summed_bias = lax.psum(partial_bias, ('wide', 'narrow'))]
    all_gather x5 -> x0, waiting for transfers between devices: 85.5 us -> none  [the longest x4 85.5 us: per_device(): rows_in = lax.all_gather(current, 'narrow', axis=1, tiled=True)]
    all_to_all x0 -> x5, waiting for transfers between devices: none -> 81.1 us  [exchange(): return lax.all_to_all(blocks, axes, split_axis=0, concat_axis=0, tiled=True)]
    all_to_all x2 -> x3, blocking collectives: 91.6 us -> 51.4 us  [exchange(): return lax.all_to_all(blocks, axes, split_axis=0, concat_axis=0, tiled=True)]
    all_to_all x0 -> x5, starting transfers between devices: none -> 36.2 us  [exchange(): return lax.all_to_all(blocks, axes, split_axis=0, concat_axis=0, tiled=True)]
    dot_general x6, matrix products: 42.8 us -> 10.9 us  [the longest x1 5.99 us: per_device(): lax.dot_general(fields, flat_chol, (((1,), (1,)), ((), ())), preferred_el...]
    transpose x0 -> x3, local copies, waits for them, and re-layouts: none -> 12.3 us  [the longest x1 11.4 us: per_device(): operator.transpose(2, 1, 3, 0, 4).reshape(share, orbitals, orbitals)]
    reshape x1 -> x9, local copies, waits for them, and re-layouts: 21.4 us -> 32.8 us  [the longest x1 21.4 us: per_device(): operator.reshape(wide_count, narrow_count, share, row_count, col_count)]
  transfers between devices with their start and end apart: 8 -> 7, of which waited for: 6 -> 5; matrix products, arithmetic and copies ran while one was open for 6% -> 6% of each run, Pallas kernels for 0% -> 0%
where the time goes in v1:
time: 253 us; the launch traced here: 252 us
  waiting for transfers between devices  90.7 us (36%)
  local copies, waits for them, and re-layouts  52.4 us (21%)
  blocking collectives  51.4 us (20%)
  starting transfers between devices  39.2 us (15%)
  matrix products  12.4 us (5%)
  other arithmetic  5.41 us (2%)
    all_to_all x5, waiting for transfers between devices, exchange(): return lax.all_to_all(blocks, axes, split_axis=0, concat_axis=0, tiled=True)  81.1 us
    all_to_all x3, blocking collectives, exchange(): return lax.all_to_all(blocks, axes, split_axis=0, concat_axis=0, tiled=True)  51.4 us
    all_to_all x5, starting transfers between devices, exchange(): return lax.all_to_all(blocks, axes, split_axis=0, concat_axis=0, tiled=True)  36.2 us
    reshape x1, local copies, waits for them, and re-layouts, per_device(): operator.reshape(wide_count, narrow_count, share, row_count, col_count)  21.4 us
    transpose x1, local copies, waits for them, and re-layouts, per_device(): operator.transpose(2, 1, 3, 0, 4).reshape(share, orbitals, orbitals)  11.4 us
    ppermute x1, waiting for transfers between devices, slot_walkers(): before = lax.ppermute(walkers, WIDE, up)  6.38 us
    dot_general x1, matrix products, per_device(): lax.dot_general(fields, flat_chol, (((1,), (1,)), ((), ())), preferred_el...  5.99 us
  transfers between devices with their start and end apart: 7, of which 5 were waited for; matrix products, arithmetic and copies ran while one was open for 6% of the time, Pallas kernels for 0%

profile of v1, /device:TPU:1, one launch (start us, length us, event | category | flops | bytes accessed | tf_op | source)
XLA Modules:
  0.0 252.3 jit_solution(1456053808168392507)
XLA Ops:
  0.6 0.0 copy-start
  0.6 1.5 convolution_convert_fusion.3
  2.2 0.3 copy.84
  2.5 0.4 reshape.143
  2.8 0.1 copy.85
  3.0 25.5 %all_to_all.40 = bf16[32,16,384]{2,1,0:T(8,128)(2,1)S(1)} all-to-all(bf16[32,16,384]{2,1,0:T(8,128)(2,1)S(1)} %copy.85), channel_id=1, replica_groups=mesh['z'=8,'x'=4,'y'=4,'c'=2] {'z','x'}, dimensions={0} | all-to-all | bytes 786432 | tf_op jit(solution)/shard_map/all_to_all | solution.py:15
  28.4 0.0 copy-done
  28.4 0.7 convolution_convert_fusion.2
  29.2 0.4 reshape.146
  29.6 0.0 copy-start.6
  29.6 1.8 copy.107
  31.4 6.9 %all-to-all-start.2 = ((bf16[8,32,2,1024]{3,2,1,0:T(2,128)(2,1)}), bf16[8,32,2,1024]{3,2,1,0:T(2,128)(2,1)S(1)}, u32[]{:S(2)}, u32[]{:S(2)}) async-start(bf16[8,32,2,1024]{3,2,1,0:T(2,128)(2,1)} %bitcast.39), calls=%async_computation.2 | async-start | bytes 2097152 | tf_op jit(solution)/shard_map/all_to_all | solution.py:15
  38.3 15.0 %all-to-all-done.2 = bf16[8,32,2,1024]{3,2,1,0:T(2,128)(2,1)S(1)} async-done(((bf16[8,32,2,1024]{3,2,1,0:T(2,128)(2,1)}), bf16[8,32,2,1024]{3,2,1,0:T(2,128)(2,1)S(1)}, u32[]{:S(2)}, u32[]{:S(2)}) %all-to-all-start.2) | async-done | bytes 1048608 | tf_op jit(solution)/shard_map/all_to_all | solution.py:15
  53.3 1.9 reduce_sum.21
  55.1 4.0 %all-to-all-start.3 = ((bf16[32,2,1024]{2,1,0:T(2,128)(2,1)}), bf16[32,2,1024]{2,1,0:T(2,128)(2,1)S(1)}, u32[]{:S(2)}, u32[]{:S(2)}) async-start(bf16[32,2,1024]{2,1,0:T(2,128)(2,1)} %reduce_sum.21), calls=%async_computation.3 | async-start | bytes 262144 | tf_op jit(solution)/shard_map/all_to_all | solution.py:15
  59.2 0.0 copy-done.6
  59.2 0.0 copy-start.1
  59.2 0.1 dynamic-slice_convert_fusion
  59.3 9.3 %all-to-all-done.3 = bf16[32,2,1024]{2,1,0:T(2,128)(2,1)S(1)} async-done(((bf16[32,2,1024]{2,1,0:T(2,128)(2,1)}), bf16[32,2,1024]{2,1,0:T(2,128)(2,1)S(1)}, u32[]{:S(2)}, u32[]{:S(2)}) %all-to-all-start.3) | async-done | bytes 131104 | tf_op jit(solution)/shard_map/all_to_all | solution.py:15
  68.6 0.0 copy-start.4
  68.6 0.7 add_convert_fusion
  69.4 0.1 broadcast_in_dim.39
  69.4 0.1 broadcast_in_dim.40
  69.5 12.8 %all_to_all.41 = bf16[32,2,1152]{2,1,0:T(2,128)(2,1)S(1)} all-to-all(bf16[32,2,1152]{2,1,0:T(2,128)(2,1)S(1)} %broadcast_in_dim.40), channel_id=1, replica_groups=mesh['z'=8,'x'=4,'y'=4,'c'=2] {'z','x'}, dimensions={0} | all-to-all | bytes 294912 | tf_op jit(solution)/shard_map/all_to_all | solution.py:15
  82.4 1.1 broadcast_in_dim.41
  83.5 6.9 %all-to-all-start.5 = ((bf16[8,32,2,1152]{3,1,2,0:T(8,128)(2,1)}), bf16[8,32,2,1152]{3,1,2,0:T(8,128)(2,1)S(1)}, u32[]{:S(2)}, u32[]{:S(2)}) async-start(bf16[8,32,2,1152]{3,1,2,0:T(8,128)(2,1)} %broadcast_in_dim.41), calls=%async_computation.5 | async-start | bytes 2359296 | tf_op jit(solution)/shard_map/all_to_all | solution.py:15
  90.5 0.0 copy-done.1
  90.5 1.6 collective-permute-start
  92.1 1.3 collective-permute-start.1
  93.4 0.1 broadcast_in_dim.20
  93.5 0.5 add_multiply_fusion
  94.0 6.4 %collective-permute-done = bf16[16,96,128]{2,1,0:T(8,128)(2,1)S(1)} collective-permute-done((bf16[16,96,128]{2,1,0:T(8,128)(2,1)S(1)}, bf16[16,96,128]{2,1,0:T(8,128)(2,1)S(1)}, u32[]{:S(2)}, u32[]{:S(2)}) %collective-permute-start) | collective-permute-done | bytes 393248 | tf_op jit(solution)/shard_map/ppermute | solution.py:21
  100.4 0.7 copy-done.3
  101.2 3.2 %collective-permute-done.1 = bf16[16,96,128]{2,1,0:T(8,128)(2,1)} collective-permute-done((bf16[16,96,128]{2,1,0:T(8,128)(2,1)S(1)}, bf16[16,96,128]{2,1,0:T(8,128)(2,1)}, u32[]{:S(2)}, u32[]{:S(2)}) %collective-permute-start.1) | collective-permute-done | bytes 393248 | tf_op jit(solution)/shard_map/ppermute | solution.py:22
  104.4 1.2 pad_maximum_fusion
  105.6 0.0 copy-done.4
  105.6 0.6 gather_fusion
  106.3 0.9 broadcast_select_fusion
  107.1 0.0 all-to-all-done.5
  107.1 5.7 %all-to-all-start = ((bf16[8,2,96,128]{3,2,1,0:T(8,128)(2,1)}), bf16[8,2,96,128]{3,2,1,0:T(8,128)(2,1)S(1)}, u32[]{:S(2)}, u32[]{:S(2)}) async-start(bf16[8,2,96,128]{3,2,1,0:T(8,128)(2,1)} %broadcast_select_fusion), calls=%async_computation | async-start | bytes 786432 | tf_op jit(solution)/shard_map/all_to_all | solution.py:15
  112.8 0.1 slice.11
  113.0 0.0 copy-start.5
  113.0 1.1 copy.91
  114.1 1.2 reshape.148
  115.3 0.2 copy.103
  115.5 0.0 copy-done.5
  115.5 0.1 copy.90
  115.7 0.1 reshape.147
  115.8 6.0 %convolution_convert_fusion = bf16[512,2304]{1,0:T(8,128)(2,1)S(1)} fusion(bf16[2304,1024]{1,0:T(8,128)(2,1)} %bitcast.52, bf16[512,1024]{1,0:T(8,128)(2,1)} %reshape.148, s32[512]{0:T(512)S(1)} %fusion.9), kind=kOutput, calls=%fused_computation.1 | convolution fusion | flops 2954756096 | bytes 8128512 | tf_op jit(solution)/shard_map/dot_general | solution.py:72
  121.8 2.3 reshape.150
  124.2 0.0 all-to-all-done
  124.2 12.7 %all-to-all-start.6 = ((bf16[256,2,2304]{2,1,0:T(2,128)(2,1)}), bf16[256,2,2304]{2,1,0:T(2,128)(2,1)}, u32[]{:S(2)}, u32[]{:S(2)}) async-start(bf16[256,2,2304]{2,1,0:T(2,128)(2,1)} %reshape.150), calls=%async_computation.6 | async-start | bytes 4718592 | tf_op jit(solution)/shard_map/all_to_all | solution.py:15
  136.8 0.8 copy.83
  137.6 56.9 %all-to-all-done.6 = bf16[256,2,2304]{2,1,0:T(2,128)(2,1)} async-done(((bf16[256,2,2304]{2,1,0:T(2,128)(2,1)}), bf16[256,2,2304]{2,1,0:T(2,128)(2,1)}, u32[]{:S(2)}, u32[]{:S(2)}) %all-to-all-start.6) | async-done | bytes 2359328 | tf_op jit(solution)/shard_map/all_to_all | solution.py:15
  194.5 1.9 copy.92
  196.4 21.4 %reshape.151 = bf16[32,8,2,96,24]{4,3,1,0,2:T(8,128)(2,1)} reshape(bf16[256,2,2304]{2,0,1:T(8,128)(2,1)S(1)} %copy.92) | data formatting | bytes 4718592 | tf_op jit(solution)/shard_map/reshape | solution.py:76
  217.8 11.4 %copy.93 = bf16[2,8,96,32,24]{2,1,4,3,0:T(8,128)(2,1)} copy(bf16[2,8,96,32,24]{4,2,1,3,0:T(8,128)(2,1)} %bitcast.42) | data formatting | bytes 4718592 | tf_op jit(solution)/shard_map/transpose | solution.py:78
  229.2 5.0 %reshape.152 = bf16[2,768,768]{1,2,0:T(8,128)(2,1)S(1)} reshape(bf16[2,8,96,32,24]{2,1,4,3,0:T(8,128)(2,1)} %copy.93) | data formatting | bytes 4718592 | tf_op jit(solution)/shard_map/reshape | solution.py:78
  234.3 1.0 convolution_convert_fusion.4
  235.3 1.0 fusion.2
  236.4 1.0 fusion.3
  237.4 1.1 fusion.1
  238.5 13.1 %all_to_all.42 = bf16[8,2,96,128]{3,2,1,0:T(8,128)(2,1)S(1)} all-to-all(bf16[8,2,96,128]{3,2,1,0:T(8,128)(2,1)S(1)} %bitcast.47), channel_id=1, replica_groups=mesh['z'=8,'x'=4,'y'=4,'c'=2] {'y','c'}, dimensions={0} | all-to-all | bytes 786432 | tf_op jit(solution)/shard_map/all_to_all | solution.py:15
  251.6 0.7 copy.110
  (13 shorter events, 0.2 us)
Async XLA Ops:
  0.6 27.8 %copy-start = (bf16[4,96,1024]{2,1,0:T(8,128)(2,1)S(1)}, bf16[4,96,1024]{2,1,0:T(8,128)(2,1)}, u32[]{:S(2)}) copy-start(bf16[4,96,1024]{2,1,0:T(8,128)(2,1)} %param.9) | copy-start | bytes 2359300
  29.6 29.6 %copy-start.6 = (s32[16]{0:T(128)S(1)}, s32[16]{0:T(128)}, u32[]{:S(2)}) copy-start(s32[16]{0:T(128)} %param.11) | copy-start | bytes 196
  31.4 21.9 %all-to-all-start.2 = ((bf16[8,32,2,1024]{3,2,1,0:T(2,128)(2,1)}), bf16[8,32,2,1024]{3,2,1,0:T(2,128)(2,1)S(1)}, u32[]{:S(2)}, u32[]{:S(2)}) async-start(bf16[8,32,2,1024]{3,2,1,0:T(2,128)(2,1)} %bitcast.39), calls=%async_computation.2 | async-start | bytes 2097152 | tf_op jit(solution)/shard_map/all_to_all | solution.py:15
  55.1 13.4 %all-to-all-start.3 = ((bf16[32,2,1024]{2,1,0:T(2,128)(2,1)}), bf16[32,2,1024]{2,1,0:T(2,128)(2,1)S(1)}, u32[]{:S(2)}, u32[]{:S(2)}) async-start(bf16[32,2,1024]{2,1,0:T(2,128)(2,1)} %reduce_sum.21), calls=%async_computation.3 | async-start | bytes 262144 | tf_op jit(solution)/shard_map/all_to_all | solution.py:15
  59.2 31.3 %copy-start.1 = (bf16[16,96,128]{2,1,0:T(8,128)(2,1)S(1)}, bf16[16,96,128]{2,1,0:T(8,128)(2,1)}, u32[]{:S(2)}) copy-start(bf16[16,96,128]{2,1,0:T(8,128)(2,1)} %param.6) | copy-start | bytes 1179652
  68.6 37.0 %copy-start.4 = (f32[2,1024]{1,0:T(2,128)}, f32[2,1024]{1,0:T(2,128)S(1)}, u32[]{:S(2)}) copy-start(f32[2,1024]{1,0:T(2,128)S(1)} %convert_reduce_fusion) | copy-start | bytes 24580
  83.5 23.6 %all-to-all-start.5 = ((bf16[8,32,2,1152]{3,1,2,0:T(8,128)(2,1)}), bf16[8,32,2,1152]{3,1,2,0:T(8,128)(2,1)S(1)}, u32[]{:S(2)}, u32[]{:S(2)}) async-start(bf16[8,32,2,1152]{3,1,2,0:T(8,128)(2,1)} %broadcast_in_dim.41), calls=%async_computation.5 | async-start | bytes 2359296 | tf_op jit(solution)/shard_map/all_to_all | solution.py:15
  90.5 10.0 %collective-permute-start = (bf16[16,96,128]{2,1,0:T(8,128)(2,1)S(1)}, bf16[16,96,128]{2,1,0:T(8,128)(2,1)S(1)}, u32[]{:S(2)}, u32[]{:S(2)}) collective-permute-start(bf16[16,96,128]{2,1,0:T(8,128)(2,1)S(1)} %copy-done.1), channel_id=1, source_target_pairs={{0,8},{8,16},{16,24},{24,32},{32,40},{40,48},{48,56},{56,64},{64,7... | collective-permute-start | bytes 1179656 | tf_op jit(solution)/shard_map/ppermute | solution.py:21
  92.1 12.3 %collective-permute-start.1 = (bf16[16,96,128]{2,1,0:T(8,128)(2,1)S(1)}, bf16[16,96,128]{2,1,0:T(8,128)(2,1)}, u32[]{:S(2)}, u32[]{:S(2)}) collective-permute-start(bf16[16,96,128]{2,1,0:T(8,128)(2,1)S(1)} %copy-done.1), channel_id=1, source_target_pairs={{8,0},{16,8},{24,16},{32,24},{40,32},{48,40},{56,48},{64,56},{72,6... | collective-permute-start | bytes 1179656 | tf_op jit(solution)/shard_map/ppermute | solution.py:22
  100.4 0.7 copy-start.3
  107.1 17.0 %all-to-all-start = ((bf16[8,2,96,128]{3,2,1,0:T(8,128)(2,1)}), bf16[8,2,96,128]{3,2,1,0:T(8,128)(2,1)S(1)}, u32[]{:S(2)}, u32[]{:S(2)}) async-start(bf16[8,2,96,128]{3,2,1,0:T(8,128)(2,1)} %broadcast_select_fusion), calls=%async_computation | async-start | bytes 786432 | tf_op jit(solution)/shard_map/all_to_all | solution.py:15
  113.0 2.5 %copy-start.5 = (s32[32]{0:T(128)S(1)}, s32[32]{0:T(128)}, u32[]{:S(2)}) copy-start(s32[32]{0:T(128)} %add_multiply_fusion) | copy-start | bytes 388
  124.2 70.3 %all-to-all-start.6 = ((bf16[256,2,2304]{2,1,0:T(2,128)(2,1)}), bf16[256,2,2304]{2,1,0:T(2,128)(2,1)}, u32[]{:S(2)}, u32[]{:S(2)}) async-start(bf16[256,2,2304]{2,1,0:T(2,128)(2,1)} %reshape.150), calls=%async_computation.6 | async-start | bytes 4718592 | tf_op jit(solution)/shard_map/all_to_all | solution.py:15
  229.2 5.1 %copy-start.2 = (bf16[2,8,96,128]{3,2,1,0:T(8,128)(2,1)S(1)}, bf16[2,8,96,128]{3,2,1,0:T(8,128)(2,1)}, u32[]{:S(2)}) copy-start(bf16[2,8,96,128]{3,2,1,0:T(8,128)(2,1)} %copy.83) | copy-start | bytes 1179652

commit v2 on v1

v2 whole, which is shorter than its diff:
```python
import math

import jax
import jax.numpy as jnp
from jax import lax
from jax.experimental import pallas as pl
from jax.experimental.pallas import tpu as pltpu
from jax.sharding import Mesh, PartitionSpec as P

time_step = 0.01
WIDE = ("z", "x")
WIDE_X = ("x", "z")
NARROW = ("y", "c")
PLANE = ("x", "y", "c")
MIXED = ("x", "y", "c", "z")
ALL = WIDE + NARROW
LANES = 128


def exchange(blocks, axes):
    return lax.all_to_all(blocks, axes, split_axis=0, concat_axis=0, tiled=True)


def slot_walkers(walkers, offset, wide_count):
    up = [(i, (i + 1) % wide_count) for i in range(wide_count - 1)]
    down = [(j, i) for i, j in up]
    before = lax.ppermute(walkers, WIDE, up)
    after = lax.ppermute(walkers, WIDE, down)
    padded = jnp.concatenate([before, walkers, after], axis=0)
    return jnp.take(padded, offset, axis=0)


def packed_cholesky(cholesky):
    row_count, col_count, vectors = cholesky.shape
    by_col = cholesky.transpose(1, 0, 2)
    full = col_count * row_count // LANES
    rest = LANES - row_count
    tail = by_col[full:].reshape(full, rest, vectors)
    return jnp.concatenate([by_col[:full], tail], axis=1).reshape(full * LANES, vectors)


def propagate_kernel(blocks_ref, current_ref, out_ref, matrix_ref, term_ref, total_ref):
    share = blocks_ref.shape[0]
    f32, bf16 = jnp.float32, jnp.bfloat16
    lane = lax.broadcasted_iota(jnp.int32, (32, 128), 1)

    def assemble(s, carry):
        def rows_of(t, n):
            at = t * 128
            pieces = [
                blocks_ref[s, x * 64 + n * 8 : x * 64 + n * 8 + 8, at : at + 128]
                for x in range(4)
            ]
            return jnp.concatenate([piece.astype(f32) for piece in pieces], axis=0)

        for j in range(24):
            chunks = []
            for n in range(8):
                if j < 18:
                    chunk = rows_of(j, n)
                else:
                    q = 3 * (j - 18)
                    chunk = jnp.where(
                        lane < 32,
                        pltpu.roll(rows_of(q, n), 32, 1),
                        jnp.where(
                            lane < 64,
                            pltpu.roll(rows_of(q + 1, n), 64, 1),
                            pltpu.roll(rows_of(q + 2, n), 96, 1),
                        ),
                    )
                chunks.append(chunk)
            for half in range(2):
                first, second, third, fourth = chunks[4 * half : 4 * half + 4]
                second = pltpu.roll(second, 96, 1)
                third = pltpu.roll(third, 64, 1)
                fourth = pltpu.roll(fourth, 32, 1)
                tiles = (
                    jnp.where(lane < 96, first, second),
                    jnp.where(lane < 64, second, third),
                    jnp.where(lane < 32, third, fourth),
                )
                for k, tile in enumerate(tiles):
                    at = half * 384 + k * 128
                    matrix_ref[s, j * 32 : (j + 1) * 32, at : at + 128] = tile.astype(bf16)
        return carry

    lax.fori_loop(0, share, assemble, 0)
    for s in range(share):
        start = current_ref[s].astype(f32)
        term_ref[s] = start
        total_ref[s] = start
    for degree in range(1, 5):
        for s in range(share):
            rows = [
                term_ref[s, pl.ds(x * 24 + j, 8, stride=96), :]
                for j in range(24)
                for x in range(4)
            ]
            ordered = jnp.concatenate(rows, axis=0).astype(bf16)
            product = lax.dot_general(
                ordered, matrix_ref[s], (((0,), (0,)), ((), ())), preferred_element_type=f32
            )
            product = product.T * (1.0 / degree)
            if degree < 4:
                product = product.astype(bf16).astype(f32)
                term_ref[s] = product
                total_ref[s] = total_ref[s] + product
            else:
                out_ref[s] = (total_ref[s] + product).astype(bf16)


def propagate(blocks, current):
    share, orbitals, electrons = current.shape
    f32, bf16 = jnp.float32, jnp.bfloat16
    return pl.pallas_call(
        propagate_kernel,
        out_shape=jax.ShapeDtypeStruct(current.shape, bf16),
        scratch_shapes=[
            pltpu.VMEM((share, orbitals, orbitals), bf16),
            pltpu.VMEM((share, orbitals, electrons), f32),
            pltpu.VMEM((share, orbitals, electrons), f32),
        ],
        name="propagate",
    )(blocks, current)


def per_device(walkers, intersection_inverse, noise, half_cholesky, cholesky, comb_source):
    walk_local, row_count, electrons = walkers.shape
    vectors = cholesky.shape[2]
    z_count, x_count = lax.axis_size("z"), lax.axis_size("x")
    wide_count = z_count * x_count
    narrow_count = lax.axis_size(NARROW)
    plane_count = x_count * narrow_count
    share = walk_local // narrow_count
    rows_here = z_count * share
    z_at = lax.axis_index("z")
    wide_at = lax.axis_index(WIDE)
    narrow_at = lax.axis_index(NARROW)
    root_step = math.sqrt(time_step)
    f32, bf16, i32 = jnp.float32, jnp.bfloat16, jnp.int32

    with jax.named_scope("slots"):
        offset = comb_source - (wide_at - 1) * walk_local
        chosen = slot_walkers(walkers, offset, wide_count)
        chosen = chosen.reshape(narrow_count, share, row_count, electrons)
        chosen = exchange(chosen, NARROW)
        current = chosen.transpose(1, 0, 2, 3).reshape(share, narrow_count * row_count, electrons)

    with jax.named_scope("side"):
        own_noise = lax.dynamic_slice_in_dim(noise, narrow_at * share, share, 0)
        own_offset = lax.dynamic_slice_in_dim(offset, narrow_at * share, share, 0).astype(bf16)
        own_offset = jnp.broadcast_to(own_offset[:, None], (share, LANES))
        side = jnp.concatenate([own_noise, own_offset], axis=1)
        side = exchange(jnp.broadcast_to(side[None], (z_count,) + side.shape), ("z",))
        side = side.reshape(rows_here, vectors + LANES)

    with jax.named_scope("rotate"):
        rotated = jnp.einsum(
            "wiq,wqp->wpi", walkers, intersection_inverse, preferred_element_type=f32
        ).astype(bf16)
        rotated = rotated.reshape(walk_local, z_count, x_count, -1).transpose(2, 1, 0, 3)
        pairs = exchange(rotated.reshape(wide_count, walk_local, -1), WIDE_X)

    with jax.named_scope("bias"):
        pairs = pairs.reshape(x_count, z_count, narrow_count, share, -1).transpose(0, 2, 1, 3, 4)
        pairs = pairs.reshape(wide_count * walk_local, -1)
        partial = jnp.dot(pairs, half_cholesky.reshape(-1, vectors), preferred_element_type=f32)
        partial = partial.astype(bf16).reshape(plane_count, rows_here, vectors)
        partial = exchange(partial, PLANE)
        partial = jnp.sum(partial.astype(f32), axis=0).astype(bf16)
        partial = exchange(jnp.broadcast_to(partial[None], (z_count,) + partial.shape), ("z",))
        bias = jnp.sum(partial.astype(f32), axis=0)
        force_bias = lax.dynamic_slice_in_dim(bias, z_at * share, share, 0)

    with jax.named_scope("field"):
        aux = root_step * side[:, :vectors].astype(f32) + time_step * bias
        aux = jnp.concatenate([aux.astype(bf16), side[:, vectors:]], axis=1)
        aux = exchange(jnp.broadcast_to(aux[None], (plane_count,) + aux.shape), PLANE)
        aux = aux.reshape(plane_count * rows_here, vectors + LANES)
        slot = jnp.arange(plane_count * rows_here, dtype=i32)
        slot_x = slot // (narrow_count * rows_here)
        slot_z = (slot // share) % z_count
        source = aux[:, vectors].astype(i32) + (slot_z * x_count + slot_x - 1) * walk_local
        block, inner = source // walk_local, source % walk_local
        row = (block % x_count) * narrow_count + inner // share
        row = row * rows_here + (block // x_count) * share + inner % share
        pick = (row[:, None] == slot[None]).astype(bf16)
        fields = jnp.dot(pick, aux[:, :vectors], preferred_element_type=f32).astype(bf16)

    with jax.named_scope("operator"):
        operator = lax.dot_general(
            fields,
            packed_cholesky(cholesky),
            (((1,), (1,)), ((), ())),
            preferred_element_type=f32,
        ).astype(bf16)
        operator = exchange(operator.reshape(wide_count * narrow_count, share, -1), MIXED)

    with jax.named_scope("taylor"):
        propagated = propagate(operator.transpose(1, 0, 2), current)
        propagated = propagated.reshape(share, narrow_count, row_count, electrons)
        new_walkers = exchange(propagated.transpose(1, 0, 2, 3), NARROW)
    return (new_walkers.reshape(walk_local, row_count, electrons), force_bias)


def solution(mesh):
    fine = Mesh(mesh.devices.reshape(8, 4, 4, 2), ALL)
    in_specs = (
        P(WIDE, NARROW, None),
        P(WIDE, None, None),
        P(WIDE, None),
        P(WIDE, NARROW, None),
        P(NARROW, WIDE, None),
        P(WIDE),
    )
    out_specs = (P(WIDE, NARROW, None), P(ALL, None))
    return jax.shard_map(
        per_device, mesh=fine, in_specs=in_specs, out_specs=out_specs, check_vma=False
    )
```

time: 253 us -> 222 us (0.88)
  local copies, waits for them, and re-layouts: 52.4 us -> 22.1 us
  blocking collectives: 51.4 us -> 23.4 us
  waiting for transfers between devices: 90.7 us -> 103 us
  Pallas kernels: 0 us -> 8.01 us
  starting transfers between devices: 39.2 us -> 45.9 us
  matrix products: 12.4 us -> 9.19 us
  other arithmetic: 5.41 us -> 8.19 us
    all_to_all x3 -> x1, blocking collectives: 51.4 us -> 23.4 us  [exchange(): return lax.all_to_all(blocks, axes, split_axis=0, concat_axis=0, tiled=True)]
    reshape x8 -> x6, local copies, waits for them, and re-layouts: 30.5 us -> 2.85 us  [the longest x1 1.77 us: per_device(): propagated = propagated.reshape(share, narrow_count, row_count, electrons)]
    all_to_all x5 -> x7, waiting for transfers between devices: 81.1 us -> 97.4 us  [exchange(): return lax.all_to_all(blocks, axes, split_axis=0, concat_axis=0, tiled=True)]
    transpose x2 -> x1, local copies, waits for them, and re-layouts: 11.6 us -> 0.13 us  [per_device(): rotated.reshape(walk_local, z_count, x_count, -1).transpose(2, 1, 0, 3)]
    pallas_call x0 -> x1, Pallas kernels: none -> 8.01 us  [propagate(): pl.pallas_call(propagate_kernel, out_shape=jax.ShapeDtypeStruct(current.s...]
    ppermute x1, waiting for transfers between devices: 6.38 us -> 0.01 us  [slot_walkers(): before = lax.ppermute(walkers, WIDE, up)]
    concatenate x1 -> x3, other arithmetic: 0.01 us -> 4.86 us  [the longest x1 4.85 us: packed_cholesky(): jnp.concatenate([by_col[:full], tail], axis=1)]
    unnamed x16 -> x12, local copies, waits for them, and re-layouts: 1.7 us -> 6.33 us
  transfers between devices with their start and end apart: 7 -> 9, of which waited for: 5 -> 6; matrix products, arithmetic and copies ran while one was open for 6% -> 12% of each run, Pallas kernels for 0% -> 0%
where the time goes in v2:
time: 222 us; the launch traced here: 221 us
  waiting for transfers between devices  103 us (46%)
  starting transfers between devices  45.9 us (21%)
  blocking collectives  23.4 us (11%)
  local copies, waits for them, and re-layouts  22.1 us (10%)
  matrix products  9.19 us (4%)
  other arithmetic  8.19 us (4%)
  Pallas kernels  8.01 us (4%)
    all_to_all x7, waiting for transfers between devices, exchange(): return lax.all_to_all(blocks, axes, split_axis=0, concat_axis=0, tiled=True)  97.4 us
    all_to_all x7, starting transfers between devices, exchange(): return lax.all_to_all(blocks, axes, split_axis=0, concat_axis=0, tiled=True)  39.9 us
    all_to_all x1, blocking collectives, exchange(): return lax.all_to_all(blocks, axes, split_axis=0, concat_axis=0, tiled=True)  23.4 us
    pallas_call x1, Pallas kernels, propagate(): pl.pallas_call(propagate_kernel, out_shape=jax.ShapeDtypeStruct(current.s...  8.01 us
    unnamed x12, local copies, waits for them, and re-layouts  6.33 us
    dot_general x1, matrix products, per_device(): lax.dot_general(fields, packed_cholesky(cholesky), (((1,), (1,)), ((), ()...  5.99 us
    ppermute x1, waiting for transfers between devices, slot_walkers(): after = lax.ppermute(walkers, WIDE, down)  5.74 us
    concatenate x1, other arithmetic, packed_cholesky(): jnp.concatenate([by_col[:full], tail], axis=1)  4.85 us
  transfers between devices with their start and end apart: 9, of which 6 were waited for; matrix products, arithmetic and copies ran while one was open for 12% of the time, Pallas kernels for 0%

profile of v2, /device:TPU:1, one launch (start us, length us, event | category | flops | bytes accessed | tf_op | source)
XLA Modules:
  0.0 220.7 jit_solution(9796333495935288906)
XLA Ops:
  0.6 0.0 copy-start
  0.6 1.5 convolution_convert_fusion.3
  2.2 0.3 copy.35
  2.5 0.5 reshape.163
  3.0 0.1 copy.36
  3.1 23.4 %all_to_all.40 = bf16[32,16,384]{2,1,0:T(8,128)(2,1)S(1)} all-to-all(bf16[32,16,384]{2,1,0:T(8,128)(2,1)S(1)} %bitcast.40), channel_id=1, replica_groups=mesh['z'=8,'x'=4,'y'=4,'c'=2] {'x','z'}, dimensions={0} | all-to-all | bytes 786432 | tf_op jit(solution)/shard_map/rotate/all_to_all | solution.py:21
  26.5 0.1 reshape.165
  26.6 0.3 copy.49
  26.9 0.1 reshape.166
  27.0 0.0 copy-done
  27.1 0.0 copy-start.4
  27.1 1.7 convolution_convert_fusion.2
  28.8 9.5 %all-to-all-start.2 = ((bf16[32,16,1024]{2,1,0:T(8,128)(2,1)}), bf16[32,16,1024]{2,1,0:T(8,128)(2,1)S(1)}, u32[]{:S(2)}, u32[]{:S(2)}) async-start(bf16[32,16,1024]{2,1,0:T(8,128)(2,1)} %bitcast.4), calls=%async_computation.2 | async-start | bytes 2097152 | tf_op jit(solution)/shard_map/bias/all_to_all | solution.py:21
  38.3 0.0 copy-done.4
  38.3 0.1 dynamic-slice_convert_fusion
  38.4 0.7 constant_dynamic-slice_fusion.1
  39.1 0.1 broadcast_in_dim.22
  39.2 16.0 %all-to-all-done.2 = bf16[32,16,1024]{2,1,0:T(8,128)(2,1)S(1)} async-done(((bf16[32,16,1024]{2,1,0:T(8,128)(2,1)}), bf16[32,16,1024]{2,1,0:T(8,128)(2,1)S(1)}, u32[]{:S(2)}, u32[]{:S(2)}) %all-to-all-start.2) | async-done | bytes 1048608 | tf_op jit(solution)/shard_map/bias/all_to_all | solution.py:21
  55.2 0.6 broadcast_in_dim.23
  55.8 3.3 %all-to-all-start = ((bf16[8,2,1152]{2,1,0:T(2,128)(2,1)}), bf16[8,2,1152]{2,1,0:T(2,128)(2,1)S(1)}, u32[]{:S(2)}, u32[]{:S(2)}) async-start(bf16[8,2,1152]{2,1,0:T(2,128)(2,1)} %broadcast_in_dim.23), calls=%async_computation | async-start | bytes 73728 | tf_op jit(solution)/shard_map/side/all_to_all | solution.py:21
  59.2 0.2 reduce_sum.21
  59.3 6.7 %all-to-all-done = bf16[8,2,1152]{2,1,0:T(2,128)(2,1)S(1)} async-done(((bf16[8,2,1152]{2,1,0:T(2,128)(2,1)}), bf16[8,2,1152]{2,1,0:T(2,128)(2,1)S(1)}, u32[]{:S(2)}, u32[]{:S(2)}) %all-to-all-start) | async-done | bytes 36896 | tf_op jit(solution)/shard_map/side/all_to_all | solution.py:21
  66.1 0.7 broadcast_in_dim.42
  66.8 0.0 copy-start.1
  66.8 3.5 %all-to-all-start.3 = ((bf16[8,16,1024]{2,1,0:T(8,128)(2,1)}), bf16[8,16,1024]{2,1,0:T(8,128)(2,1)S(1)}, u32[]{:S(2)}, u32[]{:S(2)}) async-start(bf16[8,16,1024]{2,1,0:T(8,128)(2,1)} %broadcast_in_dim.42), calls=%async_computation.3 | async-start | bytes 524288 | tf_op jit(solution)/shard_map/bias/all_to_all | solution.py:21
  70.4 9.9 %all-to-all-done.3 = bf16[8,16,1024]{2,1,0:T(8,128)(2,1)S(1)} async-done(((bf16[8,16,1024]{2,1,0:T(8,128)(2,1)}), bf16[8,16,1024]{2,1,0:T(8,128)(2,1)S(1)}, u32[]{:S(2)}, u32[]{:S(2)}) %all-to-all-start.3) | async-done | bytes 262176 | tf_op jit(solution)/shard_map/bias/all_to_all | solution.py:21
  80.4 0.0 copy-start.3
  80.4 0.6 copy-done.3
  81.0 1.2 broadcast_in_dim.43
  82.2 6.4 %all-to-all-start.4 = ((bf16[32,16,1152]{2,1,0:T(8,128)(2,1)}), bf16[32,16,1152]{2,1,0:T(8,128)(2,1)S(1)}, u32[]{:S(2)}, u32[]{:S(2)}) async-start(bf16[32,16,1152]{2,1,0:T(8,128)(2,1)} %broadcast_in_dim.43), calls=%async_computation.4 | async-start | bytes 2359296 | tf_op jit(solution)/shard_map/field/all_to_all | solution.py:21
  88.6 0.0 copy-done.1
  88.6 1.3 collective-permute-start.1
  89.9 4.7 %collective-permute-start = (bf16[16,96,128]{2,1,0:T(8,128)(2,1)S(1)}, bf16[16,96,128]{2,1,0:T(8,128)(2,1)}, u32[]{:S(2)}, u32[]{:S(2)}) collective-permute-start(bf16[16,96,128]{2,1,0:T(8,128)(2,1)S(1)} %copy-done.1), channel_id=1, source_target_pairs={{0,8},{8,16},{16,24},{24,32},{32,40},{40,48},{48,56},{56,64},{64,7... | collective-permute-start | bytes 1179656 | tf_op jit(solution)/shard_map/slots/ppermute | solution.py:27
  94.7 5.0 %copy.46 = bf16[96,24,1024]{2,0,1:T(8,128)(2,1)S(1)} copy(bf16[96,24,1024]{2,1,0:T(8,128)(2,1)} %param.10) | data formatting | bytes 9437184 | tf_op args[4]
  99.6 0.1 slice.31
  99.7 2.2 %slice.30 = bf16[18,96,1024]{2,1,0:T(8,128)(2,1)} slice(bf16[24,96,1024]{2,1,0:T(8,128)(2,1)S(1)} %bitcast.31), slice={[0:18], [0:96], [0:1024]} | slice | bytes 7077888 | tf_op jit(solution)/shard_map/operator/slice | solution.py:39
  101.9 0.1 broadcast_in_dim.44
  102.0 4.8 %pad_maximum_fusion = bf16[18,128,1024]{2,1,0:T(8,128)(2,1)} fusion(bf16[18,32,1024]{2,1,0:T(8,128)(2,1)S(1)} %bitcast.33, bf16[18,96,1024]{2,1,0:T(8,128)(2,1)} %slice.30), kind=kLoop, calls=%fused_computation.1 | loop fusion | flops 9437184 | bytes 9437184 | tf_op jit(solution)/shard_map/operator/concatenate | solution.py:39
  106.9 5.7 %collective-permute-done.1 = bf16[16,96,128]{2,1,0:T(8,128)(2,1)} collective-permute-done((bf16[16,96,128]{2,1,0:T(8,128)(2,1)S(1)}, bf16[16,96,128]{2,1,0:T(8,128)(2,1)}, u32[]{:S(2)}, u32[]{:S(2)}) %collective-permute-start.1) | collective-permute-done | bytes 393248 | tf_op jit(solution)/shard_map/slots/ppermute | solution.py:28
  112.6 0.0 collective-permute-done
  112.6 1.2 pad_maximum_fusion.1
  113.8 0.6 gather_fusion
  114.5 0.9 broadcast_select_fusion
  115.3 0.0 all-to-all-done.4
  115.3 0.0 copy-start.2
  115.3 5.0 %all-to-all-start.6 = ((bf16[8,2,96,128]{3,2,1,0:T(8,128)(2,1)}), bf16[8,2,96,128]{3,2,1,0:T(8,128)(2,1)S(1)}, u32[]{:S(2)}, u32[]{:S(2)}) async-start(bf16[8,2,96,128]{3,2,1,0:T(8,128)(2,1)} %broadcast_select_fusion), calls=%async_computation.6 | async-start | bytes 786432 | tf_op jit(solution)/shard_map/slots/all_to_all | solution.py:21
  120.3 0.9 fusion.16
  121.2 0.0 copy-done.2
  121.2 6.0 %convolution_convert_fusion = bf16[512,2304]{1,0:T(8,128)(2,1)S(1)} fusion(bf16[2304,1024]{1,0:T(8,128)(2,1)} %bitcast.34, bf16[512,1152]{1,0:T(8,128)(2,1)} %bitcast.44, s32[512]{0:T(512)S(1)} %fusion.16), kind=kOutput, calls=%fused_computation.3 | convolution fusion | flops 2954756096 | bytes 8128512 | tf_op jit(solution)/shard_map/operator/dot_general | solution.py:192
  127.2 2.3 %reshape.172 = bf16[256,2,2304]{2,1,0:T(2,128)(2,1)} reshape(bf16[512,2304]{1,0:T(8,128)(2,1)S(1)} %convolution_convert_fusion) | data formatting | bytes 4718592 | tf_op jit(solution)/shard_map/operator/reshape | solution.py:198
  129.5 0.0 all-to-all-done.6
  129.5 7.3 %all-to-all-start.5 = ((bf16[256,2,2304]{2,1,0:T(2,128)(2,1)}), bf16[256,2,2304]{2,1,0:T(2,128)(2,1)S(1)}, u32[]{:S(2)}, u32[]{:S(2)}) async-start(bf16[256,2,2304]{2,1,0:T(2,128)(2,1)} %reshape.172), calls=%async_computation.5 | async-start | bytes 4718592 | tf_op jit(solution)/shard_map/operator/all_to_all | solution.py:21
  136.8 0.8 copy.40
  137.6 58.4 %all-to-all-done.5 = bf16[256,2,2304]{2,1,0:T(2,128)(2,1)S(1)} async-done(((bf16[256,2,2304]{2,1,0:T(2,128)(2,1)}), bf16[256,2,2304]{2,1,0:T(2,128)(2,1)S(1)}, u32[]{:S(2)}, u32[]{:S(2)}) %all-to-all-start.5) | async-done | bytes 2359328 | tf_op jit(solution)/shard_map/operator/all_to_all | solution.py:21
  196.0 1.6 copy.47
  197.6 8.0 %propagate.1 = bf16[2,768,128]{2,1,0:T(8,128)(2,1)} custom-call(bf16[2,256,2304]{2,1,0:T(8,128)(2,1)} %bitcast.32, bf16[2,768,128]{2,1,0:T(8,128)(2,1)} %bitcast.37), custom_call_target="tpu_custom_call" | custom-call | tf_op jit(solution)/shard_map/taylor/propagate/pallas_call | solution.py:116
  205.6 1.8 copy.48
  207.4 4.9 %all-to-all-start.7 = ((bf16[8,2,96,128]{3,2,1,0:T(8,128)(2,1)}), bf16[8,2,96,128]{3,2,1,0:T(8,128)(2,1)S(1)}, u32[]{:S(2)}, u32[]{:S(2)}) async-start(bf16[8,2,96,128]{3,2,1,0:T(8,128)(2,1)} %bitcast.27), calls=%async_computation.7 | async-start | bytes 786432 | tf_op jit(solution)/shard_map/taylor/all_to_all | solution.py:21
  212.3 1.4 constant_dynamic-slice_fusion
  213.6 6.4 %all-to-all-done.7 = bf16[8,2,96,128]{3,2,1,0:T(8,128)(2,1)S(1)} async-done(((bf16[8,2,96,128]{3,2,1,0:T(8,128)(2,1)}), bf16[8,2,96,128]{3,2,1,0:T(8,128)(2,1)S(1)}, u32[]{:S(2)}, u32[]{:S(2)}) %all-to-all-start.7) | async-done | bytes 393248 | tf_op jit(solution)/shard_map/taylor/all_to_all | solution.py:21
  220.0 0.7 copy.51
  (9 shorter events, 0.1 us)
Async XLA Ops:
  0.6 26.4 %copy-start = (bf16[4,96,1024]{2,1,0:T(8,128)(2,1)S(1)}, bf16[4,96,1024]{2,1,0:T(8,128)(2,1)}, u32[]{:S(2)}) copy-start(bf16[4,96,1024]{2,1,0:T(8,128)(2,1)} %param.9) | copy-start | bytes 2359300
  27.1 11.2 %copy-start.4 = (s32[16]{0:T(128)S(1)}, s32[16]{0:T(128)}, u32[]{:S(2)}) copy-start(s32[16]{0:T(128)} %param.11) | copy-start | bytes 196
  28.8 26.4 %all-to-all-start.2 = ((bf16[32,16,1024]{2,1,0:T(8,128)(2,1)}), bf16[32,16,1024]{2,1,0:T(8,128)(2,1)S(1)}, u32[]{:S(2)}, u32[]{:S(2)}) async-start(bf16[32,16,1024]{2,1,0:T(8,128)(2,1)} %bitcast.4), calls=%async_computation.2 | async-start | bytes 2097152 | tf_op jit(solution)/shard_map/bias/all_to_all | solution.py:21
  55.8 10.3 %all-to-all-start = ((bf16[8,2,1152]{2,1,0:T(2,128)(2,1)}), bf16[8,2,1152]{2,1,0:T(2,128)(2,1)S(1)}, u32[]{:S(2)}, u32[]{:S(2)}) async-start(bf16[8,2,1152]{2,1,0:T(2,128)(2,1)} %broadcast_in_dim.23), calls=%async_computation | async-start | bytes 73728 | tf_op jit(solution)/shard_map/side/all_to_all | solution.py:21
  66.8 21.8 %copy-start.1 = (bf16[16,96,128]{2,1,0:T(8,128)(2,1)S(1)}, bf16[16,96,128]{2,1,0:T(8,128)(2,1)}, u32[]{:S(2)}) copy-start(bf16[16,96,128]{2,1,0:T(8,128)(2,1)} %param.6) | copy-start | bytes 1179652
  66.8 13.5 %all-to-all-start.3 = ((bf16[8,16,1024]{2,1,0:T(8,128)(2,1)}), bf16[8,16,1024]{2,1,0:T(8,128)(2,1)S(1)}, u32[]{:S(2)}, u32[]{:S(2)}) async-start(bf16[8,16,1024]{2,1,0:T(8,128)(2,1)} %broadcast_in_dim.42), calls=%async_computation.3 | async-start | bytes 524288 | tf_op jit(solution)/shard_map/bias/all_to_all | solution.py:21
  80.4 0.6 copy-start.3
  82.2 33.1 %all-to-all-start.4 = ((bf16[32,16,1152]{2,1,0:T(8,128)(2,1)}), bf16[32,16,1152]{2,1,0:T(8,128)(2,1)S(1)}, u32[]{:S(2)}, u32[]{:S(2)}) async-start(bf16[32,16,1152]{2,1,0:T(8,128)(2,1)} %broadcast_in_dim.43), calls=%async_computation.4 | async-start | bytes 2359296 | tf_op jit(solution)/shard_map/field/all_to_all | solution.py:21
  88.6 24.0 %collective-permute-start.1 = (bf16[16,96,128]{2,1,0:T(8,128)(2,1)S(1)}, bf16[16,96,128]{2,1,0:T(8,128)(2,1)}, u32[]{:S(2)}, u32[]{:S(2)}) collective-permute-start(bf16[16,96,128]{2,1,0:T(8,128)(2,1)S(1)} %copy-done.1), channel_id=1, source_target_pairs={{8,0},{16,8},{24,16},{32,24},{40,32},{48,40},{56,48},{64,56},{72,6... | collective-permute-start | bytes 1179656 | tf_op jit(solution)/shard_map/slots/ppermute | solution.py:28
  89.9 22.7 %collective-permute-start = (bf16[16,96,128]{2,1,0:T(8,128)(2,1)S(1)}, bf16[16,96,128]{2,1,0:T(8,128)(2,1)}, u32[]{:S(2)}, u32[]{:S(2)}) collective-permute-start(bf16[16,96,128]{2,1,0:T(8,128)(2,1)S(1)} %copy-done.1), channel_id=1, source_target_pairs={{0,8},{8,16},{16,24},{24,32},{32,40},{40,48},{48,56},{56,64},{64,7... | collective-permute-start | bytes 1179656 | tf_op jit(solution)/shard_map/slots/ppermute | solution.py:27
  115.3 5.9 %copy-start.2 = (bf16[32,16,1152]{2,1,0:T(8,128)(2,1)}, bf16[32,16,1152]{2,1,0:T(8,128)(2,1)S(1)}, u32[]{:S(2)}) copy-start(bf16[32,16,1152]{2,1,0:T(8,128)(2,1)S(1)} %all-to-all-done.4) | copy-start | bytes 3538948
  115.3 14.2 %all-to-all-start.6 = ((bf16[8,2,96,128]{3,2,1,0:T(8,128)(2,1)}), bf16[8,2,96,128]{3,2,1,0:T(8,128)(2,1)S(1)}, u32[]{:S(2)}, u32[]{:S(2)}) async-start(bf16[8,2,96,128]{3,2,1,0:T(8,128)(2,1)} %broadcast_select_fusion), calls=%async_computation.6 | async-start | bytes 786432 | tf_op jit(solution)/shard_map/slots/all_to_all | solution.py:21
  129.5 66.4 %all-to-all-start.5 = ((bf16[256,2,2304]{2,1,0:T(2,128)(2,1)}), bf16[256,2,2304]{2,1,0:T(2,128)(2,1)S(1)}, u32[]{:S(2)}, u32[]{:S(2)}) async-start(bf16[256,2,2304]{2,1,0:T(2,128)(2,1)} %reshape.172), calls=%async_computation.5 | async-start | bytes 4718592 | tf_op jit(solution)/shard_map/operator/all_to_all | solution.py:21
  207.4 12.6 %all-to-all-start.7 = ((bf16[8,2,96,128]{3,2,1,0:T(8,128)(2,1)}), bf16[8,2,96,128]{3,2,1,0:T(8,128)(2,1)S(1)}, u32[]{:S(2)}, u32[]{:S(2)}) async-start(bf16[8,2,96,128]{3,2,1,0:T(8,128)(2,1)} %bitcast.27), calls=%async_computation.7 | async-start | bytes 786432 | tf_op jit(solution)/shard_map/taylor/all_to_all | solution.py:21

commit v3 on v2

v3 whole, which is shorter than its diff:
```python
import math

import jax
import jax.numpy as jnp
from jax import lax
from jax.experimental import pallas as pl
from jax.experimental.pallas import tpu as pltpu
from jax.sharding import Mesh, PartitionSpec as P


time_step = 0.01
WIDE = ("z", "x")
WIDE_X = ("x", "z")
NARROW = ("y", "c")
PLANE = ("x", "y", "c")
MIXED = ("x", "y", "c", "z")
ALL = WIDE + NARROW
LANES = 128


def exchange(blocks, axes):
    return lax.all_to_all(blocks, axes, split_axis=0, concat_axis=0, tiled=True)


def ordered_kernel(at_ref, *refs):
    *piece_refs, out_ref = refs
    for k, piece_ref in enumerate(piece_refs):
        out_ref[at_ref[0] ^ k] = piece_ref[...]


def gathered(array, axis):
    count = lax.axis_size(axis)
    pieces = [array]
    for k in range(1, count):
        pieces.append(lax.ppermute(array, axis, [(i, i ^ k) for i in range(count)]))
    in_vmem = pl.BlockSpec(memory_space=pltpu.VMEM)
    return pl.pallas_call(
        ordered_kernel,
        in_specs=[pl.BlockSpec(memory_space=pltpu.SMEM)] + [in_vmem] * count,
        out_specs=in_vmem,
        out_shape=jax.ShapeDtypeStruct((count,) + array.shape, array.dtype),
        name="ordered",
    )(lax.axis_index(axis).astype(jnp.int32).reshape(1), *pieces)


def dealt(blocks, axes):
    count = lax.axis_size(axes)
    at = lax.axis_index(axes)
    pieces = []
    for k in range(count):
        piece = lax.dynamic_index_in_dim(blocks, at ^ k, 0, keepdims=False)
        if k:
            piece = lax.ppermute(piece, axes, [(i, i ^ k) for i in range(count)])
        pieces.append(piece)
    return pieces


def slot_walkers(walkers, offset, wide_count):
    up = [(i, (i + 1) % wide_count) for i in range(wide_count - 1)]
    down = [(j, i) for i, j in up]
    before = lax.ppermute(walkers, WIDE, up)
    after = lax.ppermute(walkers, WIDE, down)
    padded = jnp.concatenate([before, walkers, after], axis=0)
    return jnp.take(padded, offset, axis=0)


def packed_cholesky(cholesky):
    row_count, col_count, vectors = cholesky.shape
    by_col = cholesky.transpose(1, 0, 2)
    full = col_count * row_count // LANES
    rest = LANES - row_count
    tail = by_col[full:].reshape(full, rest, vectors)
    return jnp.concatenate([by_col[:full], tail], axis=1).reshape(full * LANES, vectors)


def propagate_kernel(at_ref, blocks_ref, *refs):
    *current_refs, out_ref, matrix_ref, term_ref, total_ref = refs
    share = blocks_ref.shape[0]
    f32, bf16 = jnp.float32, jnp.bfloat16
    lane = lax.broadcasted_iota(jnp.int32, (32, 128), 1)

    def assemble(s, carry):
        def rows_of(t, n):
            at = t * 128
            pieces = [
                blocks_ref[s, x * 64 + n * 8 : x * 64 + n * 8 + 8, at : at + 128]
                for x in range(4)
            ]
            return jnp.concatenate([piece.astype(f32) for piece in pieces], axis=0)

        for j in range(24):
            chunks = []
            for n in range(8):
                if j < 18:
                    chunk = rows_of(j, n)
                else:
                    q = 3 * (j - 18)
                    chunk = jnp.where(
                        lane < 32,
                        pltpu.roll(rows_of(q, n), 32, 1),
                        jnp.where(
                            lane < 64,
                            pltpu.roll(rows_of(q + 1, n), 64, 1),
                            pltpu.roll(rows_of(q + 2, n), 96, 1),
                        ),
                    )
                chunks.append(chunk)
            for half in range(2):
                first, second, third, fourth = chunks[4 * half : 4 * half + 4]
                second = pltpu.roll(second, 96, 1)
                third = pltpu.roll(third, 64, 1)
                fourth = pltpu.roll(fourth, 32, 1)
                tiles = (
                    jnp.where(lane < 96, first, second),
                    jnp.where(lane < 64, second, third),
                    jnp.where(lane < 32, third, fourth),
                )
                for k, tile in enumerate(tiles):
                    at = half * 384 + k * 128
                    matrix_ref[s, j * 32 : (j + 1) * 32, at : at + 128] = tile.astype(bf16)
        return carry

    lax.fori_loop(0, share, assemble, 0)
    narrow, _, rows_each, _ = out_ref.shape
    for k, current_ref in enumerate(current_refs):
        first_row = pl.multiple_of((at_ref[0] ^ k) * rows_each, 8)
        for s in range(share):
            start = current_ref[s].astype(f32)
            term_ref[s, pl.ds(first_row, rows_each), :] = start
            total_ref[s, pl.ds(first_row, rows_each), :] = start
    for degree in range(1, 5):
        for s in range(share):
            rows = [
                term_ref[s, pl.ds(x * 24 + j, 8, stride=96), :]
                for j in range(24)
                for x in range(4)
            ]
            ordered = jnp.concatenate(rows, axis=0).astype(bf16)
            product = lax.dot_general(
                ordered, matrix_ref[s], (((0,), (0,)), ((), ())), preferred_element_type=f32
            )
            product = product.T * (1.0 / degree)
            if degree < 4:
                product = product.astype(bf16).astype(f32)
                term_ref[s] = product
                total_ref[s] = total_ref[s] + product
            else:
                product = (total_ref[s] + product).astype(bf16)
                for n in range(narrow):
                    out_ref[n, s] = product[n * rows_each : (n + 1) * rows_each]


def propagate(narrow_at, blocks, current):
    narrow = len(current)
    share, rows_each, electrons = current[0].shape
    orbitals = narrow * rows_each
    f32, bf16 = jnp.float32, jnp.bfloat16
    in_vmem = pl.BlockSpec(memory_space=pltpu.VMEM)
    return pl.pallas_call(
        propagate_kernel,
        in_specs=[pl.BlockSpec(memory_space=pltpu.SMEM)] + [in_vmem] * (1 + narrow),
        out_specs=in_vmem,
        out_shape=jax.ShapeDtypeStruct((narrow, share, rows_each, electrons), bf16),
        scratch_shapes=[
            pltpu.VMEM((share, orbitals, orbitals), bf16),
            pltpu.VMEM((share, orbitals, electrons), f32),
            pltpu.VMEM((share, orbitals, electrons), f32),
        ],
        name="propagate",
    )(narrow_at.astype(jnp.int32).reshape(1), blocks, *current)


def per_device(walkers, intersection_inverse, noise, half_cholesky, cholesky, comb_source):
    walk_local, row_count, electrons = walkers.shape
    vectors = cholesky.shape[2]
    z_count, x_count = lax.axis_size("z"), lax.axis_size("x")
    wide_count = z_count * x_count
    narrow_count = lax.axis_size(NARROW)
    plane_count = x_count * narrow_count
    share = walk_local // narrow_count
    rows_here = z_count * share
    z_at = lax.axis_index("z")
    wide_at = lax.axis_index(WIDE)
    narrow_at = lax.axis_index(NARROW)
    root_step = math.sqrt(time_step)
    f32, bf16, i32 = jnp.float32, jnp.bfloat16, jnp.int32

    packed = packed_cholesky(cholesky)

    offset = comb_source - (wide_at - 1) * walk_local
    chosen = slot_walkers(walkers, offset, wide_count)

    chosen = chosen.reshape(narrow_count, share, row_count, electrons)
    current = dealt(chosen, NARROW)

    own_noise = lax.dynamic_slice_in_dim(noise, narrow_at * share, share, 0)
    own_offset = lax.dynamic_slice_in_dim(offset, narrow_at * share, share, 0).astype(bf16)
    own_offset = jnp.broadcast_to(own_offset[:, None], (share, LANES))
    side = jnp.concatenate([own_noise, own_offset], axis=1)
    side = gathered(side, "z").reshape(rows_here, vectors + LANES)

    rotated = jnp.einsum(
        "wiq,wqp->wpi", walkers, intersection_inverse, preferred_element_type=f32
    ).astype(bf16)
    rotated = rotated.reshape(walk_local, z_count, x_count, -1).transpose(2, 1, 0, 3)
    pairs = exchange(rotated.reshape(wide_count, walk_local, -1), WIDE_X)

    pairs = pairs.reshape(x_count, z_count, narrow_count, share, -1).transpose(0, 2, 1, 3, 4)
    pairs = pairs.reshape(wide_count * walk_local, -1)
    partial = jnp.dot(pairs, half_cholesky.reshape(-1, vectors), preferred_element_type=f32)
    partial = partial.astype(bf16).reshape(plane_count, rows_here, vectors)
    partial = exchange(partial, PLANE)

    partial = jnp.sum(partial.astype(f32), axis=0).astype(bf16)
    partial = exchange(jnp.broadcast_to(partial[None], (z_count,) + partial.shape), ("z",))
    bias = jnp.sum(partial.astype(f32), axis=0)
    force_bias = lax.dynamic_slice_in_dim(bias, z_at * share, share, 0)

    aux = root_step * side[:, :vectors].astype(f32) + time_step * bias
    aux = jnp.concatenate([aux.astype(bf16), side[:, vectors:]], axis=1)
    aux = exchange(jnp.broadcast_to(aux[None], (plane_count,) + aux.shape), PLANE)
    aux = aux.reshape(plane_count * rows_here, vectors + LANES)
    slot = jnp.arange(plane_count * rows_here, dtype=i32)
    slot_x = slot // (narrow_count * rows_here)
    slot_z = (slot // share) % z_count
    source = aux[:, vectors].astype(i32) + (slot_z * x_count + slot_x - 1) * walk_local
    block, inner = source // walk_local, source % walk_local
    row = (block % x_count) * narrow_count + inner // share
    row = row * rows_here + (block // x_count) * share + inner % share
    pick = (row[:, None] == slot[None]).astype(bf16)
    fields = jnp.dot(pick, aux[:, :vectors], preferred_element_type=f32).astype(bf16)

    operator = lax.dot_general(
        fields,
        packed,
        (((1,), (1,)), ((), ())),
        preferred_element_type=f32,
    ).astype(bf16)
    operator = exchange(operator.reshape(wide_count * narrow_count, share, -1), MIXED)

    propagated = propagate(narrow_at, operator.transpose(1, 0, 2), current)
    new_walkers = exchange(propagated, NARROW)
    return (new_walkers.reshape(walk_local, row_count, electrons), force_bias)


def solution(mesh):
    fine = Mesh(mesh.devices.reshape(8, 4, 4, 2), ALL)
    in_specs = (
        P(WIDE, NARROW, None),
        P(WIDE, None, None),
        P(WIDE, None),
        P(WIDE, NARROW, None),
        P(NARROW, WIDE, None),
        P(WIDE),
    )
    out_specs = (P(WIDE, NARROW, None), P(ALL, None))

    return jax.shard_map(
        per_device, mesh=fine, in_specs=in_specs, out_specs=out_specs, check_vma=False
    )
```

time: 222 us -> 223 us (level)
  the two profiles are of different devices: /device:TPU:1 before, /device:TPU:96 now
where the time goes in v3:
time: 223 us; the launch traced here: 222 us
  waiting for transfers between devices  96.5 us (43%)
  starting transfers between devices  55 us (25%)
  blocking collectives  23.7 us (11%)
  local copies, waits for them, and re-layouts  20.5 us (9%)
  Pallas kernels  9.56 us (4%)
  matrix products  9.19 us (4%)
  other arithmetic  6.24 us (3%)
    ppermute x1, waiting for transfers between devices, slot_walkers(): after = lax.ppermute(walkers, WIDE, down)  51.4 us
    all_to_all x5, waiting for transfers between devices, exchange(): return lax.all_to_all(blocks, axes, split_axis=0, concat_axis=0, tiled=True)  34.1 us
    all_to_all x5, starting transfers between devices, exchange(): return lax.all_to_all(blocks, axes, split_axis=0, concat_axis=0, tiled=True)  27 us
    all_to_all x1, blocking collectives, exchange(): return lax.all_to_all(blocks, axes, split_axis=0, concat_axis=0, tiled=True)  23.7 us
    ppermute x7, starting transfers between devices, gathered(): pieces.append(lax.ppermute(array, axis, [(i, i ^ k) for i in range(count)]))  13.6 us
    pallas_call x1, Pallas kernels, propagate(): pl.pallas_call(propagate_kernel, in_specs=[pl.BlockSpec(memory_space=pltp...  8.15 us
    ppermute x7, starting transfers between devices, dealt(): piece = lax.ppermute(piece, axes, [(i, i ^ k) for i in range(count)])  8.1 us
    unnamed x34, local copies, waits for them, and re-layouts  7.03 us
  transfers between devices with their start and end apart: 21, of which 11 were waited for; matrix products, arithmetic and copies ran while one was open for 8% of the time, Pallas kernels for 1%

profile of v3, /device:TPU:96, one launch (start us, length us, event | category | flops | bytes accessed | tf_op | source)
XLA Modules:
  0.0 221.8 jit_solution(18056479523073360412)
XLA Ops:
  0.6 1.5 convolution_convert_fusion.3
  2.2 0.3 copy.24
  2.5 0.5 reshape.164
  3.0 0.1 copy.25
  3.1 23.7 %all_to_all.30 = bf16[32,16,384]{2,1,0:T(8,128)(2,1)S(1)} all-to-all(bf16[32,16,384]{2,1,0:T(8,128)(2,1)S(1)} %bitcast.49), channel_id=1, replica_groups=mesh['z'=8,'x'=4,'y'=4,'c'=2] {'x','z'}, dimensions={0} | all-to-all | bytes 786432 | tf_op jit(solution)/shard_map/all_to_all | solution.py:22
  26.8 0.1 reshape.166
  26.9 0.3 copy.34
  27.2 0.1 reshape.167
  27.4 1.7 convolution_convert_fusion.2
  29.1 5.6 %all-to-all-start.1 = ((bf16[32,16,1024]{2,1,0:T(8,128)(2,1)}), bf16[32,16,1024]{2,1,0:T(8,128)(2,1)S(1)}, u32[]{:S(2)}, u32[]{:S(2)}) async-start(bf16[32,16,1024]{2,1,0:T(8,128)(2,1)} %bitcast.6), calls=%async_computation.1 | async-start | bytes 2097152 | tf_op jit(solution)/shard_map/all_to_all | solution.py:22
  34.8 16.8 %all-to-all-done.1 = bf16[32,16,1024]{2,1,0:T(8,128)(2,1)S(1)} async-done(((bf16[32,16,1024]{2,1,0:T(8,128)(2,1)}), bf16[32,16,1024]{2,1,0:T(8,128)(2,1)S(1)}, u32[]{:S(2)}, u32[]{:S(2)}) %all-to-all-start.1) | async-done | bytes 1048608 | tf_op jit(solution)/shard_map/all_to_all | solution.py:22
  51.5 0.2 reduce_sum.21
  51.7 0.7 broadcast_in_dim.35
  52.4 5.1 %all-to-all-start.2 = ((bf16[8,16,1024]{2,1,0:T(8,128)(2,1)}), bf16[8,16,1024]{2,1,0:T(8,128)(2,1)S(1)}, u32[]{:S(2)}, u32[]{:S(2)}) async-start(bf16[8,16,1024]{2,1,0:T(8,128)(2,1)} %broadcast_in_dim.35), calls=%async_computation.2 | async-start | bytes 524288 | tf_op jit(solution)/shard_map/all_to_all | solution.py:22
  57.6 0.7 constant_dynamic-slice_fusion.1
  58.4 0.6 collective-permute-start
  59.1 0.1 collective-permute-start.1
  59.2 3.7 %collective-permute-start.2 = (bf16[2,1152]{1,0:T(2,128)(2,1)S(1)}, bf16[2,1152]{1,0:T(2,128)(2,1)S(1)}, u32[]{:S(2)}, u32[]{:S(2)}) collective-permute-start(bf16[2,1152]{1,0:T(2,128)(2,1)S(1)} %pad_maximum_fusion.3.refs_0_), channel_id=1, source_target_pairs={{0,96},{32,64},{64,32},{96,0},{128,224},{160,192},{192,160},{224,1... | collective-permute-start | bytes 13832 | tf_op jit(solution)/shard_map/ppermute | solution.py:35
  62.9 2.7 %collective-permute-start.3 = (bf16[2,1152]{1,0:T(2,128)(2,1)S(1)}, bf16[2,1152]{1,0:T(2,128)(2,1)S(1)}, u32[]{:S(2)}, u32[]{:S(2)}) collective-permute-start(bf16[2,1152]{1,0:T(2,128)(2,1)S(1)} %pad_maximum_fusion.3.refs_0_), channel_id=1, source_target_pairs={{0,128},{32,160},{64,192},{96,224},{128,0},{160,32},{192,64},{224,... | collective-permute-start | bytes 13832 | tf_op jit(solution)/shard_map/ppermute | solution.py:35
  65.6 1.5 collective-permute-start.4
  67.0 4.5 %collective-permute-start.5 = (bf16[2,1152]{1,0:T(2,128)(2,1)S(1)}, bf16[2,1152]{1,0:T(2,128)(2,1)S(1)}, u32[]{:S(2)}, u32[]{:S(2)}) collective-permute-start(bf16[2,1152]{1,0:T(2,128)(2,1)S(1)} %pad_maximum_fusion.3.refs_0_), channel_id=1, source_target_pairs={{0,192},{32,224},{64,128},{96,160},{128,64},{160,96},{192,0},{224,... | collective-permute-start | bytes 13832 | tf_op jit(solution)/shard_map/ppermute | solution.py:35
  71.5 0.6 collective-permute-start.6
  72.1 0.1 collective-permute-done.4.refs_5_
  72.2 0.9 collective-permute-done.5.refs_6_
  73.1 3.2 %collective-permute-done.6.refs_7_ = bf16[2,1152]{1,0:T(2,128)(2,1)S(1)} collective-permute-done((bf16[2,1152]{1,0:T(2,128)(2,1)S(1)}, bf16[2,1152]{1,0:T(2,128)(2,1)S(1)}, u32[]{:S(2)}, u32[]{:S(2)}) %collective-permute-start.6) | collective-permute-done | bytes 4640 | tf_op jit(solution)/shard_map/ppermute | solution.py:35
  76.4 0.5 copy-done.14
  76.9 1.4 ordered.1
  78.4 0.8 reshape.163
  79.2 0.6 copy-done.3
  79.9 1.1 broadcast_in_dim.36
  81.0 4.2 %all-to-all-start.3 = ((bf16[32,16,1152]{2,1,0:T(8,128)(2,1)}), bf16[32,16,1152]{2,1,0:T(8,128)(2,1)S(1)}, u32[]{:S(2)}, u32[]{:S(2)}) async-start(bf16[32,16,1152]{2,1,0:T(8,128)(2,1)} %broadcast_in_dim.36), calls=%async_computation.3 | async-start | bytes 2359296 | tf_op jit(solution)/shard_map/all_to_all | solution.py:22
  85.2 5.0 %copy.32 = bf16[96,24,1024]{2,0,1:T(8,128)(2,1)S(1)} copy(bf16[96,24,1024]{2,1,0:T(8,128)(2,1)} %param.10) | data formatting | bytes 9437184 | tf_op args[4]
  90.2 0.1 slice.31
  90.3 0.4 slice.30
  90.7 2.6 %pad_maximum_fusion = bf16[18,128,1024]{2,1,0:T(8,128)(2,1)} fusion(bf16[18,32,1024]{2,1,0:T(8,128)(2,1)S(1)} %bitcast.45, bf16[18,96,1024]{2,1,0:T(8,128)(2,1)S(1)} %slice.30), kind=kLoop, calls=%fused_computation.1 | loop fusion | flops 9437184 | bytes 9437184 | tf_op jit(solution)/shard_map/concatenate | solution.py:73
  93.4 9.9 %all-to-all-done.3 = bf16[32,16,1152]{2,1,0:T(8,128)(2,1)S(1)} async-done(((bf16[32,16,1152]{2,1,0:T(8,128)(2,1)}), bf16[32,16,1152]{2,1,0:T(8,128)(2,1)S(1)}, u32[]{:S(2)}, u32[]{:S(2)}) %all-to-all-start.3) | async-done | bytes 1179680 | tf_op jit(solution)/shard_map/all_to_all | solution.py:22
  103.3 0.9 fusion.16
  104.2 0.1 copy-done.2
  104.3 6.0 %convolution_convert_fusion = bf16[512,2304]{1,0:T(8,128)(2,1)S(1)} fusion(bf16[2304,1024]{1,0:T(8,128)(2,1)} %bitcast.46, bf16[512,1152]{1,0:T(8,128)(2,1)} %bitcast.53, s32[512]{0:T(512)S(1)} %fusion.16), kind=kOutput, calls=%fused_computation.3 | convolution fusion | flops 2954756096 | bytes 8128512 | tf_op jit(solution)/shard_map/dot_general | solution.py:233
  110.3 2.4 %reshape.173 = bf16[256,2,2304]{2,1,0:T(2,128)(2,1)} reshape(bf16[512,2304]{1,0:T(8,128)(2,1)S(1)} %convolution_convert_fusion) | data formatting | bytes 4718592 | tf_op jit(solution)/shard_map/reshape | solution.py:239
  112.7 8.6 %all-to-all-start.4 = ((bf16[256,2,2304]{2,1,0:T(2,128)(2,1)}), bf16[256,2,2304]{2,1,0:T(2,128)(2,1)S(1)}, u32[]{:S(2)}, u32[]{:S(2)}) async-start(bf16[256,2,2304]{2,1,0:T(2,128)(2,1)} %reshape.173), calls=%async_computation.4 | async-start | bytes 4718592 | tf_op jit(solution)/shard_map/all_to_all | solution.py:22
  121.2 4.4 %collective-permute-start.8 = (bf16[16,96,128]{2,1,0:T(8,128)(2,1)S(1)}, bf16[16,96,128]{2,1,0:T(8,128)(2,1)}, u32[]{:S(2)}, u32[]{:S(2)}) collective-permute-start(bf16[16,96,128]{2,1,0:T(8,128)(2,1)S(1)} %copy-done.1), channel_id=1, source_target_pairs={{8,0},{16,8},{24,16},{32,24},{40,32},{48,40},{56,48},{64,56},{72,6... | collective-permute-start | bytes 1179656 | tf_op jit(solution)/shard_map/ppermute | solution.py:62
  125.6 1.9 collective-permute-start.7
  127.7 51.4 %collective-permute-done.8 = bf16[16,96,128]{2,1,0:T(8,128)(2,1)} collective-permute-done((bf16[16,96,128]{2,1,0:T(8,128)(2,1)S(1)}, bf16[16,96,128]{2,1,0:T(8,128)(2,1)}, u32[]{:S(2)}, u32[]{:S(2)}) %collective-permute-start.8) | collective-permute-done | bytes 393248 | tf_op jit(solution)/shard_map/ppermute | solution.py:62
  179.1 3.8 %collective-permute-done.7 = bf16[16,96,128]{2,1,0:T(8,128)(2,1)} collective-permute-done((bf16[16,96,128]{2,1,0:T(8,128)(2,1)S(1)}, bf16[16,96,128]{2,1,0:T(8,128)(2,1)}, u32[]{:S(2)}, u32[]{:S(2)}) %collective-permute-start.7) | collective-permute-done | bytes 393248 | tf_op jit(solution)/shard_map/ppermute | solution.py:61
  182.8 2.3 %pad_maximum_fusion.1 = bf16[48,96,128]{2,1,0:T(8,128)(2,1)} fusion(bf16[16,96,128]{2,1,0:T(8,128)(2,1)} %collective-permute-done.8, bf16[16,96,128]{2,1,0:T(8,128)(2,1)S(1)} %copy-done.1, bf16[16,96,128]{2,1,0:T(8,128)(2,1)} %collective-permute-done.7), kind=kLoop, calls=%fused_computation.8 | loop fusion | flops 1179648 | bytes 2359296 | tf_op jit(solution)/shard_map/concatenate | solution.py:63
  185.1 1.9 gather_fusion
  187.0 0.1 broadcast_select_fusion
  187.1 0.7 dynamic-slice_bitcast_fusion
  187.7 1.5 collective-permute-start.10
  189.2 0.4 collective-permute-start.11
  189.6 3.0 %collective-permute-start.12 = (bf16[2,96,128]{2,1,0:T(8,128)(2,1)S(1)}, bf16[2,96,128]{2,1,0:T(8,128)(2,1)}, u32[]{:S(2)}, u32[]{:S(2)}) collective-permute-start(bf16[2,96,128]{2,1,0:T(8,128)(2,1)S(1)} %get-tuple-element.7), channel_id=1, source_target_pairs={{0,4},{1,5},{2,6},{3,7},{4,0},{5,1},{6,2},{7,3},{8,12},{9,13},{10,... | collective-permute-start | bytes 147464 | tf_op jit(solution)/shard_map/ppermute | solution.py:53
  192.6 0.1 collective-permute-start.13
  192.8 2.9 %collective-permute-start.14 = (bf16[2,96,128]{2,1,0:T(8,128)(2,1)S(1)}, bf16[2,96,128]{2,1,0:T(8,128)(2,1)}, u32[]{:S(2)}, u32[]{:S(2)}) collective-permute-start(bf16[2,96,128]{2,1,0:T(8,128)(2,1)S(1)} %get-tuple-element.5), channel_id=1, source_target_pairs={{0,6},{1,7},{2,4},{3,5},{4,2},{5,3},{6,0},{7,1},{8,14},{9,15},{10,... | collective-permute-start | bytes 147464 | tf_op jit(solution)/shard_map/ppermute | solution.py:53
  195.6 0.2 collective-permute-start.15
  195.9 1.6 copy.33
  197.5 0.7 collective-permute-done.13.refs_5_
  198.2 1.1 collective-permute-done.14.refs_6_
  199.3 1.3 collective-permute-done.15.refs_7_
  200.6 8.2 %propagate.1 = bf16[8,2,96,128]{3,2,1,0:T(8,128)(2,1)} custom-call(s32[1]{0:T(128)} %bitcast.at_ref, bf16[2,256,2304]{2,1,0:T(8,128)(2,1)} %bitcast.44, bf16[2,96,128]{2,1,0:T(8,128)(2,1)} %get-tuple-element.11.refs_0_, bf16[2,96,128]{2,1,0:T(8,128)(2,1)} %copy-done.4, bf16[2,96,128]{2,1,0:T(8,128)(2,1)} %copy-done.5, bf16[2,96,128]{2,1,0:T(8,128)(2,1)} %copy-done.6, ...), custom_call_target="tpu_custom_call" | custom-call | tf_op jit(solution)/shard_map/propagate/pallas_call | solution.py:159
  208.7 3.5 %all-to-all-start.5 = ((bf16[8,2,96,128]{3,2,1,0:T(8,128)(2,1)}), bf16[8,2,96,128]{3,2,1,0:T(8,128)(2,1)S(1)}, u32[]{:S(2)}, u32[]{:S(2)}) async-start(bf16[8,2,96,128]{3,2,1,0:T(8,128)(2,1)} %propagate.1), calls=%async_computation.5 | async-start | bytes 786432 | tf_op jit(solution)/shard_map/all_to_all | solution.py:22
  212.2 1.4 constant_dynamic-slice_fusion
  213.6 7.5 %all-to-all-done.5 = bf16[8,2,96,128]{3,2,1,0:T(8,128)(2,1)S(1)} async-done(((bf16[8,2,96,128]{3,2,1,0:T(8,128)(2,1)}), bf16[8,2,96,128]{3,2,1,0:T(8,128)(2,1)S(1)}, u32[]{:S(2)}, u32[]{:S(2)}) %all-to-all-start.5) | async-done | bytes 393248 | tf_op jit(solution)/shard_map/all_to_all | solution.py:22
  221.0 0.7 copy.36
  (51 shorter events, 0.4 us)
Async XLA Ops:
  0.6 26.7 %copy-start = (bf16[4,96,1024]{2,1,0:T(8,128)(2,1)S(1)}, bf16[4,96,1024]{2,1,0:T(8,128)(2,1)}, u32[]{:S(2)}) copy-start(bf16[4,96,1024]{2,1,0:T(8,128)(2,1)} %param.9) | copy-start | bytes 2359300
  27.4 7.4 %copy-start.15 = (s32[16]{0:T(128)S(1)}, s32[16]{0:T(128)}, u32[]{:S(2)}) copy-start(s32[16]{0:T(128)} %param.11) | copy-start | bytes 196
  29.1 22.4 %all-to-all-start.1 = ((bf16[32,16,1024]{2,1,0:T(8,128)(2,1)}), bf16[32,16,1024]{2,1,0:T(8,128)(2,1)S(1)}, u32[]{:S(2)}, u32[]{:S(2)}) async-start(bf16[32,16,1024]{2,1,0:T(8,128)(2,1)} %bitcast.6), calls=%async_computation.1 | async-start | bytes 2097152 | tf_op jit(solution)/shard_map/all_to_all | solution.py:22
  52.4 26.8 %all-to-all-start.2 = ((bf16[8,16,1024]{2,1,0:T(8,128)(2,1)}), bf16[8,16,1024]{2,1,0:T(8,128)(2,1)S(1)}, u32[]{:S(2)}, u32[]{:S(2)}) async-start(bf16[8,16,1024]{2,1,0:T(8,128)(2,1)} %broadcast_in_dim.35), calls=%async_computation.2 | async-start | bytes 524288 | tf_op jit(solution)/shard_map/all_to_all | solution.py:22
  58.4 17.9 %copy-start.7 = (bf16[2,1152]{1,0:T(2,128)(2,1)}, bf16[2,1152]{1,0:T(2,128)(2,1)S(1)}, u32[]{:S(2)}) copy-start(bf16[2,1152]{1,0:T(2,128)(2,1)S(1)} %pad_maximum_fusion.3.refs_0_) | copy-start | bytes 13828
  58.4 8.6 %collective-permute-start = (bf16[2,1152]{1,0:T(2,128)(2,1)S(1)}, bf16[2,1152]{1,0:T(2,128)(2,1)S(1)}, u32[]{:S(2)}, u32[]{:S(2)}) collective-permute-start(bf16[2,1152]{1,0:T(2,128)(2,1)S(1)} %pad_maximum_fusion.3.refs_0_), channel_id=1, source_target_pairs={{0,32},{32,0},{64,96},{96,64},{128,160},{160,128},{192,224},{224,1... | collective-permute-start | bytes 13832 | tf_op jit(solution)/shard_map/ppermute | solution.py:35
  59.1 12.4 %collective-permute-start.1 = (bf16[2,1152]{1,0:T(2,128)(2,1)S(1)}, bf16[2,1152]{1,0:T(2,128)(2,1)S(1)}, u32[]{:S(2)}, u32[]{:S(2)}) collective-permute-start(bf16[2,1152]{1,0:T(2,128)(2,1)S(1)} %pad_maximum_fusion.3.refs_0_), channel_id=1, source_target_pairs={{0,64},{32,96},{64,0},{96,32},{128,192},{160,224},{192,128},{224,1... | collective-permute-start | bytes 13832 | tf_op jit(solution)/shard_map/ppermute | solution.py:35
  59.2 12.9 %collective-permute-start.2 = (bf16[2,1152]{1,0:T(2,128)(2,1)S(1)}, bf16[2,1152]{1,0:T(2,128)(2,1)S(1)}, u32[]{:S(2)}, u32[]{:S(2)}) collective-permute-start(bf16[2,1152]{1,0:T(2,128)(2,1)S(1)} %pad_maximum_fusion.3.refs_0_), channel_id=1, source_target_pairs={{0,96},{32,64},{64,32},{96,0},{128,224},{160,192},{192,160},{224,1... | collective-permute-start | bytes 13832 | tf_op jit(solution)/shard_map/ppermute | solution.py:35
  62.9 9.2 %collective-permute-start.3 = (bf16[2,1152]{1,0:T(2,128)(2,1)S(1)}, bf16[2,1152]{1,0:T(2,128)(2,1)S(1)}, u32[]{:S(2)}, u32[]{:S(2)}) collective-permute-start(bf16[2,1152]{1,0:T(2,128)(2,1)S(1)} %pad_maximum_fusion.3.refs_0_), channel_id=1, source_target_pairs={{0,128},{32,160},{64,192},{96,224},{128,0},{160,32},{192,64},{224,... | collective-permute-start | bytes 13832 | tf_op jit(solution)/shard_map/ppermute | solution.py:35
  65.6 6.6 %collective-permute-start.4 = (bf16[2,1152]{1,0:T(2,128)(2,1)S(1)}, bf16[2,1152]{1,0:T(2,128)(2,1)S(1)}, u32[]{:S(2)}, u32[]{:S(2)}) collective-permute-start(bf16[2,1152]{1,0:T(2,128)(2,1)S(1)} %pad_maximum_fusion.3.refs_0_), channel_id=1, source_target_pairs={{0,160},{32,128},{64,224},{96,192},{128,32},{160,0},{192,96},{224,... | collective-permute-start | bytes 13832 | tf_op jit(solution)/shard_map/ppermute | solution.py:35
  67.0 9.3 %copy-start.8 = (bf16[2,1152]{1,0:T(2,128)(2,1)}, bf16[2,1152]{1,0:T(2,128)(2,1)S(1)}, u32[]{:S(2)}) copy-start(bf16[2,1152]{1,0:T(2,128)(2,1)S(1)} %collective-permute-done.refs_1_) | copy-start | bytes 13828
  67.0 6.1 %collective-permute-start.5 = (bf16[2,1152]{1,0:T(2,128)(2,1)S(1)}, bf16[2,1152]{1,0:T(2,128)(2,1)S(1)}, u32[]{:S(2)}, u32[]{:S(2)}) collective-permute-start(bf16[2,1152]{1,0:T(2,128)(2,1)S(1)} %pad_maximum_fusion.3.refs_0_), channel_id=1, source_target_pairs={{0,192},{32,224},{64,128},{96,160},{128,64},{160,96},{192,0},{224,... | collective-permute-start | bytes 13832 | tf_op jit(solution)/shard_map/ppermute | solution.py:35
  71.5 4.8 %copy-start.9 = (bf16[2,1152]{1,0:T(2,128)(2,1)}, bf16[2,1152]{1,0:T(2,128)(2,1)S(1)}, u32[]{:S(2)}) copy-start(bf16[2,1152]{1,0:T(2,128)(2,1)S(1)} %collective-permute-done.1.refs_2_) | copy-start | bytes 13828
  71.5 4.8 %collective-permute-start.6 = (bf16[2,1152]{1,0:T(2,128)(2,1)S(1)}, bf16[2,1152]{1,0:T(2,128)(2,1)S(1)}, u32[]{:S(2)}, u32[]{:S(2)}) collective-permute-start(bf16[2,1152]{1,0:T(2,128)(2,1)S(1)} %pad_maximum_fusion.3.refs_0_), channel_id=1, source_target_pairs={{0,224},{32,192},{64,160},{96,128},{128,96},{160,64},{192,32},{224... | collective-permute-start | bytes 13832 | tf_op jit(solution)/shard_map/ppermute | solution.py:35
  72.1 4.3 %copy-start.10 = (bf16[2,1152]{1,0:T(2,128)(2,1)}, bf16[2,1152]{1,0:T(2,128)(2,1)S(1)}, u32[]{:S(2)}) copy-start(bf16[2,1152]{1,0:T(2,128)(2,1)S(1)} %collective-permute-done.2.refs_3_) | copy-start | bytes 13828
  72.1 4.3 %copy-start.11 = (bf16[2,1152]{1,0:T(2,128)(2,1)}, bf16[2,1152]{1,0:T(2,128)(2,1)S(1)}, u32[]{:S(2)}) copy-start(bf16[2,1152]{1,0:T(2,128)(2,1)S(1)} %collective-permute-done.3.refs_4_) | copy-start | bytes 13828
  72.2 4.2 %copy-start.12 = (bf16[2,1152]{1,0:T(2,128)(2,1)}, bf16[2,1152]{1,0:T(2,128)(2,1)S(1)}, u32[]{:S(2)}) copy-start(bf16[2,1152]{1,0:T(2,128)(2,1)S(1)} %collective-permute-done.4.refs_5_) | copy-start | bytes 13828
  73.1 3.3 %copy-start.13 = (bf16[2,1152]{1,0:T(2,128)(2,1)}, bf16[2,1152]{1,0:T(2,128)(2,1)S(1)}, u32[]{:S(2)}) copy-start(bf16[2,1152]{1,0:T(2,128)(2,1)S(1)} %collective-permute-done.5.refs_6_) | copy-start | bytes 13828
  76.3 0.6 copy-start.14
  79.2 0.6 copy-start.3
  81.0 22.3 %all-to-all-start.3 = ((bf16[32,16,1152]{2,1,0:T(8,128)(2,1)}), bf16[32,16,1152]{2,1,0:T(8,128)(2,1)S(1)}, u32[]{:S(2)}, u32[]{:S(2)}) async-start(bf16[32,16,1152]{2,1,0:T(8,128)(2,1)} %broadcast_in_dim.36), calls=%async_computation.3 | async-start | bytes 2359296 | tf_op jit(solution)/shard_map/all_to_all | solution.py:22
  103.3 1.0 copy-start.2
  112.7 8.6 %copy-start.1 = (bf16[16,96,128]{2,1,0:T(8,128)(2,1)S(1)}, bf16[16,96,128]{2,1,0:T(8,128)(2,1)}, u32[]{:S(2)}) copy-start(bf16[16,96,128]{2,1,0:T(8,128)(2,1)} %param.6) | copy-start | bytes 1179652
  112.7 83.2 %all-to-all-start.4 = ((bf16[256,2,2304]{2,1,0:T(2,128)(2,1)}), bf16[256,2,2304]{2,1,0:T(2,128)(2,1)S(1)}, u32[]{:S(2)}, u32[]{:S(2)}) async-start(bf16[256,2,2304]{2,1,0:T(2,128)(2,1)} %reshape.173), calls=%async_computation.4 | async-start | bytes 4718592 | tf_op jit(solution)/shard_map/all_to_all | solution.py:22
  121.2 57.8 %collective-permute-start.8 = (bf16[16,96,128]{2,1,0:T(8,128)(2,1)S(1)}, bf16[16,96,128]{2,1,0:T(8,128)(2,1)}, u32[]{:S(2)}, u32[]{:S(2)}) collective-permute-start(bf16[16,96,128]{2,1,0:T(8,128)(2,1)S(1)} %copy-done.1), channel_id=1, source_target_pairs={{8,0},{16,8},{24,16},{32,24},{40,32},{48,40},{56,48},{64,56},{72,6... | collective-permute-start | bytes 1179656 | tf_op jit(solution)/shard_map/ppermute | solution.py:62
  125.6 57.2 %collective-permute-start.7 = (bf16[16,96,128]{2,1,0:T(8,128)(2,1)S(1)}, bf16[16,96,128]{2,1,0:T(8,128)(2,1)}, u32[]{:S(2)}, u32[]{:S(2)}) collective-permute-start(bf16[16,96,128]{2,1,0:T(8,128)(2,1)S(1)} %copy-done.1), channel_id=1, source_target_pairs={{0,8},{8,16},{16,24},{24,32},{32,40},{40,48},{48,56},{56,64},{64,7... | collective-permute-start | bytes 1179656 | tf_op jit(solution)/shard_map/ppermute | solution.py:61
  187.7 5.0 %collective-permute-start.9 = (bf16[2,96,128]{2,1,0:T(8,128)(2,1)S(1)}, bf16[2,96,128]{2,1,0:T(8,128)(2,1)S(1)}, u32[]{:S(2)}, u32[]{:S(2)}) collective-permute-start(bf16[2,96,128]{2,1,0:T(8,128)(2,1)S(1)} %get-tuple-element.10), channel_id=1, source_target_pairs={{0,1},{1,0},{2,3},{3,2},{4,5},{5,4},{6,7},{7,6},{8,9},{9,8},{10,11... | collective-permute-start | bytes 147464 | tf_op jit(solution)/shard_map/ppermute | solution.py:53
  187.7 7.9 %collective-permute-start.10 = (bf16[2,96,128]{2,1,0:T(8,128)(2,1)S(1)}, bf16[2,96,128]{2,1,0:T(8,128)(2,1)S(1)}, u32[]{:S(2)}, u32[]{:S(2)}) collective-permute-start(bf16[2,96,128]{2,1,0:T(8,128)(2,1)S(1)} %get-tuple-element.9), channel_id=1, source_target_pairs={{0,2},{1,3},{2,0},{3,1},{4,6},{5,7},{6,4},{7,5},{8,10},{9,11},{10,... | collective-permute-start | bytes 147464 | tf_op jit(solution)/shard_map/ppermute | solution.py:53
  189.2 8.3 %collective-permute-start.11 = (bf16[2,96,128]{2,1,0:T(8,128)(2,1)S(1)}, bf16[2,96,128]{2,1,0:T(8,128)(2,1)S(1)}, u32[]{:S(2)}, u32[]{:S(2)}) collective-permute-start(bf16[2,96,128]{2,1,0:T(8,128)(2,1)S(1)} %get-tuple-element.8), channel_id=1, source_target_pairs={{0,3},{1,2},{2,1},{3,0},{4,7},{5,6},{6,5},{7,4},{8,11},{9,10},{10,... | collective-permute-start | bytes 147464 | tf_op jit(solution)/shard_map/ppermute | solution.py:53
  189.6 7.9 %collective-permute-start.12 = (bf16[2,96,128]{2,1,0:T(8,128)(2,1)S(1)}, bf16[2,96,128]{2,1,0:T(8,128)(2,1)}, u32[]{:S(2)}, u32[]{:S(2)}) collective-permute-start(bf16[2,96,128]{2,1,0:T(8,128)(2,1)S(1)} %get-tuple-element.7), channel_id=1, source_target_pairs={{0,4},{1,5},{2,6},{3,7},{4,0},{5,1},{6,2},{7,3},{8,12},{9,13},{10,... | collective-permute-start | bytes 147464 | tf_op jit(solution)/shard_map/ppermute | solution.py:53
  192.6 5.6 %collective-permute-start.13 = (bf16[2,96,128]{2,1,0:T(8,128)(2,1)S(1)}, bf16[2,96,128]{2,1,0:T(8,128)(2,1)}, u32[]{:S(2)}, u32[]{:S(2)}) collective-permute-start(bf16[2,96,128]{2,1,0:T(8,128)(2,1)S(1)} %get-tuple-element.6), channel_id=1, source_target_pairs={{0,5},{1,4},{2,7},{3,6},{4,1},{5,0},{6,3},{7,2},{8,13},{9,12},{10,... | collective-permute-start | bytes 147464 | tf_op jit(solution)/shard_map/ppermute | solution.py:53
  192.7 4.8 %copy-start.4 = (bf16[2,96,128]{2,1,0:T(8,128)(2,1)}, bf16[2,96,128]{2,1,0:T(8,128)(2,1)S(1)}, u32[]{:S(2)}) copy-start(bf16[2,96,128]{2,1,0:T(8,128)(2,1)S(1)} %collective-permute-done.9.refs_1_) | copy-start | bytes 147460
  192.8 6.5 %collective-permute-start.14 = (bf16[2,96,128]{2,1,0:T(8,128)(2,1)S(1)}, bf16[2,96,128]{2,1,0:T(8,128)(2,1)}, u32[]{:S(2)}, u32[]{:S(2)}) collective-permute-start(bf16[2,96,128]{2,1,0:T(8,128)(2,1)S(1)} %get-tuple-element.5), channel_id=1, source_target_pairs={{0,6},{1,7},{2,4},{3,5},{4,2},{5,3},{6,0},{7,1},{8,14},{9,15},{10,... | collective-permute-start | bytes 147464 | tf_op jit(solution)/shard_map/ppermute | solution.py:53
  195.6 1.9 copy-start.5
  195.6 4.9 %collective-permute-start.15 = (bf16[2,96,128]{2,1,0:T(8,128)(2,1)S(1)}, bf16[2,96,128]{2,1,0:T(8,128)(2,1)}, u32[]{:S(2)}, u32[]{:S(2)}) collective-permute-start(bf16[2,96,128]{2,1,0:T(8,128)(2,1)S(1)} %get-tuple-element.4), channel_id=1, source_target_pairs={{0,7},{1,6},{2,5},{3,4},{4,3},{5,2},{6,1},{7,0},{8,15},{9,14},{10,... | collective-permute-start | bytes 147464 | tf_op jit(solution)/shard_map/ppermute | solution.py:53
  197.5 3.1 %copy-start.6 = (bf16[2,96,128]{2,1,0:T(8,128)(2,1)}, bf16[2,96,128]{2,1,0:T(8,128)(2,1)S(1)}, u32[]{:S(2)}) copy-start(bf16[2,96,128]{2,1,0:T(8,128)(2,1)S(1)} %collective-permute-done.11.refs_3_) | copy-start | bytes 147460
  208.7 12.3 %all-to-all-start.5 = ((bf16[8,2,96,128]{3,2,1,0:T(8,128)(2,1)}), bf16[8,2,96,128]{3,2,1,0:T(8,128)(2,1)S(1)}, u32[]{:S(2)}, u32[]{:S(2)}) async-start(bf16[8,2,96,128]{3,2,1,0:T(8,128)(2,1)} %propagate.1), calls=%async_computation.5 | async-start | bytes 786432 | tf_op jit(solution)/shard_map/all_to_all | solution.py:22

commit v4 on v3

--- a/solution.py
+++ b/solution.py
@@ -10,10 +10,9 @@
 
 time_step = 0.01
 WIDE = ("z", "x")
-WIDE_X = ("x", "z")
 NARROW = ("y", "c")
-PLANE = ("x", "y", "c")
-MIXED = ("x", "y", "c", "z")
+PLANE = ("x", "y")
+MIXED = ("c", "x", "y", "z")
 ALL = WIDE + NARROW
 LANES = 128
 
@@ -22,25 +21,83 @@
     return lax.all_to_all(blocks, axes, split_axis=0, concat_axis=0, tiled=True)
 
 
-def ordered_kernel(at_ref, *refs):
-    *piece_refs, out_ref = refs
-    for k, piece_ref in enumerate(piece_refs):
-        out_ref[at_ref[0] ^ k] = piece_ref[...]
+def ordered_kernel(at_ref, pieces_ref, out_ref):
+    for k in range(out_ref.shape[0]):
+        out_ref[at_ref[0] ^ k] = pieces_ref[k]
 
 
 def gathered(array, axis):
     count = lax.axis_size(axis)
-    pieces = [array]
-    for k in range(1, count):
-        pieces.append(lax.ppermute(array, axis, [(i, i ^ k) for i in range(count)]))
+    pieces = array[None]
+    while pieces.shape[0] < count:
+        bit = pieces.shape[0]
+        received = lax.ppermute(pieces, axis, [(i, i ^ bit) for i in range(count)])
+        pieces = jnp.concatenate([pieces, received], axis=0)
     in_vmem = pl.BlockSpec(memory_space=pltpu.VMEM)
     return pl.pallas_call(
         ordered_kernel,
-        in_specs=[pl.BlockSpec(memory_space=pltpu.SMEM)] + [in_vmem] * count,
+        in_specs=[pl.BlockSpec(memory_space=pltpu.SMEM), in_vmem],
         out_specs=in_vmem,
-        out_shape=jax.ShapeDtypeStruct((count,) + array.shape, array.dtype),
+        out_shape=jax.ShapeDtypeStruct(pieces.shape, array.dtype),
         name="ordered",
-    )(lax.axis_index(axis).astype(jnp.int32).reshape(1), *pieces)
+    )(lax.axis_index(axis).astype(jnp.int32).reshape(1), pieces)
+
+
+def operator_kernel(at_ref, own_ref, other_ref, packed_ref, out_ref, fields_ref):
+    f32, bf16, i32 = jnp.float32, jnp.bfloat16, jnp.int32
+    vectors = packed_ref.shape[1]
+    rows = own_ref.shape[0]
+    core_at = at_ref[0]
+
+    @pl.when(pl.program_id(0) == 0)
+    def _():
+        slot = lax.broadcasted_iota(i32, (rows, LANES), 0)
+        lane = lax.broadcasted_iota(i32, (rows, LANES), 1)
+        base = (((slot >> 1) & 7) * 4 + (slot >> 6) - 1) * 16
+        tables = (own_ref, other_ref)
+        for k, table in enumerate(tables):
+            source = table[:, vectors:].astype(f32).astype(i32) + base
+            block, inner = source >> 4, source & 15
+            row = (((inner >> 1) & 1) ^ core_at) * rows + (block & 3) * 64
+            row = row + (inner >> 2) * 16 + (block >> 2) * 2 + (inner & 1)
+            fields = jnp.zeros((rows, vectors), f32)
+            for half, picked in enumerate(tables):
+                hits = [
+                    (row == lane + (half * rows + at)).astype(f32).astype(bf16)
+                    for at in range(0, rows, LANES)
+                ]
+                pick = jnp.concatenate(hits, axis=1)
+                fields = fields + jnp.dot(
+                    pick, picked[:, :vectors], preferred_element_type=f32
+                )
+            fields_ref[k ^ core_at] = fields.astype(bf16)
+
+    for half in range(2):
+        product = lax.dot_general(
+            fields_ref[half], packed_ref[...], (((1,), (1,)), ((), ())), preferred_element_type=f32
+        )
+        out_ref[half * rows : (half + 1) * rows, :] = product.astype(bf16)
+
+
+def operator_rows(core_at, own, other, packed):
+    rows = own.shape[0]
+    columns, vectors = packed.shape
+    width = 384
+    whole = pl.BlockSpec(own.shape, lambda i: (0, 0))
+    return pl.pallas_call(
+        operator_kernel,
+        grid=(columns // width,),
+        in_specs=[
+            pl.BlockSpec(memory_space=pltpu.SMEM),
+            whole,
+            whole,
+            pl.BlockSpec((width, vectors), lambda i: (i, 0)),
+        ],
+        out_specs=pl.BlockSpec((2 * rows, width), lambda i: (0, i)),
+        out_shape=jax.ShapeDtypeStruct((2 * rows, columns), jnp.bfloat16),
+        scratch_shapes=[pltpu.VMEM((2, rows, vectors), jnp.bfloat16)],
+        name="operator_rows",
+    )(core_at.astype(jnp.int32).reshape(1), own, other, packed)
 
 
 def dealt(blocks, axes):
@@ -82,8 +139,9 @@
     def assemble(s, carry):
         def rows_of(t, n):
             at = t * 128
+            first = (n & 1) * 128 + (n >> 1) * 8
             pieces = [
-                blocks_ref[s, x * 64 + n * 8 : x * 64 + n * 8 + 8, at : at + 128]
+                blocks_ref[s, first + x * 32 : first + x * 32 + 8, at : at + 128]
                 for x in range(4)
             ]
             return jnp.concatenate([piece.astype(f32) for piece in pieces], axis=0)
@@ -176,14 +234,16 @@
     z_count, x_count = lax.axis_size("z"), lax.axis_size("x")
     wide_count = z_count * x_count
     narrow_count = lax.axis_size(NARROW)
-    plane_count = x_count * narrow_count
+    plane_count = lax.axis_size(PLANE)
+    core_at = lax.axis_index("c")
+    swap = [(0, 1), (1, 0)]
     share = walk_local // narrow_count
     rows_here = z_count * share
     z_at = lax.axis_index("z")
     wide_at = lax.axis_index(WIDE)
     narrow_at = lax.axis_index(NARROW)
     root_step = math.sqrt(time_step)
-    f32, bf16, i32 = jnp.float32, jnp.bfloat16, jnp.int32
+    f32, bf16 = jnp.float32, jnp.bfloat16
 
     packed = packed_cholesky(cholesky)
 
@@ -202,12 +262,18 @@
     rotated = jnp.einsum(
         "wiq,wqp->wpi", walkers, intersection_inverse, preferred_element_type=f32
     ).astype(bf16)
-    rotated = rotated.reshape(walk_local, z_count, x_count, -1).transpose(2, 1, 0, 3)
-    pairs = exchange(rotated.reshape(wide_count, walk_local, -1), WIDE_X)
-
-    pairs = pairs.reshape(x_count, z_count, narrow_count, share, -1).transpose(0, 2, 1, 3, 4)
-    pairs = pairs.reshape(wide_count * walk_local, -1)
-    partial = jnp.dot(pairs, half_cholesky.reshape(-1, vectors), preferred_element_type=f32)
+    rotated = rotated.reshape(walk_local, wide_count, -1).transpose(1, 0, 2)
+    pairs = exchange(rotated, WIDE)
+
+    y_count, core_count = lax.axis_size("y"), lax.axis_size("c")
+    pairs = pairs.reshape(z_count, x_count, y_count, core_count, share, -1)
+    pairs = pairs.transpose(3, 1, 2, 0, 4, 5).reshape(core_count, plane_count * rows_here, -1)
+    half_flat = half_cholesky.reshape(-1, vectors)
+    mine = lax.dynamic_index_in_dim(pairs, core_at, 0, keepdims=False)
+    theirs = lax.dynamic_index_in_dim(pairs, 1 - core_at, 0, keepdims=False)
+    sent = jnp.dot(theirs, half_flat, preferred_element_type=f32).astype(bf16)
+    received = lax.ppermute(sent, "c", swap)
+    partial = jnp.dot(mine, half_flat, preferred_element_type=f32) + received.astype(f32)
     partial = partial.astype(bf16).reshape(plane_count, rows_here, vectors)
     partial = exchange(partial, PLANE)
 
@@ -220,22 +286,9 @@
     aux = jnp.concatenate([aux.astype(bf16), side[:, vectors:]], axis=1)
     aux = exchange(jnp.broadcast_to(aux[None], (plane_count,) + aux.shape), PLANE)
     aux = aux.reshape(plane_count * rows_here, vectors + LANES)
-    slot = jnp.arange(plane_count * rows_here, dtype=i32)
-    slot_x = slot // (narrow_count * rows_here)
-    slot_z = (slot // share) % z_count
-    source = aux[:, vectors].astype(i32) + (slot_z * x_count + slot_x - 1) * walk_local
-    block, inner = source // walk_local, source % walk_local
-    row = (block % x_count) * narrow_count + inner // share
-    row = row * rows_here + (block // x_count) * share + inner % share
-    pick = (row[:, None] == slot[None]).astype(bf16)
-    fields = jnp.dot(pick, aux[:, :vectors], preferred_element_type=f32).astype(bf16)
-
-    operator = lax.dot_general(
-        fields,
-        packed,
-        (((1,), (1,)), ((), ())),
-        preferred_element_type=f32,
-    ).astype(bf16)
+    other = lax.ppermute(aux, "c", swap)
+
+    operator = operator_rows(core_at, aux, other, packed)
     operator = exchange(operator.reshape(wide_count * narrow_count, share, -1), MIXED)
 
     propagated = propagate(narrow_at, operator.transpose(1, 0, 2), current)

time: 223 us -> 217 us (0.973)
  the two profiles are of different devices: /device:TPU:96 before, /device:TPU:6 now
where the time goes in v4:
time: 217 us; the launch traced here: 216 us
  waiting for transfers between devices  94.7 us (44%)
  starting transfers between devices  54.2 us (25%)
  local copies, waits for them, and re-layouts  24.5 us (11%)
  Pallas kernels  18.2 us (8%)
  blocking collectives  14 us (6%)
  other arithmetic  5.98 us (3%)
  matrix products  3.21 us (1%)
    ppermute x1, waiting for transfers between devices, slot_walkers(): before = lax.ppermute(walkers, WIDE, up)  51.9 us
    all_to_all x5, starting transfers between devices, exchange(): return lax.all_to_all(blocks, axes, split_axis=0, concat_axis=0, tiled=True)  34.1 us
    all_to_all x5, waiting for transfers between devices, exchange(): return lax.all_to_all(blocks, axes, split_axis=0, concat_axis=0, tiled=True)  26.9 us
    all_to_all x1, blocking collectives, exchange(): return lax.all_to_all(blocks, axes, split_axis=0, concat_axis=0, tiled=True)  14 us
    ppermute x3, waiting for transfers between devices, gathered(): received = lax.ppermute(pieces, axis, [(i, i ^ bit) for i in range(count)])  8.83 us
    pallas_call x1, Pallas kernels, operator_rows(): pl.pallas_call(operator_kernel, grid=(columns // width,), in_specs=[pl.Bl...  8.66 us
    pallas_call x1, Pallas kernels, propagate(): pl.pallas_call(propagate_kernel, in_specs=[pl.BlockSpec(memory_space=pltp...  8.15 us
    unnamed x20, local copies, waits for them, and re-layouts  7.41 us
  transfers between devices with their start and end apart: 19, of which 12 were waited for; matrix products, arithmetic and copies ran while one was open for 9% of the time, Pallas kernels for 1%

profile of v4, /device:TPU:6, one launch (start us, length us, event | category | flops | bytes accessed | tf_op | source)
XLA Modules:
  0.0 215.8 jit_solution(12757279599664237511)
XLA Ops:
  0.6 1.5 convolution_convert_fusion.1
  2.2 0.3 copy.22
  2.5 0.4 reshape.62
  2.8 0.9 copy.23
  3.7 11.6 %all-to-all-start = ((bf16[32,16,384]{2,1,0:T(8,128)(2,1)}), bf16[32,16,384]{2,1,0:T(8,128)(2,1)S(1)}, u32[]{:S(2)}, u32[]{:S(2)}) async-start(bf16[32,16,384]{2,1,0:T(8,128)(2,1)} %copy.23), calls=%async_computation | async-start | bytes 786432 | tf_op jit(solution)/shard_map/all_to_all | solution.py:21
  15.3 14.0 %all-to-all-done = bf16[32,16,384]{2,1,0:T(8,128)(2,1)S(1)} async-done(((bf16[32,16,384]{2,1,0:T(8,128)(2,1)}), bf16[32,16,384]{2,1,0:T(8,128)(2,1)S(1)}, u32[]{:S(2)}, u32[]{:S(2)}) %all-to-all-start) | async-done | bytes 393248 | tf_op jit(solution)/shard_map/all_to_all | solution.py:21
  29.3 0.1 reshape.63
  29.4 0.3 copy.24
  29.8 0.8 constant_dynamic-slice_fusion.2
  30.6 0.4 convolution_convert_fusion
  31.0 0.1 collective-permute-start.3
  31.2 0.7 constant_dynamic-slice_fusion.3
  31.9 1.1 collective-permute-done.3
  33.0 1.3 add_convert_fusion
  34.3 7.5 %all-to-all-start.1 = ((bf16[16,16,1024]{2,1,0:T(8,128)(2,1)}), bf16[16,16,1024]{2,1,0:T(8,128)(2,1)S(1)}, u32[]{:S(2)}, u32[]{:S(2)}) async-start(bf16[16,16,1024]{2,1,0:T(8,128)(2,1)} %bitcast.9), calls=%async_computation.1 | async-start | bytes 1048576 | tf_op jit(solution)/shard_map/all_to_all | solution.py:21
  41.8 0.1 dynamic-slice_convert_fusion
  41.8 0.1 broadcast_in_dim.35
  41.9 0.7 collective-permute-start
  42.6 3.0 %collective-permute-done = bf16[1,2,1152]{2,1,0:T(2,128)(2,1)S(1)} collective-permute-done((bf16[1,2,1152]{2,1,0:T(2,128)(2,1)S(1)}, bf16[1,2,1152]{2,1,0:T(2,128)(2,1)S(1)}, u32[]{:S(2)}, u32[]{:S(2)}) %collective-permute-start) | collective-permute-done | bytes 4640 | tf_op jit(solution)/shard_map/ppermute | solution.py:34
  45.6 0.5 collective-permute-start.1
  46.2 5.3 %all-to-all-done.1 = bf16[16,16,1024]{2,1,0:T(8,128)(2,1)S(1)} async-done(((bf16[16,16,1024]{2,1,0:T(8,128)(2,1)}), bf16[16,16,1024]{2,1,0:T(8,128)(2,1)S(1)}, u32[]{:S(2)}, u32[]{:S(2)}) %all-to-all-start.1) | async-done | bytes 524320 | tf_op jit(solution)/shard_map/all_to_all | solution.py:21
  51.5 0.1 reduce_sum.21
  51.6 0.7 broadcast_in_dim.37
  52.3 3.4 %all-to-all-start.2 = ((bf16[8,16,1024]{2,1,0:T(8,128)(2,1)}), bf16[8,16,1024]{2,1,0:T(8,128)(2,1)S(1)}, u32[]{:S(2)}, u32[]{:S(2)}) async-start(bf16[8,16,1024]{2,1,0:T(8,128)(2,1)} %broadcast_in_dim.37), calls=%async_computation.2 | async-start | bytes 524288 | tf_op jit(solution)/shard_map/all_to_all | solution.py:21
  55.8 5.9 %collective-permute-start.2 = (bf16[4,2,1152]{2,1,0:T(2,128)(2,1)S(1)}, bf16[4,2,1152]{2,1,0:T(2,128)(2,1)S(1)}, u32[]{:S(2)}, u32[]{:S(2)}) collective-permute-start(bf16[4,2,1152]{2,1,0:T(2,128)(2,1)S(1)} %pad_maximum_fusion.4), channel_id=1, source_target_pairs={{0,128},{32,160},{64,192},{96,224},{128,0},{160,32},{192,64},{224,... | collective-permute-start | bytes 55304 | tf_op jit(solution)/shard_map/ppermute | solution.py:34
  61.7 5.8 %collective-permute-done.2 = bf16[4,2,1152]{2,1,0:T(2,128)(2,1)S(1)} collective-permute-done((bf16[4,2,1152]{2,1,0:T(2,128)(2,1)S(1)}, bf16[4,2,1152]{2,1,0:T(2,128)(2,1)S(1)}, u32[]{:S(2)}, u32[]{:S(2)}) %collective-permute-start.2) | collective-permute-done | bytes 18464 | tf_op jit(solution)/shard_map/ppermute | solution.py:34
  67.5 0.7 pad_maximum_fusion.2.pieces_ref
  68.2 1.4 ordered.1
  69.6 0.8 reshape.61
  70.5 0.6 copy-done.4
  71.1 14.0 %all_to_all.30 = bf16[16,16,1152]{2,1,0:T(8,128)(2,1)S(1)} all-to-all(bf16[16,16,1152]{2,1,0:T(8,128)(2,1)S(1)} %broadcast_in_dim.38), channel_id=1, replica_groups=mesh['z'=8,'x'=4,'y'=4,'c'=2] {'x','y'}, dimensions={0} | all-to-all | bytes 1179648 | tf_op jit(solution)/shard_map/all_to_all | solution.py:21
  85.1 5.2 %copy.39 = bf16[96,24,1024]{2,0,1:T(8,128)(2,1)S(1)} copy(bf16[96,24,1024]{2,1,0:T(8,128)(2,1)} %param.10) | data formatting | bytes 9437184 | tf_op args[4]
  90.3 0.4 slice.20
  90.7 0.1 slice.21
  90.9 2.7 %pad_maximum_fusion = bf16[18,128,1024]{2,1,0:T(8,128)(2,1)} fusion(bf16[18,32,1024]{2,1,0:T(8,128)(2,1)S(1)} %bitcast.56, bf16[18,96,1024]{2,1,0:T(8,128)(2,1)S(1)} %slice.20), kind=kLoop, calls=%fused_computation.1 | loop fusion | flops 9437184 | bytes 9437184 | tf_op jit(solution)/shard_map/concatenate | solution.py:130
  93.5 0.9 copy-done.3
  94.4 8.7 %operator_rows.1 = bf16[512,2304]{1,0:T(8,128)(2,1)} custom-call(s32[1]{0:T(128)} %bitcast.1.at_ref, bf16[256,1152]{1,0:T(8,128)(2,1)} %bitcast.59, bf16[256,1152]{1,0:T(8,128)(2,1)} %copy-done.3, bf16[2304,1024]{1,0:T(8,128)(2,1)} %bitcast.52), custom_call_target="tpu_custom_call" | custom-call | tf_op jit(solution)/shard_map/operator_rows/pallas_call | solution.py:87
  103.1 5.7 %reshape.70 = bf16[256,2,2304]{2,1,0:T(2,128)(2,1)} reshape(bf16[512,2304]{1,0:T(8,128)(2,1)} %operator_rows.1) | data formatting | bytes 4718592 | tf_op jit(solution)/shard_map/reshape | solution.py:292
  108.8 7.5 %all-to-all-start.4 = ((bf16[256,2,2304]{2,1,0:T(2,128)(2,1)}), bf16[256,2,2304]{2,1,0:T(2,128)(2,1)S(1)}, u32[]{:S(2)}, u32[]{:S(2)}) async-start(bf16[256,2,2304]{2,1,0:T(2,128)(2,1)} %reshape.70), calls=%async_computation.4 | async-start | bytes 4718592 | tf_op jit(solution)/shard_map/all_to_all | solution.py:21
  116.3 3.5 %collective-permute-start.5 = (bf16[16,96,128]{2,1,0:T(8,128)(2,1)S(1)}, bf16[16,96,128]{2,1,0:T(8,128)(2,1)}, u32[]{:S(2)}, u32[]{:S(2)}) collective-permute-start(bf16[16,96,128]{2,1,0:T(8,128)(2,1)S(1)} %copy-done.2), channel_id=1, source_target_pairs={{0,8},{8,16},{16,24},{24,32},{32,40},{40,48},{48,56},{56,64},{64,7... | collective-permute-start | bytes 1179656 | tf_op jit(solution)/shard_map/ppermute | solution.py:118
  119.8 2.4 %collective-permute-start.6 = (bf16[16,96,128]{2,1,0:T(8,128)(2,1)S(1)}, bf16[16,96,128]{2,1,0:T(8,128)(2,1)}, u32[]{:S(2)}, u32[]{:S(2)}) collective-permute-start(bf16[16,96,128]{2,1,0:T(8,128)(2,1)S(1)} %copy-done.2), channel_id=1, source_target_pairs={{8,0},{16,8},{24,16},{32,24},{40,32},{48,40},{56,48},{64,56},{72,6... | collective-permute-start | bytes 1179656 | tf_op jit(solution)/shard_map/ppermute | solution.py:119
  122.2 0.1 broadcast_in_dim.39
  122.3 51.9 %collective-permute-done.5 = bf16[16,96,128]{2,1,0:T(8,128)(2,1)} collective-permute-done((bf16[16,96,128]{2,1,0:T(8,128)(2,1)S(1)}, bf16[16,96,128]{2,1,0:T(8,128)(2,1)}, u32[]{:S(2)}, u32[]{:S(2)}) %collective-permute-start.5) | collective-permute-done | bytes 393248 | tf_op jit(solution)/shard_map/ppermute | solution.py:118
  174.2 3.2 %collective-permute-done.6 = bf16[16,96,128]{2,1,0:T(8,128)(2,1)} collective-permute-done((bf16[16,96,128]{2,1,0:T(8,128)(2,1)S(1)}, bf16[16,96,128]{2,1,0:T(8,128)(2,1)}, u32[]{:S(2)}, u32[]{:S(2)}) %collective-permute-start.6) | collective-permute-done | bytes 393248 | tf_op jit(solution)/shard_map/ppermute | solution.py:119
  177.4 2.2 %pad_maximum_fusion.1 = bf16[48,96,128]{2,1,0:T(8,128)(2,1)} fusion(bf16[16,96,128]{2,1,0:T(8,128)(2,1)} %collective-permute-done.6, bf16[16,96,128]{2,1,0:T(8,128)(2,1)S(1)} %copy-done.2, bf16[16,96,128]{2,1,0:T(8,128)(2,1)} %collective-permute-done.5), kind=kLoop, calls=%fused_computation.6 | loop fusion | flops 1179648 | bytes 2359296 | tf_op jit(solution)/shard_map/concatenate | solution.py:120
  179.6 1.9 gather_fusion
  181.5 0.1 broadcast_select_fusion
  181.6 0.7 dynamic-slice_bitcast_fusion
  182.3 2.6 %collective-permute-start.10 = (bf16[2,96,128]{2,1,0:T(8,128)(2,1)S(1)}, bf16[2,96,128]{2,1,0:T(8,128)(2,1)S(1)}, u32[]{:S(2)}, u32[]{:S(2)}) collective-permute-start(bf16[2,96,128]{2,1,0:T(8,128)(2,1)S(1)} %get-tuple-element.7), channel_id=1, source_target_pairs={{0,4},{1,5},{2,6},{3,7},{4,0},{5,1},{6,2},{7,3},{8,12},{9,13},{10,... | collective-permute-start | bytes 147464 | tf_op jit(solution)/shard_map/ppermute | solution.py:110
  184.9 2.6 %collective-permute-start.12 = (bf16[2,96,128]{2,1,0:T(8,128)(2,1)S(1)}, bf16[2,96,128]{2,1,0:T(8,128)(2,1)S(1)}, u32[]{:S(2)}, u32[]{:S(2)}) collective-permute-start(bf16[2,96,128]{2,1,0:T(8,128)(2,1)S(1)} %get-tuple-element.5), channel_id=1, source_target_pairs={{0,6},{1,7},{2,4},{3,5},{4,2},{5,3},{6,0},{7,1},{8,14},{9,15},{10,... | collective-permute-start | bytes 147464 | tf_op jit(solution)/shard_map/ppermute | solution.py:110
  187.5 1.0 collective-permute-start.13
  188.5 0.0 collective-permute-start.7
  188.5 0.3 collective-permute-start.8
  188.9 1.1 collective-permute-done.11.refs_5_
  189.9 0.5 collective-permute-start.9
  190.4 1.7 copy.40
  192.1 0.3 collective-permute-done.13.refs_7_
  192.3 0.5 collective-permute-done.8.refs_2_
  192.8 1.1 collective-permute-done.9.refs_3_
  193.8 8.2 %propagate.1 = bf16[8,2,96,128]{3,2,1,0:T(8,128)(2,1)} custom-call(s32[1]{0:T(128)} %bitcast.at_ref, bf16[2,256,2304]{2,1,0:T(8,128)(2,1)} %bitcast.55, bf16[2,96,128]{2,1,0:T(8,128)(2,1)} %get-tuple-element.11.refs_0_, bf16[2,96,128]{2,1,0:T(8,128)(2,1)} %collective-permute-done.7.refs_1_, bf16[2,96,128]{2,1,0:T(8,128)(2,1)} %collective-permute-done.8.refs_2_, ...), custom_call_target="tpu_custom_call" | custom-call | tf_op jit(solution)/shard_map/propagate/pallas_call | solution.py:217
  202.0 4.2 %all-to-all-start.5 = ((bf16[8,2,96,128]{3,2,1,0:T(8,128)(2,1)}), bf16[8,2,96,128]{3,2,1,0:T(8,128)(2,1)S(1)}, u32[]{:S(2)}, u32[]{:S(2)}) async-start(bf16[8,2,96,128]{3,2,1,0:T(8,128)(2,1)} %propagate.1), calls=%async_computation.5 | async-start | bytes 786432 | tf_op jit(solution)/shard_map/all_to_all | solution.py:21
  206.2 1.4 constant_dynamic-slice_fusion
  207.5 7.5 %all-to-all-done.5 = bf16[8,2,96,128]{3,2,1,0:T(8,128)(2,1)S(1)} async-done(((bf16[8,2,96,128]{3,2,1,0:T(8,128)(2,1)}), bf16[8,2,96,128]{3,2,1,0:T(8,128)(2,1)S(1)}, u32[]{:S(2)}, u32[]{:S(2)}) %all-to-all-start.5) | async-done | bytes 393248 | tf_op jit(solution)/shard_map/all_to_all | solution.py:21
  215.1 0.7 copy.42
  (36 shorter events, 0.3 us)
Async XLA Ops:
  0.6 30.0 %copy-start = (bf16[4,96,1024]{2,1,0:T(8,128)(2,1)S(1)}, bf16[4,96,1024]{2,1,0:T(8,128)(2,1)}, u32[]{:S(2)}) copy-start(bf16[4,96,1024]{2,1,0:T(8,128)(2,1)} %param.9) | copy-start | bytes 2359300
  3.7 25.6 %all-to-all-start = ((bf16[32,16,384]{2,1,0:T(8,128)(2,1)}), bf16[32,16,384]{2,1,0:T(8,128)(2,1)S(1)}, u32[]{:S(2)}, u32[]{:S(2)}) async-start(bf16[32,16,384]{2,1,0:T(8,128)(2,1)} %copy.23), calls=%async_computation | async-start | bytes 786432 | tf_op jit(solution)/shard_map/all_to_all | solution.py:21
  15.3 16.6 %copy-start.8 = (s32[16]{0:T(128)S(1)}, s32[16]{0:T(128)}, u32[]{:S(2)}) copy-start(s32[16]{0:T(128)} %param.11) | copy-start | bytes 196
  31.0 2.0 collective-permute-start.3
  34.3 17.2 %all-to-all-start.1 = ((bf16[16,16,1024]{2,1,0:T(8,128)(2,1)}), bf16[16,16,1024]{2,1,0:T(8,128)(2,1)S(1)}, u32[]{:S(2)}, u32[]{:S(2)}) async-start(bf16[16,16,1024]{2,1,0:T(8,128)(2,1)} %bitcast.9), calls=%async_computation.1 | async-start | bytes 1048576 | tf_op jit(solution)/shard_map/all_to_all | solution.py:21
  41.9 3.7 %collective-permute-start = (bf16[1,2,1152]{2,1,0:T(2,128)(2,1)S(1)}, bf16[1,2,1152]{2,1,0:T(2,128)(2,1)S(1)}, u32[]{:S(2)}, u32[]{:S(2)}) collective-permute-start(bf16[1,2,1152]{2,1,0:T(2,128)(2,1)S(1)} %maximum_bitcast_fusion), channel_id=1, source_target_pairs={{0,32},{32,0},{64,96},{96,64},{128,160},{160,128},{192,224},{224,1... | collective-permute-start | bytes 13832 | tf_op jit(solution)/shard_map/ppermute | solution.py:34
  45.6 10.1 %collective-permute-start.1 = (bf16[2,2,1152]{2,1,0:T(2,128)(2,1)S(1)}, bf16[2,2,1152]{2,1,0:T(2,128)(2,1)S(1)}, u32[]{:S(2)}, u32[]{:S(2)}) collective-permute-start(bf16[2,2,1152]{2,1,0:T(2,128)(2,1)S(1)} %pad_maximum_fusion.5), channel_id=1, source_target_pairs={{0,64},{32,96},{64,0},{96,32},{128,192},{160,224},{192,128},{224,1... | collective-permute-start | bytes 27656 | tf_op jit(solution)/shard_map/ppermute | solution.py:34
  52.3 18.0 %all-to-all-start.2 = ((bf16[8,16,1024]{2,1,0:T(8,128)(2,1)}), bf16[8,16,1024]{2,1,0:T(8,128)(2,1)S(1)}, u32[]{:S(2)}, u32[]{:S(2)}) async-start(bf16[8,16,1024]{2,1,0:T(8,128)(2,1)} %broadcast_in_dim.37), calls=%async_computation.2 | async-start | bytes 524288 | tf_op jit(solution)/shard_map/all_to_all | solution.py:21
  55.8 11.7 %collective-permute-start.2 = (bf16[4,2,1152]{2,1,0:T(2,128)(2,1)S(1)}, bf16[4,2,1152]{2,1,0:T(2,128)(2,1)S(1)}, u32[]{:S(2)}, u32[]{:S(2)}) collective-permute-start(bf16[4,2,1152]{2,1,0:T(2,128)(2,1)S(1)} %pad_maximum_fusion.4), channel_id=1, source_target_pairs={{0,128},{32,160},{64,192},{96,224},{128,0},{160,32},{192,64},{224,... | collective-permute-start | bytes 55304 | tf_op jit(solution)/shard_map/ppermute | solution.py:34
  70.4 0.6 copy-start.4
  85.1 5.2 %copy-start.1 = (bf16[16,16,1152]{2,1,0:T(8,128)(2,1)}, bf16[16,16,1152]{2,1,0:T(8,128)(2,1)S(1)}, u32[]{:S(2)}) copy-start(bf16[16,16,1152]{2,1,0:T(8,128)(2,1)S(1)} %all_to_all.30) | copy-start | bytes 1769476
  85.1 8.4 %collective-permute-start.4 = (bf16[256,1152]{1,0:T(8,128)(2,1)S(1)}, bf16[256,1152]{1,0:T(8,128)(2,1)S(1)}, u32[]{:S(2)}, u32[]{:S(2)}) collective-permute-start(bf16[256,1152]{1,0:T(8,128)(2,1)S(1)} %bitcast.58), channel_id=1, source_target_pairs={{0,1},{1,0},{2,3},{3,2},{4,5},{5,4},{6,7},{7,6},{8,9},{9,8},{10,11... | collective-permute-start | bytes 1769480 | tf_op jit(solution)/shard_map/ppermute | solution.py:289
  93.5 0.9 copy-start.3
  108.8 7.5 %copy-start.2 = (bf16[16,96,128]{2,1,0:T(8,128)(2,1)S(1)}, bf16[16,96,128]{2,1,0:T(8,128)(2,1)}, u32[]{:S(2)}) copy-start(bf16[16,96,128]{2,1,0:T(8,128)(2,1)} %param.6) | copy-start | bytes 1179652
  108.8 81.6 %all-to-all-start.4 = ((bf16[256,2,2304]{2,1,0:T(2,128)(2,1)}), bf16[256,2,2304]{2,1,0:T(2,128)(2,1)S(1)}, u32[]{:S(2)}, u32[]{:S(2)}) async-start(bf16[256,2,2304]{2,1,0:T(2,128)(2,1)} %reshape.70), calls=%async_computation.4 | async-start | bytes 4718592 | tf_op jit(solution)/shard_map/all_to_all | solution.py:21
  116.3 57.9 %collective-permute-start.5 = (bf16[16,96,128]{2,1,0:T(8,128)(2,1)S(1)}, bf16[16,96,128]{2,1,0:T(8,128)(2,1)}, u32[]{:S(2)}, u32[]{:S(2)}) collective-permute-start(bf16[16,96,128]{2,1,0:T(8,128)(2,1)S(1)} %copy-done.2), channel_id=1, source_target_pairs={{0,8},{8,16},{16,24},{24,32},{32,40},{40,48},{48,56},{56,64},{64,7... | collective-permute-start | bytes 1179656 | tf_op jit(solution)/shard_map/ppermute | solution.py:118
  119.8 57.5 %collective-permute-start.6 = (bf16[16,96,128]{2,1,0:T(8,128)(2,1)S(1)}, bf16[16,96,128]{2,1,0:T(8,128)(2,1)}, u32[]{:S(2)}, u32[]{:S(2)}) collective-permute-start(bf16[16,96,128]{2,1,0:T(8,128)(2,1)S(1)} %copy-done.2), channel_id=1, source_target_pairs={{8,0},{16,8},{24,16},{32,24},{40,32},{48,40},{56,48},{64,56},{72,6... | collective-permute-start | bytes 1179656 | tf_op jit(solution)/shard_map/ppermute | solution.py:119
  182.3 6.2 %collective-permute-start.10 = (bf16[2,96,128]{2,1,0:T(8,128)(2,1)S(1)}, bf16[2,96,128]{2,1,0:T(8,128)(2,1)S(1)}, u32[]{:S(2)}, u32[]{:S(2)}) collective-permute-start(bf16[2,96,128]{2,1,0:T(8,128)(2,1)S(1)} %get-tuple-element.7), channel_id=1, source_target_pairs={{0,4},{1,5},{2,6},{3,7},{4,0},{5,1},{6,2},{7,3},{8,12},{9,13},{10,... | collective-permute-start | bytes 147464 | tf_op jit(solution)/shard_map/ppermute | solution.py:110
  184.9 5.0 %collective-permute-start.11 = (bf16[2,96,128]{2,1,0:T(8,128)(2,1)S(1)}, bf16[2,96,128]{2,1,0:T(8,128)(2,1)S(1)}, u32[]{:S(2)}, u32[]{:S(2)}) collective-permute-start(bf16[2,96,128]{2,1,0:T(8,128)(2,1)S(1)} %get-tuple-element.6), channel_id=1, source_target_pairs={{0,5},{1,4},{2,7},{3,6},{4,1},{5,0},{6,3},{7,2},{8,13},{9,12},{10,... | collective-permute-start | bytes 147464 | tf_op jit(solution)/shard_map/ppermute | solution.py:110
  184.9 7.2 %collective-permute-start.12 = (bf16[2,96,128]{2,1,0:T(8,128)(2,1)S(1)}, bf16[2,96,128]{2,1,0:T(8,128)(2,1)S(1)}, u32[]{:S(2)}, u32[]{:S(2)}) collective-permute-start(bf16[2,96,128]{2,1,0:T(8,128)(2,1)S(1)} %get-tuple-element.5), channel_id=1, source_target_pairs={{0,6},{1,7},{2,4},{3,5},{4,2},{5,3},{6,0},{7,1},{8,14},{9,15},{10,... | collective-permute-start | bytes 147464 | tf_op jit(solution)/shard_map/ppermute | solution.py:110
  187.5 4.8 %collective-permute-start.13 = (bf16[2,96,128]{2,1,0:T(8,128)(2,1)S(1)}, bf16[2,96,128]{2,1,0:T(8,128)(2,1)}, u32[]{:S(2)}, u32[]{:S(2)}) collective-permute-start(bf16[2,96,128]{2,1,0:T(8,128)(2,1)S(1)} %get-tuple-element.4), channel_id=1, source_target_pairs={{0,7},{1,6},{2,5},{3,4},{4,3},{5,2},{6,1},{7,0},{8,15},{9,14},{10,... | collective-permute-start | bytes 147464 | tf_op jit(solution)/shard_map/ppermute | solution.py:110
  188.5 3.8 %collective-permute-start.7 = (bf16[2,96,128]{2,1,0:T(8,128)(2,1)S(1)}, bf16[2,96,128]{2,1,0:T(8,128)(2,1)}, u32[]{:S(2)}, u32[]{:S(2)}) collective-permute-start(bf16[2,96,128]{2,1,0:T(8,128)(2,1)S(1)} %get-tuple-element.10), channel_id=1, source_target_pairs={{0,1},{1,0},{2,3},{3,2},{4,5},{5,4},{6,7},{7,6},{8,9},{9,8},{10,11... | collective-permute-start | bytes 147464 | tf_op jit(solution)/shard_map/ppermute | solution.py:110
  188.5 3.5 %copy-start.5 = (bf16[2,96,128]{2,1,0:T(8,128)(2,1)}, bf16[2,96,128]{2,1,0:T(8,128)(2,1)S(1)}, u32[]{:S(2)}) copy-start(bf16[2,96,128]{2,1,0:T(8,128)(2,1)S(1)} %collective-permute-done.10.refs_4_) | copy-start | bytes 147460
  188.5 4.3 %collective-permute-start.8 = (bf16[2,96,128]{2,1,0:T(8,128)(2,1)S(1)}, bf16[2,96,128]{2,1,0:T(8,128)(2,1)}, u32[]{:S(2)}, u32[]{:S(2)}) collective-permute-start(bf16[2,96,128]{2,1,0:T(8,128)(2,1)S(1)} %get-tuple-element.9), channel_id=1, source_target_pairs={{0,2},{1,3},{2,0},{3,1},{4,6},{5,7},{6,4},{7,5},{8,10},{9,11},{10,... | collective-permute-start | bytes 147464 | tf_op jit(solution)/shard_map/ppermute | solution.py:110
  189.9 2.1 copy-start.6
  189.9 3.9 %collective-permute-start.9 = (bf16[2,96,128]{2,1,0:T(8,128)(2,1)S(1)}, bf16[2,96,128]{2,1,0:T(8,128)(2,1)}, u32[]{:S(2)}, u32[]{:S(2)}) collective-permute-start(bf16[2,96,128]{2,1,0:T(8,128)(2,1)S(1)} %get-tuple-element.8), channel_id=1, source_target_pairs={{0,3},{1,2},{2,1},{3,0},{4,7},{5,6},{6,5},{7,4},{8,11},{9,10},{10,... | collective-permute-start | bytes 147464 | tf_op jit(solution)/shard_map/ppermute | solution.py:110
  192.0 1.8 copy-start.7
  202.0 13.1 %all-to-all-start.5 = ((bf16[8,2,96,128]{3,2,1,0:T(8,128)(2,1)}), bf16[8,2,96,128]{3,2,1,0:T(8,128)(2,1)S(1)}, u32[]{:S(2)}, u32[]{:S(2)}) async-start(bf16[8,2,96,128]{3,2,1,0:T(8,128)(2,1)} %propagate.1), calls=%async_computation.5 | async-start | bytes 786432 | tf_op jit(solution)/shard_map/all_to_all | solution.py:21

commit v5 on v3

--- a/solution.py
+++ b/solution.py
@@ -10,10 +10,9 @@
 
 time_step = 0.01
 WIDE = ("z", "x")
-WIDE_X = ("x", "z")
 NARROW = ("y", "c")
-PLANE = ("x", "y", "c")
-MIXED = ("x", "y", "c", "z")
+PLANE = ("x", "y")
+MIXED = ("c", "x", "y", "z")
 ALL = WIDE + NARROW
 LANES = 128
 
@@ -22,25 +21,54 @@
     return lax.all_to_all(blocks, axes, split_axis=0, concat_axis=0, tiled=True)
 
 
-def ordered_kernel(at_ref, *refs):
-    *piece_refs, out_ref = refs
-    for k, piece_ref in enumerate(piece_refs):
-        out_ref[at_ref[0] ^ k] = piece_ref[...]
-
-
-def gathered(array, axis):
-    count = lax.axis_size(axis)
-    pieces = [array]
-    for k in range(1, count):
-        pieces.append(lax.ppermute(array, axis, [(i, i ^ k) for i in range(count)]))
-    in_vmem = pl.BlockSpec(memory_space=pltpu.VMEM)
-    return pl.pallas_call(
-        ordered_kernel,
-        in_specs=[pl.BlockSpec(memory_space=pltpu.SMEM)] + [in_vmem] * count,
-        out_specs=in_vmem,
-        out_shape=jax.ShapeDtypeStruct((count,) + array.shape, array.dtype),
-        name="ordered",
-    )(lax.axis_index(axis).astype(jnp.int32).reshape(1), *pieces)
+def fields_kernel(at_ref, own_hbm, other_hbm, out_ref, own_ref, other_ref, sems):
+    f32, bf16, i32 = jnp.float32, jnp.bfloat16, jnp.int32
+    vectors = out_ref.shape[2]
+    rows = own_ref.shape[0]
+    core_at = at_ref[0]
+    own_copy = pltpu.make_async_copy(own_hbm, own_ref, sems.at[0])
+    other_copy = pltpu.make_async_copy(other_hbm, other_ref, sems.at[1])
+    own_copy.start()
+    other_copy.start()
+    own_copy.wait()
+    other_copy.wait()
+    slot = lax.broadcasted_iota(i32, (rows, LANES), 0)
+    lane = lax.broadcasted_iota(i32, (rows, LANES), 1)
+    base = (((slot >> 1) & 7) * 4 + (slot >> 6) - 1) * 16
+    tables = (own_ref, other_ref)
+    for k, table in enumerate(tables):
+        source = table[:, vectors:].astype(f32).astype(i32) + base
+        block, inner = source >> 4, source & 15
+        row = (((inner >> 1) & 1) ^ core_at) * rows + (block & 3) * 64
+        row = row + (inner >> 2) * 16 + (block >> 2) * 2 + (inner & 1)
+        fields = jnp.zeros((rows, vectors), f32)
+        for half, picked in enumerate(tables):
+            hits = [
+                (row == lane + (half * rows + at)).astype(f32).astype(bf16)
+                for at in range(0, rows, LANES)
+            ]
+            pick = jnp.concatenate(hits, axis=1)
+            fields = fields + jnp.dot(pick, picked[:, :vectors], preferred_element_type=f32)
+        out_ref[k ^ core_at] = fields.astype(bf16)
+
+
+def picked_fields(core_at, own, other):
+    rows, width = own.shape
+    vectors = width - LANES
+    anywhere = pl.BlockSpec(memory_space=pl.ANY)
+    fields = pl.pallas_call(
+        fields_kernel,
+        in_specs=[pl.BlockSpec(memory_space=pltpu.SMEM), anywhere, anywhere],
+        out_specs=pl.BlockSpec(memory_space=pltpu.VMEM),
+        out_shape=jax.ShapeDtypeStruct((2, rows, vectors), own.dtype),
+        scratch_shapes=[
+            pltpu.VMEM(own.shape, own.dtype),
+            pltpu.VMEM(own.shape, own.dtype),
+            pltpu.SemaphoreType.DMA((2,)),
+        ],
+        name="fields",
+    )(core_at.astype(jnp.int32).reshape(1), own, other)
+    return fields.reshape(2 * rows, vectors)
 
 
 def dealt(blocks, axes):
@@ -64,13 +92,34 @@
     return jnp.take(padded, offset, axis=0)
 
 
+def pack_kernel(chol_ref, out_ref, wide_ref):
+    row_count, col_count, width = chol_ref.shape
+    f32, bf16 = jnp.float32, jnp.bfloat16
+    full = out_ref.shape[0]
+    for at in range(0, width, LANES):
+        wide_ref[...] = chol_ref[:, :, at : at + LANES].astype(f32).reshape(row_count * col_count, LANES)
+        for j in range(full):
+            out_ref[j, :row_count, at : at + LANES] = wide_ref[pl.ds(j, row_count, stride=col_count), :].astype(bf16)
+        for j in range(full, col_count):
+            column = wide_ref[pl.ds(j, row_count, stride=col_count), :].astype(bf16)
+            for p in range(3):
+                out_ref[3 * (j - full) + p, row_count:, at : at + LANES] = column[p * 32 : (p + 1) * 32]
+
+
 def packed_cholesky(cholesky):
     row_count, col_count, vectors = cholesky.shape
-    by_col = cholesky.transpose(1, 0, 2)
     full = col_count * row_count // LANES
-    rest = LANES - row_count
-    tail = by_col[full:].reshape(full, rest, vectors)
-    return jnp.concatenate([by_col[:full], tail], axis=1).reshape(full * LANES, vectors)
+    width = 256
+    packed = pl.pallas_call(
+        pack_kernel,
+        grid=(vectors // width,),
+        in_specs=[pl.BlockSpec((row_count, col_count, width), lambda i: (0, 0, i))],
+        out_specs=pl.BlockSpec((full, LANES, width), lambda i: (0, 0, i)),
+        out_shape=jax.ShapeDtypeStruct((full, LANES, vectors), cholesky.dtype),
+        scratch_shapes=[pltpu.VMEM((row_count * col_count, LANES), jnp.float32)],
+        name="pack",
+    )(cholesky)
+    return packed.reshape(full * LANES, vectors)
 
 
 def propagate_kernel(at_ref, blocks_ref, *refs):
@@ -82,8 +131,9 @@
     def assemble(s, carry):
         def rows_of(t, n):
             at = t * 128
+            first = (n & 1) * 128 + (n >> 1) * 8
             pieces = [
-                blocks_ref[s, x * 64 + n * 8 : x * 64 + n * 8 + 8, at : at + 128]
+                blocks_ref[s, first + x * 32 : first + x * 32 + 8, at : at + 128]
                 for x in range(4)
             ]
             return jnp.concatenate([piece.astype(f32) for piece in pieces], axis=0)
@@ -176,14 +226,16 @@
     z_count, x_count = lax.axis_size("z"), lax.axis_size("x")
     wide_count = z_count * x_count
     narrow_count = lax.axis_size(NARROW)
-    plane_count = x_count * narrow_count
+    plane_count = lax.axis_size(PLANE)
+    core_at = lax.axis_index("c")
+    swap = [(0, 1), (1, 0)]
     share = walk_local // narrow_count
     rows_here = z_count * share
     z_at = lax.axis_index("z")
     wide_at = lax.axis_index(WIDE)
     narrow_at = lax.axis_index(NARROW)
     root_step = math.sqrt(time_step)
-    f32, bf16, i32 = jnp.float32, jnp.bfloat16, jnp.int32
+    f32, bf16 = jnp.float32, jnp.bfloat16
 
     packed = packed_cholesky(cholesky)
 
@@ -194,47 +246,46 @@
     current = dealt(chosen, NARROW)
 
     own_noise = lax.dynamic_slice_in_dim(noise, narrow_at * share, share, 0)
+    own_noise = own_noise.reshape(rows_here, LANES)
     own_offset = lax.dynamic_slice_in_dim(offset, narrow_at * share, share, 0).astype(bf16)
-    own_offset = jnp.broadcast_to(own_offset[:, None], (share, LANES))
-    side = jnp.concatenate([own_noise, own_offset], axis=1)
-    side = gathered(side, "z").reshape(rows_here, vectors + LANES)
+    own_offset = jnp.broadcast_to(own_offset[:, None, None], (share, z_count, LANES))
+    side = jnp.concatenate([own_noise, own_offset.reshape(rows_here, LANES)], axis=1)
 
     rotated = jnp.einsum(
         "wiq,wqp->wpi", walkers, intersection_inverse, preferred_element_type=f32
     ).astype(bf16)
-    rotated = rotated.reshape(walk_local, z_count, x_count, -1).transpose(2, 1, 0, 3)
-    pairs = exchange(rotated.reshape(wide_count, walk_local, -1), WIDE_X)
-
-    pairs = pairs.reshape(x_count, z_count, narrow_count, share, -1).transpose(0, 2, 1, 3, 4)
-    pairs = pairs.reshape(wide_count * walk_local, -1)
-    partial = jnp.dot(pairs, half_cholesky.reshape(-1, vectors), preferred_element_type=f32)
+    rotated = rotated.reshape(walk_local, wide_count, -1).transpose(1, 0, 2)
+    pairs = exchange(rotated, WIDE)
+
+    y_count, core_count = lax.axis_size("y"), lax.axis_size("c")
+    pairs = pairs.reshape(z_count, x_count, y_count, core_count, share, -1)
+    pairs = pairs.transpose(3, 1, 2, 0, 4, 5).reshape(core_count, plane_count * rows_here, -1)
+    half_flat = half_cholesky.reshape(-1, vectors)
+    mine = lax.dynamic_index_in_dim(pairs, core_at, 0, keepdims=False)
+    theirs = lax.dynamic_index_in_dim(pairs, 1 - core_at, 0, keepdims=False)
+    sent = jnp.dot(theirs, half_flat, preferred_element_type=f32).astype(bf16)
+    received = lax.ppermute(sent, "c", swap)
+    partial = jnp.dot(mine, half_flat, preferred_element_type=f32) + received.astype(f32)
     partial = partial.astype(bf16).reshape(plane_count, rows_here, vectors)
     partial = exchange(partial, PLANE)
 
     partial = jnp.sum(partial.astype(f32), axis=0).astype(bf16)
+    partial = jnp.concatenate([partial, side], axis=1)
     partial = exchange(jnp.broadcast_to(partial[None], (z_count,) + partial.shape), ("z",))
-    bias = jnp.sum(partial.astype(f32), axis=0)
+    bias = jnp.sum(partial[:, :, :vectors].astype(f32), axis=0)
     force_bias = lax.dynamic_slice_in_dim(bias, z_at * share, share, 0)
 
-    aux = root_step * side[:, :vectors].astype(f32) + time_step * bias
-    aux = jnp.concatenate([aux.astype(bf16), side[:, vectors:]], axis=1)
+    noises = partial[:, :, vectors : vectors + LANES].reshape(rows_here, vectors)
+    offsets = partial[:, ::z_count, vectors + LANES :].reshape(rows_here, LANES)
+    aux = root_step * noises.astype(f32) + time_step * bias
+    aux = jnp.concatenate([aux.astype(bf16), offsets], axis=1)
     aux = exchange(jnp.broadcast_to(aux[None], (plane_count,) + aux.shape), PLANE)
     aux = aux.reshape(plane_count * rows_here, vectors + LANES)
-    slot = jnp.arange(plane_count * rows_here, dtype=i32)
-    slot_x = slot // (narrow_count * rows_here)
-    slot_z = (slot // share) % z_count
-    source = aux[:, vectors].astype(i32) + (slot_z * x_count + slot_x - 1) * walk_local
-    block, inner = source // walk_local, source % walk_local
-    row = (block % x_count) * narrow_count + inner // share
-    row = row * rows_here + (block // x_count) * share + inner % share
-    pick = (row[:, None] == slot[None]).astype(bf16)
-    fields = jnp.dot(pick, aux[:, :vectors], preferred_element_type=f32).astype(bf16)
-
+    other = lax.ppermute(aux, "c", swap)
+
+    fields = picked_fields(core_at, aux, other)
     operator = lax.dot_general(
-        fields,
-        packed,
-        (((1,), (1,)), ((), ())),
-        preferred_element_type=f32,
+        fields, packed, (((1,), (1,)), ((), ())), preferred_element_type=f32
     ).astype(bf16)
     operator = exchange(operator.reshape(wide_count * narrow_count, share, -1), MIXED)
 

time: 223 us -> 208 us (0.933)
  the two profiles are of different devices: /device:TPU:96 before, /device:TPU:6 now
where the time goes in v5:
time: 208 us; the launch traced here: 207 us
  waiting for transfers between devices  90.8 us (44%)
  starting transfers between devices  43.9 us (21%)
  blocking collectives  28.8 us (14%)
  Pallas kernels  17.7 us (9%)
  local copies, waits for them, and re-layouts  14.1 us (7%)
  matrix products  8.51 us (4%)
  other arithmetic  2.63 us (1%)
    ppermute x1, waiting for transfers between devices, slot_walkers(): before = lax.ppermute(walkers, WIDE, up)  51.9 us
    all_to_all x4, waiting for transfers between devices, exchange(): return lax.all_to_all(blocks, axes, split_axis=0, concat_axis=0, tiled=True)  30.2 us
    all_to_all x4, starting transfers between devices, exchange(): return lax.all_to_all(blocks, axes, split_axis=0, concat_axis=0, tiled=True)  29.8 us
    all_to_all x2, blocking collectives, exchange(): return lax.all_to_all(blocks, axes, split_axis=0, concat_axis=0, tiled=True)  28.8 us
    pallas_call x1, Pallas kernels, propagate(): pl.pallas_call(propagate_kernel, in_specs=[pl.BlockSpec(memory_space=pltp...  8.15 us
    ppermute x7, starting transfers between devices, dealt(): piece = lax.ppermute(piece, axes, [(i, i ^ k) for i in range(count)])  8.12 us
    pallas_call x1, Pallas kernels, packed_cholesky(): pl.pallas_call(pack_kernel, grid=(vectors // width,), in_specs=[pl.BlockS...  6.48 us
    dot_general x1, matrix products, per_device(): lax.dot_general(fields, packed, (((1,), (1,)), ((), ())), preferred_eleme...  5.31 us
  transfers between devices with their start and end apart: 15, of which 10 were waited for; matrix products, arithmetic and copies ran while one was open for 4% of the time, Pallas kernels for 3%

profile of v5, /device:TPU:6, one launch (start us, length us, event | category | flops | bytes accessed | tf_op | source)
XLA Modules:
  0.0 207.4 jit_solution(18011578161999061821)
XLA Ops:
  0.6 0.0 copy-start
  0.6 1.5 convolution_convert_fusion.2
  2.2 0.3 copy.14
  2.5 0.4 reshape.66
  2.8 0.9 copy.15
  3.7 11.6 %all-to-all-start = ((bf16[32,16,384]{2,1,0:T(8,128)(2,1)}), bf16[32,16,384]{2,1,0:T(8,128)(2,1)S(1)}, u32[]{:S(2)}, u32[]{:S(2)}) async-start(bf16[32,16,384]{2,1,0:T(8,128)(2,1)} %copy.15), calls=%async_computation | async-start | bytes 786432 | tf_op jit(solution)/shard_map/all_to_all | solution.py:21
  15.3 14.0 %all-to-all-done = bf16[32,16,384]{2,1,0:T(8,128)(2,1)S(1)} async-done(((bf16[32,16,384]{2,1,0:T(8,128)(2,1)}), bf16[32,16,384]{2,1,0:T(8,128)(2,1)S(1)}, u32[]{:S(2)}, u32[]{:S(2)}) %all-to-all-start) | async-done | bytes 393248 | tf_op jit(solution)/shard_map/all_to_all | solution.py:21
  29.3 0.1 reshape.67
  29.4 0.3 copy.16
  29.8 0.8 constant_dynamic-slice_fusion.3
  30.6 0.0 copy-start.8
  30.6 0.4 convolution_convert_fusion.1
  31.1 0.1 collective-permute-start
  31.2 1.9 collective-permute-done
  33.1 1.2 add_convert_fusion
  34.3 7.4 %all-to-all-start.1 = ((bf16[16,16,1024]{2,1,0:T(8,128)(2,1)}), bf16[16,16,1024]{2,1,0:T(8,128)(2,1)S(1)}, u32[]{:S(2)}, u32[]{:S(2)}) async-start(bf16[16,16,1024]{2,1,0:T(8,128)(2,1)} %bitcast.7), calls=%async_computation.1 | async-start | bytes 1048576 | tf_op jit(solution)/shard_map/all_to_all | solution.py:21
  41.8 0.1 dynamic-slice_convert_fusion
  41.8 0.1 broadcast_in_dim.36
  41.9 0.1 broadcast_in_dim.37
  42.0 0.7 constant_dynamic-slice_fusion.1
  42.7 8.7 %all-to-all-done.1 = bf16[16,16,1024]{2,1,0:T(8,128)(2,1)S(1)} async-done(((bf16[16,16,1024]{2,1,0:T(8,128)(2,1)}), bf16[16,16,1024]{2,1,0:T(8,128)(2,1)S(1)}, u32[]{:S(2)}, u32[]{:S(2)}) %all-to-all-start.1) | async-done | bytes 524320 | tf_op jit(solution)/shard_map/all_to_all | solution.py:21
  51.5 0.1 reduce_sum.21
  51.6 0.1 broadcast_in_dim.38
  51.7 14.8 %all_to_all.30 = bf16[8,16,1280]{2,1,0:T(8,128)(2,1)S(1)} all-to-all(bf16[8,16,1280]{2,1,0:T(8,128)(2,1)S(1)} %broadcast_in_dim.39), channel_id=1, replica_groups=mesh['z'=8,'x'=4,'y'=4,'c'=2] {'z'}, dimensions={0} | all-to-all | bytes 655360 | tf_op jit(solution)/shard_map/all_to_all | solution.py:21
  66.6 0.6 copy-done.4
  67.3 14.0 %all_to_all.31 = bf16[16,16,1152]{2,1,0:T(8,128)(2,1)S(1)} all-to-all(bf16[16,16,1152]{2,1,0:T(8,128)(2,1)S(1)} %broadcast_in_dim.40), channel_id=1, replica_groups=mesh['z'=8,'x'=4,'y'=4,'c'=2] {'x','y'}, dimensions={0} | all-to-all | bytes 1179648 | tf_op jit(solution)/shard_map/all_to_all | solution.py:21
  81.3 0.0 collective-permute-start.1
  81.3 6.5 %pack.1 = bf16[18,128,1024]{2,1,0:T(8,128)(2,1)} custom-call(bf16[96,24,1024]{2,1,0:T(8,128)(2,1)} %chol_ref.1), custom_call_target="tpu_custom_call" | custom-call | tf_op jit(solution)/shard_map/pack/pallas_call | solution.py:113
  87.8 0.0 collective-permute-done.1.other_hbm
  87.8 0.8 copy-done.3
  88.7 3.0 %fields.1 = bf16[2,256,1024]{2,1,0:T(8,128)(2,1)} custom-call(s32[1]{0:T(128)} %bitcast.1.at_ref, bf16[256,1152]{1,0:T(8,128)(2,1)} %bitcast.53, bf16[256,1152]{1,0:T(8,128)(2,1)} %copy-done.3), custom_call_target="tpu_custom_call" | custom-call | tf_op jit(solution)/shard_map/fields/pallas_call | solution.py:59
  91.7 5.3 %convolution_convert_fusion = bf16[512,2304]{1,0:T(8,128)(2,1)S(1)} fusion(bf16[512,1024]{1,0:T(8,128)(2,1)} %bitcast.57, bf16[2304,1024]{1,0:T(8,128)(2,1)} %bitcast.50), kind=kOutput, calls=%fused_computation.1 | convolution fusion | flops 2417098752 | bytes 8126464 | tf_op jit(solution)/shard_map/dot_general | solution.py:287
  97.0 2.4 %reshape.76 = bf16[256,2,2304]{2,1,0:T(2,128)(2,1)} reshape(bf16[512,2304]{1,0:T(8,128)(2,1)S(1)} %convolution_convert_fusion) | data formatting | bytes 4718592 | tf_op jit(solution)/shard_map/reshape | solution.py:290
  99.4 7.3 %all-to-all-start.4 = ((bf16[256,2,2304]{2,1,0:T(2,128)(2,1)}), bf16[256,2,2304]{2,1,0:T(2,128)(2,1)S(1)}, u32[]{:S(2)}, u32[]{:S(2)}) async-start(bf16[256,2,2304]{2,1,0:T(2,128)(2,1)} %reshape.76), calls=%async_computation.4 | async-start | bytes 4718592 | tf_op jit(solution)/shard_map/all_to_all | solution.py:21
  106.8 3.6 %collective-permute-start.2 = (bf16[16,96,128]{2,1,0:T(8,128)(2,1)S(1)}, bf16[16,96,128]{2,1,0:T(8,128)(2,1)}, u32[]{:S(2)}, u32[]{:S(2)}) collective-permute-start(bf16[16,96,128]{2,1,0:T(8,128)(2,1)S(1)} %copy-done.2), channel_id=1, source_target_pairs={{0,8},{8,16},{16,24},{24,32},{32,40},{40,48},{48,56},{56,64},{64,7... | collective-permute-start | bytes 1179656 | tf_op jit(solution)/shard_map/ppermute | solution.py:89
  110.4 2.3 %collective-permute-start.3 = (bf16[16,96,128]{2,1,0:T(8,128)(2,1)S(1)}, bf16[16,96,128]{2,1,0:T(8,128)(2,1)}, u32[]{:S(2)}, u32[]{:S(2)}) collective-permute-start(bf16[16,96,128]{2,1,0:T(8,128)(2,1)S(1)} %copy-done.2), channel_id=1, source_target_pairs={{8,0},{16,8},{24,16},{32,24},{40,32},{48,40},{56,48},{64,56},{72,6... | collective-permute-start | bytes 1179656 | tf_op jit(solution)/shard_map/ppermute | solution.py:90
  112.7 0.1 broadcast_in_dim.41
  112.8 51.9 %collective-permute-done.2 = bf16[16,96,128]{2,1,0:T(8,128)(2,1)} collective-permute-done((bf16[16,96,128]{2,1,0:T(8,128)(2,1)S(1)}, bf16[16,96,128]{2,1,0:T(8,128)(2,1)}, u32[]{:S(2)}, u32[]{:S(2)}) %collective-permute-start.2) | collective-permute-done | bytes 393248 | tf_op jit(solution)/shard_map/ppermute | solution.py:89
  164.6 3.2 %collective-permute-done.3 = bf16[16,96,128]{2,1,0:T(8,128)(2,1)} collective-permute-done((bf16[16,96,128]{2,1,0:T(8,128)(2,1)S(1)}, bf16[16,96,128]{2,1,0:T(8,128)(2,1)}, u32[]{:S(2)}, u32[]{:S(2)}) %collective-permute-start.3) | collective-permute-done | bytes 393248 | tf_op jit(solution)/shard_map/ppermute | solution.py:90
  167.9 2.3 %pad_maximum_fusion = bf16[48,96,128]{2,1,0:T(8,128)(2,1)} fusion(bf16[16,96,128]{2,1,0:T(8,128)(2,1)} %collective-permute-done.3, bf16[16,96,128]{2,1,0:T(8,128)(2,1)S(1)} %copy-done.2, bf16[16,96,128]{2,1,0:T(8,128)(2,1)} %collective-permute-done.2), kind=kLoop, calls=%fused_computation.5 | loop fusion | flops 1179648 | bytes 2359296 | tf_op jit(solution)/shard_map/concatenate | solution.py:91
  170.1 1.9 gather_fusion
  172.0 0.1 broadcast_select_fusion
  172.2 0.7 dynamic-slice_bitcast_fusion
  172.8 2.0 collective-permute-start.10
  174.8 1.0 collective-permute-start.4
  175.8 0.0 collective-permute-start.5
  175.8 1.4 collective-permute-start.6
  177.1 0.5 collective-permute-start.7
  177.6 0.2 collective-permute-done.10.refs_7_
  177.9 2.9 %collective-permute-start.8 = (bf16[2,96,128]{2,1,0:T(8,128)(2,1)S(1)}, bf16[2,96,128]{2,1,0:T(8,128)(2,1)}, u32[]{:S(2)}, u32[]{:S(2)}) collective-permute-start(bf16[2,96,128]{2,1,0:T(8,128)(2,1)S(1)} %get-tuple-element.6), channel_id=1, source_target_pairs={{0,5},{1,4},{2,7},{3,6},{4,1},{5,0},{6,3},{7,2},{8,13},{9,12},{10,... | collective-permute-start | bytes 147464 | tf_op jit(solution)/shard_map/ppermute | solution.py:81
  180.8 0.0 collective-permute-done.4.refs_1_
  180.8 0.4 collective-permute-start.9
  181.2 0.0 all-to-all-done.4
  181.2 1.7 copy.29
  182.8 0.0 collective-permute-done.5.refs_2_
  182.9 0.0 collective-permute-done.6.refs_3_
  182.9 0.5 collective-permute-done.7.refs_4_
  183.4 0.7 collective-permute-done.8.refs_5_
  184.1 2.1 %collective-permute-done.9.refs_6_ = bf16[2,96,128]{2,1,0:T(8,128)(2,1)} collective-permute-done((bf16[2,96,128]{2,1,0:T(8,128)(2,1)S(1)}, bf16[2,96,128]{2,1,0:T(8,128)(2,1)}, u32[]{:S(2)}, u32[]{:S(2)}) %collective-permute-start.9) | collective-permute-done | bytes 49184 | tf_op jit(solution)/shard_map/ppermute | solution.py:81
  186.2 8.2 %propagate.1 = bf16[8,2,96,128]{3,2,1,0:T(8,128)(2,1)} custom-call(s32[1]{0:T(128)} %bitcast.at_ref, bf16[2,256,2304]{2,1,0:T(8,128)(2,1)} %bitcast.49, bf16[2,96,128]{2,1,0:T(8,128)(2,1)} %get-tuple-element.11.refs_0_, bf16[2,96,128]{2,1,0:T(8,128)(2,1)} %copy-done.6, bf16[2,96,128]{2,1,0:T(8,128)(2,1)} %copy-done.7, ...), custom_call_target="tpu_custom_call" | custom-call | tf_op jit(solution)/shard_map/propagate/pallas_call | solution.py:209
  194.4 3.5 %all-to-all-start.5 = ((bf16[8,2,96,128]{3,2,1,0:T(8,128)(2,1)}), bf16[8,2,96,128]{3,2,1,0:T(8,128)(2,1)S(1)}, u32[]{:S(2)}, u32[]{:S(2)}) async-start(bf16[8,2,96,128]{3,2,1,0:T(8,128)(2,1)} %propagate.1), calls=%async_computation.5 | async-start | bytes 786432 | tf_op jit(solution)/shard_map/all_to_all | solution.py:21
  197.8 1.4 constant_dynamic-slice_fusion
  199.2 7.5 %all-to-all-done.5 = bf16[8,2,96,128]{3,2,1,0:T(8,128)(2,1)S(1)} async-done(((bf16[8,2,96,128]{3,2,1,0:T(8,128)(2,1)}), bf16[8,2,96,128]{3,2,1,0:T(8,128)(2,1)S(1)}, u32[]{:S(2)}, u32[]{:S(2)}) %all-to-all-start.5) | async-done | bytes 393248 | tf_op jit(solution)/shard_map/all_to_all | solution.py:21
  206.7 0.7 copy.31
  (27 shorter events, 0.3 us)
Async XLA Ops:
  0.6 30.0 %copy-start = (bf16[4,96,1024]{2,1,0:T(8,128)(2,1)S(1)}, bf16[4,96,1024]{2,1,0:T(8,128)(2,1)}, u32[]{:S(2)}) copy-start(bf16[4,96,1024]{2,1,0:T(8,128)(2,1)} %param.9) | copy-start | bytes 2359300
  3.7 25.6 %all-to-all-start = ((bf16[32,16,384]{2,1,0:T(8,128)(2,1)}), bf16[32,16,384]{2,1,0:T(8,128)(2,1)S(1)}, u32[]{:S(2)}, u32[]{:S(2)}) async-start(bf16[32,16,384]{2,1,0:T(8,128)(2,1)} %copy.15), calls=%async_computation | async-start | bytes 786432 | tf_op jit(solution)/shard_map/all_to_all | solution.py:21
  30.6 11.2 %copy-start.8 = (s32[16]{0:T(128)S(1)}, s32[16]{0:T(128)}, u32[]{:S(2)}) copy-start(s32[16]{0:T(128)} %param.11) | copy-start | bytes 196
  31.1 2.0 collective-permute-start
  34.3 17.2 %all-to-all-start.1 = ((bf16[16,16,1024]{2,1,0:T(8,128)(2,1)}), bf16[16,16,1024]{2,1,0:T(8,128)(2,1)S(1)}, u32[]{:S(2)}, u32[]{:S(2)}) async-start(bf16[16,16,1024]{2,1,0:T(8,128)(2,1)} %bitcast.7), calls=%async_computation.1 | async-start | bytes 1048576 | tf_op jit(solution)/shard_map/all_to_all | solution.py:21
  66.6 0.6 copy-start.4
  81.3 6.5 %copy-start.1 = (bf16[16,16,1152]{2,1,0:T(8,128)(2,1)}, bf16[16,16,1152]{2,1,0:T(8,128)(2,1)S(1)}, u32[]{:S(2)}) copy-start(bf16[16,16,1152]{2,1,0:T(8,128)(2,1)S(1)} %all_to_all.31) | copy-start | bytes 1769476
  81.3 6.5 %collective-permute-start.1 = (bf16[256,1152]{1,0:T(8,128)(2,1)S(1)}, bf16[256,1152]{1,0:T(8,128)(2,1)S(1)}, u32[]{:S(2)}, u32[]{:S(2)}) collective-permute-start(bf16[256,1152]{1,0:T(8,128)(2,1)S(1)} %bitcast.52), channel_id=1, source_target_pairs={{0,1},{1,0},{2,3},{3,2},{4,5},{5,4},{6,7},{7,6},{8,9},{9,8},{10,11... | collective-permute-start | bytes 1769480 | tf_op jit(solution)/shard_map/ppermute | solution.py:284
  87.8 0.8 copy-start.3
  99.4 7.3 %copy-start.2 = (bf16[16,96,128]{2,1,0:T(8,128)(2,1)S(1)}, bf16[16,96,128]{2,1,0:T(8,128)(2,1)}, u32[]{:S(2)}) copy-start(bf16[16,96,128]{2,1,0:T(8,128)(2,1)} %param.6) | copy-start | bytes 1179652
  99.4 81.8 %all-to-all-start.4 = ((bf16[256,2,2304]{2,1,0:T(2,128)(2,1)}), bf16[256,2,2304]{2,1,0:T(2,128)(2,1)S(1)}, u32[]{:S(2)}, u32[]{:S(2)}) async-start(bf16[256,2,2304]{2,1,0:T(2,128)(2,1)} %reshape.76), calls=%async_computation.4 | async-start | bytes 4718592 | tf_op jit(solution)/shard_map/all_to_all | solution.py:21
  106.8 57.9 %collective-permute-start.2 = (bf16[16,96,128]{2,1,0:T(8,128)(2,1)S(1)}, bf16[16,96,128]{2,1,0:T(8,128)(2,1)}, u32[]{:S(2)}, u32[]{:S(2)}) collective-permute-start(bf16[16,96,128]{2,1,0:T(8,128)(2,1)S(1)} %copy-done.2), channel_id=1, source_target_pairs={{0,8},{8,16},{16,24},{24,32},{32,40},{40,48},{48,56},{56,64},{64,7... | collective-permute-start | bytes 1179656 | tf_op jit(solution)/shard_map/ppermute | solution.py:89
  110.4 57.5 %collective-permute-start.3 = (bf16[16,96,128]{2,1,0:T(8,128)(2,1)S(1)}, bf16[16,96,128]{2,1,0:T(8,128)(2,1)}, u32[]{:S(2)}, u32[]{:S(2)}) collective-permute-start(bf16[16,96,128]{2,1,0:T(8,128)(2,1)S(1)} %copy-done.2), channel_id=1, source_target_pairs={{8,0},{16,8},{24,16},{32,24},{40,32},{48,40},{56,48},{64,56},{72,6... | collective-permute-start | bytes 1179656 | tf_op jit(solution)/shard_map/ppermute | solution.py:90
  172.8 5.0 %collective-permute-start.10 = (bf16[2,96,128]{2,1,0:T(8,128)(2,1)S(1)}, bf16[2,96,128]{2,1,0:T(8,128)(2,1)S(1)}, u32[]{:S(2)}, u32[]{:S(2)}) collective-permute-start(bf16[2,96,128]{2,1,0:T(8,128)(2,1)S(1)} %get-tuple-element.4), channel_id=1, source_target_pairs={{0,7},{1,6},{2,5},{3,4},{4,3},{5,2},{6,1},{7,0},{8,15},{9,14},{10,... | collective-permute-start | bytes 147464 | tf_op jit(solution)/shard_map/ppermute | solution.py:81
  174.8 6.0 %collective-permute-start.4 = (bf16[2,96,128]{2,1,0:T(8,128)(2,1)S(1)}, bf16[2,96,128]{2,1,0:T(8,128)(2,1)S(1)}, u32[]{:S(2)}, u32[]{:S(2)}) collective-permute-start(bf16[2,96,128]{2,1,0:T(8,128)(2,1)S(1)} %get-tuple-element.10), channel_id=1, source_target_pairs={{0,1},{1,0},{2,3},{3,2},{4,5},{5,4},{6,7},{7,6},{8,9},{9,8},{10,11... | collective-permute-start | bytes 147464 | tf_op jit(solution)/shard_map/ppermute | solution.py:81
  175.8 7.1 %collective-permute-start.5 = (bf16[2,96,128]{2,1,0:T(8,128)(2,1)S(1)}, bf16[2,96,128]{2,1,0:T(8,128)(2,1)S(1)}, u32[]{:S(2)}, u32[]{:S(2)}) collective-permute-start(bf16[2,96,128]{2,1,0:T(8,128)(2,1)S(1)} %get-tuple-element.9), channel_id=1, source_target_pairs={{0,2},{1,3},{2,0},{3,1},{4,6},{5,7},{6,4},{7,5},{8,10},{9,11},{10,... | collective-permute-start | bytes 147464 | tf_op jit(solution)/shard_map/ppermute | solution.py:81
  175.8 7.1 %collective-permute-start.6 = (bf16[2,96,128]{2,1,0:T(8,128)(2,1)S(1)}, bf16[2,96,128]{2,1,0:T(8,128)(2,1)}, u32[]{:S(2)}, u32[]{:S(2)}) collective-permute-start(bf16[2,96,128]{2,1,0:T(8,128)(2,1)S(1)} %get-tuple-element.8), channel_id=1, source_target_pairs={{0,3},{1,2},{2,1},{3,0},{4,7},{5,6},{6,5},{7,4},{8,11},{9,10},{10,... | collective-permute-start | bytes 147464 | tf_op jit(solution)/shard_map/ppermute | solution.py:81
  177.1 6.2 %collective-permute-start.7 = (bf16[2,96,128]{2,1,0:T(8,128)(2,1)S(1)}, bf16[2,96,128]{2,1,0:T(8,128)(2,1)}, u32[]{:S(2)}, u32[]{:S(2)}) collective-permute-start(bf16[2,96,128]{2,1,0:T(8,128)(2,1)S(1)} %get-tuple-element.7), channel_id=1, source_target_pairs={{0,4},{1,5},{2,6},{3,7},{4,0},{5,1},{6,2},{7,3},{8,12},{9,13},{10,... | collective-permute-start | bytes 147464 | tf_op jit(solution)/shard_map/ppermute | solution.py:81
  177.9 5.0 %copy-start.5 = (bf16[2,96,128]{2,1,0:T(8,128)(2,1)}, bf16[2,96,128]{2,1,0:T(8,128)(2,1)S(1)}, u32[]{:S(2)}) copy-start(bf16[2,96,128]{2,1,0:T(8,128)(2,1)S(1)} %collective-permute-done.10.refs_7_) | copy-start | bytes 147460
  177.9 6.2 %collective-permute-start.8 = (bf16[2,96,128]{2,1,0:T(8,128)(2,1)S(1)}, bf16[2,96,128]{2,1,0:T(8,128)(2,1)}, u32[]{:S(2)}, u32[]{:S(2)}) collective-permute-start(bf16[2,96,128]{2,1,0:T(8,128)(2,1)S(1)} %get-tuple-element.6), channel_id=1, source_target_pairs={{0,5},{1,4},{2,7},{3,6},{4,1},{5,0},{6,3},{7,2},{8,13},{9,12},{10,... | collective-permute-start | bytes 147464 | tf_op jit(solution)/shard_map/ppermute | solution.py:81
  180.8 2.1 copy-start.6
  180.8 5.4 %collective-permute-start.9 = (bf16[2,96,128]{2,1,0:T(8,128)(2,1)S(1)}, bf16[2,96,128]{2,1,0:T(8,128)(2,1)}, u32[]{:S(2)}, u32[]{:S(2)}) collective-permute-start(bf16[2,96,128]{2,1,0:T(8,128)(2,1)S(1)} %get-tuple-element.5), channel_id=1, source_target_pairs={{0,6},{1,7},{2,4},{3,5},{4,2},{5,3},{6,0},{7,1},{8,14},{9,15},{10,... | collective-permute-start | bytes 147464 | tf_op jit(solution)/shard_map/ppermute | solution.py:81
  182.9 3.4 %copy-start.7 = (bf16[2,96,128]{2,1,0:T(8,128)(2,1)}, bf16[2,96,128]{2,1,0:T(8,128)(2,1)S(1)}, u32[]{:S(2)}) copy-start(bf16[2,96,128]{2,1,0:T(8,128)(2,1)S(1)} %collective-permute-done.5.refs_2_) | copy-start | bytes 147460
  194.4 12.3 %all-to-all-start.5 = ((bf16[8,2,96,128]{3,2,1,0:T(8,128)(2,1)}), bf16[8,2,96,128]{3,2,1,0:T(8,128)(2,1)S(1)}, u32[]{:S(2)}, u32[]{:S(2)}) async-start(bf16[8,2,96,128]{3,2,1,0:T(8,128)(2,1)} %propagate.1), calls=%async_computation.5 | async-start | bytes 786432 | tf_op jit(solution)/shard_map/all_to_all | solution.py:21

commit v6 on v5

--- a/solution.py
+++ b/solution.py
@@ -21,17 +21,29 @@
     return lax.all_to_all(blocks, axes, split_axis=0, concat_axis=0, tiled=True)
 
 
-def fields_kernel(at_ref, own_hbm, other_hbm, out_ref, own_ref, other_ref, sems):
+def in_vmem(array):
+    return pltpu.with_memory_space_constraint(array, pltpu.VMEM)
+
+
+def in_hbm(array):
+    return pltpu.with_memory_space_constraint(array, pltpu.HBM)
+
+
+def operator_kernel(
+    at_ref, own_ref, other_ref, packed_hbm, out_hbm, fields_ref, packed_ref, out_ref, in_sems, out_sems
+):
     f32, bf16, i32 = jnp.float32, jnp.bfloat16, jnp.int32
-    vectors = out_ref.shape[2]
+    steps, width, vectors = packed_ref.shape
     rows = own_ref.shape[0]
     core_at = at_ref[0]
-    own_copy = pltpu.make_async_copy(own_hbm, own_ref, sems.at[0])
-    other_copy = pltpu.make_async_copy(other_hbm, other_ref, sems.at[1])
-    own_copy.start()
-    other_copy.start()
-    own_copy.wait()
-    other_copy.wait()
+    fetches = [
+        pltpu.make_async_copy(
+            packed_hbm.at[pl.ds(i * width, width), :], packed_ref.at[i], in_sems.at[i]
+        )
+        for i in range(steps)
+    ]
+    for fetch in fetches:
+        fetch.start()
     slot = lax.broadcasted_iota(i32, (rows, LANES), 0)
     lane = lax.broadcasted_iota(i32, (rows, LANES), 1)
     base = (((slot >> 1) & 7) * 4 + (slot >> 6) - 1) * 16
@@ -49,26 +61,48 @@
             ]
             pick = jnp.concatenate(hits, axis=1)
             fields = fields + jnp.dot(pick, picked[:, :vectors], preferred_element_type=f32)
-        out_ref[k ^ core_at] = fields.astype(bf16)
-
-
-def picked_fields(core_at, own, other):
-    rows, width = own.shape
-    vectors = width - LANES
-    anywhere = pl.BlockSpec(memory_space=pl.ANY)
-    fields = pl.pallas_call(
-        fields_kernel,
-        in_specs=[pl.BlockSpec(memory_space=pltpu.SMEM), anywhere, anywhere],
-        out_specs=pl.BlockSpec(memory_space=pltpu.VMEM),
-        out_shape=jax.ShapeDtypeStruct((2, rows, vectors), own.dtype),
+        fields_ref[k ^ core_at] = fields.astype(bf16)
+
+    writes = []
+    for i in range(steps):
+        fetches[i].wait()
+        for k in range(2):
+            product = lax.dot_general(
+                fields_ref[k], packed_ref[i], (((1,), (1,)), ((), ())), preferred_element_type=f32
+            )
+            product = product.astype(bf16).reshape(rows // 2, 2, width)
+            out_ref[i, k * (rows // 2) : (k + 1) * (rows // 2)] = product
+        write = pltpu.make_async_copy(
+            out_ref.at[i], out_hbm.at[:, :, pl.ds(i * width, width)], out_sems.at[i]
+        )
+        write.start()
+        writes.append(write)
+    for write in writes:
+        write.wait()
+
+
+def operator_blocks(core_at, own, other, packed):
+    rows, _ = own.shape
+    columns, vectors = packed.shape
+    steps = 3
+    width = columns // steps
+    whole = pl.BlockSpec(memory_space=pltpu.VMEM)
+    anywhere = pl.BlockSpec(memory_space=pltpu.HBM)
+    return pl.pallas_call(
+        operator_kernel,
+        in_specs=[pl.BlockSpec(memory_space=pltpu.SMEM), whole, whole, anywhere],
+        out_specs=anywhere,
+        out_shape=jax.ShapeDtypeStruct((rows, 2, columns), own.dtype),
         scratch_shapes=[
-            pltpu.VMEM(own.shape, own.dtype),
-            pltpu.VMEM(own.shape, own.dtype),
-            pltpu.SemaphoreType.DMA((2,)),
+            pltpu.VMEM((2, rows, vectors), own.dtype),
+            pltpu.VMEM((steps, width, vectors), own.dtype),
+            pltpu.VMEM((steps, rows, 2, width), own.dtype),
+            pltpu.SemaphoreType.DMA((steps,)),
+            pltpu.SemaphoreType.DMA((steps,)),
         ],
-        name="fields",
-    )(core_at.astype(jnp.int32).reshape(1), own, other)
-    return fields.reshape(2 * rows, vectors)
+        compiler_params=pltpu.CompilerParams(vmem_limit_bytes=28 * 2**20),
+        name="operator_blocks",
+    )(core_at.astype(jnp.int32).reshape(1), in_vmem(own), in_vmem(other), in_hbm(packed))
 
 
 def dealt(blocks, axes):
@@ -205,19 +239,20 @@
     share, rows_each, electrons = current[0].shape
     orbitals = narrow * rows_each
     f32, bf16 = jnp.float32, jnp.bfloat16
-    in_vmem = pl.BlockSpec(memory_space=pltpu.VMEM)
+    whole = pl.BlockSpec(memory_space=pltpu.VMEM)
     return pl.pallas_call(
         propagate_kernel,
-        in_specs=[pl.BlockSpec(memory_space=pltpu.SMEM)] + [in_vmem] * (1 + narrow),
-        out_specs=in_vmem,
-        out_shape=jax.ShapeDtypeStruct((narrow, share, rows_each, electrons), bf16),
+        in_specs=[pl.BlockSpec(memory_space=pltpu.SMEM)] + [whole] * (1 + narrow),
+        out_specs=whole,
+        out_shape=pltpu.VMEM((narrow, share, rows_each, electrons), bf16),
         scratch_shapes=[
             pltpu.VMEM((share, orbitals, orbitals), bf16),
             pltpu.VMEM((share, orbitals, electrons), f32),
             pltpu.VMEM((share, orbitals, electrons), f32),
         ],
+        compiler_params=pltpu.CompilerParams(vmem_limit_bytes=24 * 2**20),
         name="propagate",
-    )(narrow_at.astype(jnp.int32).reshape(1), blocks, *current)
+    )(narrow_at.astype(jnp.int32).reshape(1), in_vmem(blocks), *map(in_vmem, current))
 
 
 def per_device(walkers, intersection_inverse, noise, half_cholesky, cholesky, comb_source):
@@ -283,11 +318,7 @@
     aux = aux.reshape(plane_count * rows_here, vectors + LANES)
     other = lax.ppermute(aux, "c", swap)
 
-    fields = picked_fields(core_at, aux, other)
-    operator = lax.dot_general(
-        fields, packed, (((1,), (1,)), ((), ())), preferred_element_type=f32
-    ).astype(bf16)
-    operator = exchange(operator.reshape(wide_count * narrow_count, share, -1), MIXED)
+    operator = exchange(operator_blocks(core_at, aux, other, packed), MIXED)
 
     propagated = propagate(narrow_at, operator.transpose(1, 0, 2), current)
     new_walkers = exchange(propagated, NARROW)

time: 208 us -> 200 us (0.962)
  matrix products: 8.51 us -> 3.18 us
  local copies, waits for them, and re-layouts: 14.1 us -> 9.56 us
    dot_general x1 -> x0, matrix products: 5.31 us -> none  [per_device(): lax.dot_general(fields, packed, (((1,), (1,)), ((), ())), preferred_eleme...]
    pallas_call x1, Pallas kernels: 3.05 us -> 5.55 us  [operator_blocks(): pl.pallas_call(operator_kernel, in_specs=[pl.BlockSpec(memory_space=pltpu...]
    reshape x1 -> x0, local copies, waits for them, and re-layouts: 2.36 us -> none  [per_device(): operator.reshape(wide_count * narrow_count, share, -1)]
where the time goes in v6:
time: 200 us
  waiting for transfers between devices  92.3 us (46%)
  starting transfers between devices  44 us (22%)
  blocking collectives  28.8 us (14%)
  Pallas kernels  18.2 us (9%)
  local copies, waits for them, and re-layouts  9.56 us (5%)
  matrix products  3.18 us (2%)
  other arithmetic  2.65 us (1%)
    ppermute x1, waiting for transfers between devices, slot_walkers(): before = lax.ppermute(walkers, WIDE, up)  51.9 us
    all_to_all x4, waiting for transfers between devices, exchange(): return lax.all_to_all(blocks, axes, split_axis=0, concat_axis=0, tiled=True)  30.2 us
    all_to_all x4, starting transfers between devices, exchange(): return lax.all_to_all(blocks, axes, split_axis=0, concat_axis=0, tiled=True)  29.9 us
    all_to_all x2, blocking collectives, exchange(): return lax.all_to_all(blocks, axes, split_axis=0, concat_axis=0, tiled=True)  28.8 us
    ppermute x7, starting transfers between devices, dealt(): piece = lax.ppermute(piece, axes, [(i, i ^ k) for i in range(count)])  8.12 us
    pallas_call x1, Pallas kernels, propagate(): pl.pallas_call(propagate_kernel, in_specs=[pl.BlockSpec(memory_space=pltp...  6.36 us
    pallas_call x1, Pallas kernels, packed_cholesky(): pl.pallas_call(pack_kernel, grid=(vectors // width,), in_specs=[pl.BlockS...  6.28 us
    pallas_call x1, Pallas kernels, operator_blocks(): pl.pallas_call(operator_kernel, in_specs=[pl.BlockSpec(memory_space=pltpu...  5.55 us
  transfers between devices with their start and end apart: 15, of which 10 were waited for; matrix products, arithmetic and copies ran while one was open for 4% of the time, Pallas kernels for 3%

profile of v6, /device:TPU:6, one launch (start us, length us, event | category | flops | bytes accessed | tf_op | source)
XLA Modules:
  0.0 199.6 jit_solution(15899734478261515512)
XLA Ops:
  0.6 0.0 copy-start
  0.6 1.5 convolution_convert_fusion.1
  2.2 0.3 copy.15
  2.5 0.4 reshape.60
  2.8 0.9 copy.16
  3.7 11.6 %all-to-all-start = ((bf16[32,16,384]{2,1,0:T(8,128)(2,1)}), bf16[32,16,384]{2,1,0:T(8,128)(2,1)S(1)}, u32[]{:S(2)}, u32[]{:S(2)}) async-start(bf16[32,16,384]{2,1,0:T(8,128)(2,1)} %copy.16), calls=%async_computation | async-start | bytes 786432 | tf_op jit(solution)/shard_map/all_to_all | solution.py:21
  15.3 14.0 %all-to-all-done = bf16[32,16,384]{2,1,0:T(8,128)(2,1)S(1)} async-done(((bf16[32,16,384]{2,1,0:T(8,128)(2,1)}), bf16[32,16,384]{2,1,0:T(8,128)(2,1)S(1)}, u32[]{:S(2)}, u32[]{:S(2)}) %all-to-all-start) | async-done | bytes 393248 | tf_op jit(solution)/shard_map/all_to_all | solution.py:21
  29.3 0.1 reshape.61
  29.4 0.3 copy.17
  29.8 0.8 constant_dynamic-slice_fusion.3
  30.6 0.0 copy-done
  30.6 0.4 convolution_convert_fusion
  31.0 0.1 collective-permute-start
  31.1 1.9 collective-permute-done
  33.0 1.2 add_convert_fusion
  34.3 7.5 %all-to-all-start.1 = ((bf16[16,16,1024]{2,1,0:T(8,128)(2,1)}), bf16[16,16,1024]{2,1,0:T(8,128)(2,1)S(1)}, u32[]{:S(2)}, u32[]{:S(2)}) async-start(bf16[16,16,1024]{2,1,0:T(8,128)(2,1)} %bitcast.7), calls=%async_computation.1 | async-start | bytes 1048576 | tf_op jit(solution)/shard_map/all_to_all | solution.py:21
  41.7 0.0 copy-done.3
  41.7 0.1 dynamic-slice_convert_fusion
  41.8 0.1 broadcast_in_dim.36
  41.9 0.1 broadcast_in_dim.37
  42.0 0.7 constant_dynamic-slice_fusion.1
  42.7 8.8 %all-to-all-done.1 = bf16[16,16,1024]{2,1,0:T(8,128)(2,1)S(1)} async-done(((bf16[16,16,1024]{2,1,0:T(8,128)(2,1)}), bf16[16,16,1024]{2,1,0:T(8,128)(2,1)S(1)}, u32[]{:S(2)}, u32[]{:S(2)}) %all-to-all-start.1) | async-done | bytes 524320 | tf_op jit(solution)/shard_map/all_to_all | solution.py:21
  51.5 0.1 reduce_sum.21
  51.6 0.1 broadcast_in_dim.38
  51.7 14.8 %all_to_all.30 = bf16[8,16,1280]{2,1,0:T(8,128)(2,1)S(1)} all-to-all(bf16[8,16,1280]{2,1,0:T(8,128)(2,1)S(1)} %broadcast_in_dim.39), channel_id=1, replica_groups=mesh['z'=8,'x'=4,'y'=4,'c'=2] {'z'}, dimensions={0} | all-to-all | bytes 655360 | tf_op jit(solution)/shard_map/all_to_all | solution.py:21
  66.6 0.0 copy-start.2
  66.6 0.6 copy-done.2
  67.4 14.0 %all_to_all.31 = bf16[16,16,1152]{2,1,0:T(8,128)(2,1)S(1)} all-to-all(bf16[16,16,1152]{2,1,0:T(8,128)(2,1)S(1)} %broadcast_in_dim.40), channel_id=1, replica_groups=mesh['z'=8,'x'=4,'y'=4,'c'=2] {'x','y'}, dimensions={0} | all-to-all | bytes 1179648 | tf_op jit(solution)/shard_map/all_to_all | solution.py:21
  81.3 0.0 collective-permute-start.1
  81.3 6.3 %pack.1 = bf16[18,128,1024]{2,1,0:T(8,128)(2,1)} custom-call(bf16[96,24,1024]{2,1,0:T(8,128)(2,1)} %chol_ref.1), custom_call_target="tpu_custom_call" | custom-call | tf_op jit(solution)/shard_map/pack/pallas_call | solution.py:147
  87.6 0.0 collective-permute-done.1.other_ref
  87.6 5.5 %operator_blocks.1 = bf16[256,2,2304]{2,1,0:T(2,128)(2,1)} custom-call(s32[1]{0:T(128)} %bitcast.1.at_ref, bf16[256,1152]{1,0:T(8,128)(2,1)S(1)} %bitcast.48, bf16[256,1152]{1,0:T(8,128)(2,1)S(1)} %collective-permute-done.1.other_ref, bf16[2304,1024]{1,0:T(8,128)(2,1)} %bitcast.49), custom_call_target="tpu_custom_call" | custom-call | tf_op jit(solution)/shard_map/operator_blocks/pallas_call | solution.py:91
  93.2 0.0 copy-start.1
  93.2 7.4 %all-to-all-start.4 = ((bf16[256,2,2304]{2,1,0:T(2,128)(2,1)}), bf16[256,2,2304]{2,1,0:T(2,128)(2,1)S(1)}, u32[]{:S(2)}, u32[]{:S(2)}) async-start(bf16[256,2,2304]{2,1,0:T(2,128)(2,1)} %operator_blocks.1), calls=%async_computation.4 | async-start | bytes 4718592 | tf_op jit(solution)/shard_map/all_to_all | solution.py:21
  100.7 3.5 %collective-permute-start.2 = (bf16[16,96,128]{2,1,0:T(8,128)(2,1)S(1)}, bf16[16,96,128]{2,1,0:T(8,128)(2,1)}, u32[]{:S(2)}, u32[]{:S(2)}) collective-permute-start(bf16[16,96,128]{2,1,0:T(8,128)(2,1)S(1)} %copy-done.1), channel_id=1, source_target_pairs={{0,8},{8,16},{16,24},{24,32},{32,40},{40,48},{48,56},{56,64},{64,7... | collective-permute-start | bytes 1179656 | tf_op jit(solution)/shard_map/ppermute | solution.py:123
  104.2 2.3 %collective-permute-start.3 = (bf16[16,96,128]{2,1,0:T(8,128)(2,1)S(1)}, bf16[16,96,128]{2,1,0:T(8,128)(2,1)}, u32[]{:S(2)}, u32[]{:S(2)}) collective-permute-start(bf16[16,96,128]{2,1,0:T(8,128)(2,1)S(1)} %copy-done.1), channel_id=1, source_target_pairs={{8,0},{16,8},{24,16},{32,24},{40,32},{48,40},{56,48},{64,56},{72,6... | collective-permute-start | bytes 1179656 | tf_op jit(solution)/shard_map/ppermute | solution.py:124
  106.5 0.1 broadcast_in_dim.41
  106.7 51.9 %collective-permute-done.2 = bf16[16,96,128]{2,1,0:T(8,128)(2,1)} collective-permute-done((bf16[16,96,128]{2,1,0:T(8,128)(2,1)S(1)}, bf16[16,96,128]{2,1,0:T(8,128)(2,1)}, u32[]{:S(2)}, u32[]{:S(2)}) %collective-permute-start.2) | collective-permute-done | bytes 393248 | tf_op jit(solution)/shard_map/ppermute | solution.py:123
  158.5 3.2 %collective-permute-done.3 = bf16[16,96,128]{2,1,0:T(8,128)(2,1)} collective-permute-done((bf16[16,96,128]{2,1,0:T(8,128)(2,1)S(1)}, bf16[16,96,128]{2,1,0:T(8,128)(2,1)}, u32[]{:S(2)}, u32[]{:S(2)}) %collective-permute-start.3) | collective-permute-done | bytes 393248 | tf_op jit(solution)/shard_map/ppermute | solution.py:124
  161.7 2.3 %pad_maximum_fusion = bf16[48,96,128]{2,1,0:T(8,128)(2,1)} fusion(bf16[16,96,128]{2,1,0:T(8,128)(2,1)} %collective-permute-done.3, bf16[16,96,128]{2,1,0:T(8,128)(2,1)S(1)} %copy-done.1, bf16[16,96,128]{2,1,0:T(8,128)(2,1)} %collective-permute-done.2), kind=kLoop, calls=%fused_computation.4 | loop fusion | flops 1179648 | bytes 2359296 | tf_op jit(solution)/shard_map/concatenate | solution.py:125
  164.0 1.9 gather_fusion
  165.9 0.1 broadcast_select_fusion
  166.0 0.7 dynamic-slice_bitcast_fusion
  166.7 2.0 collective-permute-start.10
  168.6 1.0 collective-permute-start.4
  169.7 0.0 collective-permute-start.5
  169.7 1.4 collective-permute-start.6
  171.0 0.5 collective-permute-start.7
  171.5 0.2 collective-permute-done.10.refs_7_
  171.7 2.9 %collective-permute-start.8 = (bf16[2,96,128]{2,1,0:T(8,128)(2,1)}, bf16[2,96,128]{2,1,0:T(8,128)(2,1)S(1)}, u32[]{:S(2)}, u32[]{:S(2)}) collective-permute-start(bf16[2,96,128]{2,1,0:T(8,128)(2,1)} %get-tuple-element.6), channel_id=1, source_target_pairs={{0,5},{1,4},{2,7},{3,6},{4,1},{5,0},{6,3},{7,2},{8,13},{9,12},{10,... | collective-permute-start | bytes 147464 | tf_op jit(solution)/shard_map/ppermute | solution.py:115
  174.7 0.0 collective-permute-done.4.refs_1_
  174.7 0.4 collective-permute-start.9
  175.0 0.0 all-to-all-done.4
  175.0 0.2 copy.30
  175.3 0.0 collective-permute-done.5.refs_2_
  175.3 0.0 collective-permute-done.6.refs_3_
  175.3 2.0 %collective-permute-done.7.refs_4_ = bf16[2,96,128]{2,1,0:T(8,128)(2,1)S(1)} collective-permute-done((bf16[2,96,128]{2,1,0:T(8,128)(2,1)}, bf16[2,96,128]{2,1,0:T(8,128)(2,1)S(1)}, u32[]{:S(2)}, u32[]{:S(2)}) %collective-permute-start.7) | collective-permute-done | bytes 49184 | tf_op jit(solution)/shard_map/ppermute | solution.py:115
  177.3 0.7 collective-permute-done.8.refs_5_
  178.0 2.1 %collective-permute-done.9.refs_6_ = bf16[2,96,128]{2,1,0:T(8,128)(2,1)S(1)} collective-permute-done((bf16[2,96,128]{2,1,0:T(8,128)(2,1)}, bf16[2,96,128]{2,1,0:T(8,128)(2,1)S(1)}, u32[]{:S(2)}, u32[]{:S(2)}) %collective-permute-start.9) | collective-permute-done | bytes 49184 | tf_op jit(solution)/shard_map/ppermute | solution.py:115
  180.2 6.4 %propagate.1 = bf16[8,2,96,128]{3,2,1,0:T(8,128)(2,1)} custom-call(s32[1]{0:T(128)} %bitcast.at_ref, bf16[2,256,2304]{2,1,0:T(8,128)(2,1)S(1)} %bitcast.46, bf16[2,96,128]{2,1,0:T(8,128)(2,1)S(1)} %get-tuple-element.11.refs_0_, bf16[2,96,128]{2,1,0:T(8,128)(2,1)S(1)} %collective-permute-done.4.refs_1_, ...), custom_call_target="tpu_custom_call" | custom-call | tf_op jit(solution)/shard_map/propagate/pallas_call | solution.py:243
  186.5 3.5 %all-to-all-start.5 = ((bf16[8,2,96,128]{3,2,1,0:T(8,128)(2,1)}), bf16[8,2,96,128]{3,2,1,0:T(8,128)(2,1)S(1)}, u32[]{:S(2)}, u32[]{:S(2)}) async-start(bf16[8,2,96,128]{3,2,1,0:T(8,128)(2,1)} %propagate.1), calls=%async_computation.5 | async-start | bytes 786432 | tf_op jit(solution)/shard_map/all_to_all | solution.py:21
  190.0 1.4 constant_dynamic-slice_fusion
  191.4 7.5 %all-to-all-done.5 = bf16[8,2,96,128]{3,2,1,0:T(8,128)(2,1)S(1)} async-done(((bf16[8,2,96,128]{3,2,1,0:T(8,128)(2,1)}), bf16[8,2,96,128]{3,2,1,0:T(8,128)(2,1)S(1)}, u32[]{:S(2)}, u32[]{:S(2)}) %all-to-all-start.5) | async-done | bytes 393248 | tf_op jit(solution)/shard_map/all_to_all | solution.py:21
  198.8 0.7 copy.32
  (15 shorter events, 0.2 us)
Async XLA Ops:
  0.6 30.0 %copy-start = (bf16[4,96,1024]{2,1,0:T(8,128)(2,1)S(1)}, bf16[4,96,1024]{2,1,0:T(8,128)(2,1)}, u32[]{:S(2)}) copy-start(bf16[4,96,1024]{2,1,0:T(8,128)(2,1)} %param.9) | copy-start | bytes 2359300
  3.7 25.6 %all-to-all-start = ((bf16[32,16,384]{2,1,0:T(8,128)(2,1)}), bf16[32,16,384]{2,1,0:T(8,128)(2,1)S(1)}, u32[]{:S(2)}, u32[]{:S(2)}) async-start(bf16[32,16,384]{2,1,0:T(8,128)(2,1)} %copy.16), calls=%async_computation | async-start | bytes 786432 | tf_op jit(solution)/shard_map/all_to_all | solution.py:21
  31.0 2.0 %collective-permute-start = (bf16[256,1024]{1,0:T(8,128)(2,1)S(1)}, bf16[256,1024]{1,0:T(8,128)(2,1)S(1)}, u32[]{:S(2)}, u32[]{:S(2)}) collective-permute-start(bf16[256,1024]{1,0:T(8,128)(2,1)S(1)} %convolution_convert_fusion), channel_id=1, source_target_pairs={{0,1},{1,0},{2,3},{3,2},{4,5},{5,4},{6,7},{7,6},{8,9},{9,8},{10,11... | collective-permute-start | bytes 1572872 | tf_op jit(solution)/shard_map/ppermute | solution.py:302
  33.0 8.7 %copy-start.3 = (s32[16]{0:T(128)S(1)}, s32[16]{0:T(128)}, u32[]{:S(2)}) copy-start(s32[16]{0:T(128)} %param.11) | copy-start | bytes 196
  34.3 17.2 %all-to-all-start.1 = ((bf16[16,16,1024]{2,1,0:T(8,128)(2,1)}), bf16[16,16,1024]{2,1,0:T(8,128)(2,1)S(1)}, u32[]{:S(2)}, u32[]{:S(2)}) async-start(bf16[16,16,1024]{2,1,0:T(8,128)(2,1)} %bitcast.7), calls=%async_computation.1 | async-start | bytes 1048576 | tf_op jit(solution)/shard_map/all_to_all | solution.py:21
  66.6 0.6 copy-start.2
  81.3 6.3 %collective-permute-start.1 = (bf16[256,1152]{1,0:T(8,128)(2,1)S(1)}, bf16[256,1152]{1,0:T(8,128)(2,1)S(1)}, u32[]{:S(2)}, u32[]{:S(2)}) collective-permute-start(bf16[256,1152]{1,0:T(8,128)(2,1)S(1)} %bitcast.47), channel_id=1, source_target_pairs={{0,1},{1,0},{2,3},{3,2},{4,5},{5,4},{6,7},{7,6},{8,9},{9,8},{10,11... | collective-permute-start | bytes 1769480 | tf_op jit(solution)/shard_map/ppermute | solution.py:319
  93.2 7.5 %copy-start.1 = (bf16[16,96,128]{2,1,0:T(8,128)(2,1)S(1)}, bf16[16,96,128]{2,1,0:T(8,128)(2,1)}, u32[]{:S(2)}) copy-start(bf16[16,96,128]{2,1,0:T(8,128)(2,1)} %param.6) | copy-start | bytes 1179652
  93.2 81.9 %all-to-all-start.4 = ((bf16[256,2,2304]{2,1,0:T(2,128)(2,1)}), bf16[256,2,2304]{2,1,0:T(2,128)(2,1)S(1)}, u32[]{:S(2)}, u32[]{:S(2)}) async-start(bf16[256,2,2304]{2,1,0:T(2,128)(2,1)} %operator_blocks.1), calls=%async_computation.4 | async-start | bytes 4718592 | tf_op jit(solution)/shard_map/all_to_all | solution.py:21
  100.7 57.9 %collective-permute-start.2 = (bf16[16,96,128]{2,1,0:T(8,128)(2,1)S(1)}, bf16[16,96,128]{2,1,0:T(8,128)(2,1)}, u32[]{:S(2)}, u32[]{:S(2)}) collective-permute-start(bf16[16,96,128]{2,1,0:T(8,128)(2,1)S(1)} %copy-done.1), channel_id=1, source_target_pairs={{0,8},{8,16},{16,24},{24,32},{32,40},{40,48},{48,56},{56,64},{64,7... | collective-permute-start | bytes 1179656 | tf_op jit(solution)/shard_map/ppermute | solution.py:123
  104.2 57.5 %collective-permute-start.3 = (bf16[16,96,128]{2,1,0:T(8,128)(2,1)S(1)}, bf16[16,96,128]{2,1,0:T(8,128)(2,1)}, u32[]{:S(2)}, u32[]{:S(2)}) collective-permute-start(bf16[16,96,128]{2,1,0:T(8,128)(2,1)S(1)} %copy-done.1), channel_id=1, source_target_pairs={{8,0},{16,8},{24,16},{32,24},{40,32},{48,40},{56,48},{64,56},{72,6... | collective-permute-start | bytes 1179656 | tf_op jit(solution)/shard_map/ppermute | solution.py:124
  166.7 5.0 %collective-permute-start.10 = (bf16[2,96,128]{2,1,0:T(8,128)(2,1)S(1)}, bf16[2,96,128]{2,1,0:T(8,128)(2,1)S(1)}, u32[]{:S(2)}, u32[]{:S(2)}) collective-permute-start(bf16[2,96,128]{2,1,0:T(8,128)(2,1)S(1)} %get-tuple-element.4), channel_id=1, source_target_pairs={{0,7},{1,6},{2,5},{3,4},{4,3},{5,2},{6,1},{7,0},{8,15},{9,14},{10,... | collective-permute-start | bytes 147464 | tf_op jit(solution)/shard_map/ppermute | solution.py:115
  168.6 6.0 %collective-permute-start.4 = (bf16[2,96,128]{2,1,0:T(8,128)(2,1)S(1)}, bf16[2,96,128]{2,1,0:T(8,128)(2,1)S(1)}, u32[]{:S(2)}, u32[]{:S(2)}) collective-permute-start(bf16[2,96,128]{2,1,0:T(8,128)(2,1)S(1)} %get-tuple-element.10), channel_id=1, source_target_pairs={{0,1},{1,0},{2,3},{3,2},{4,5},{5,4},{6,7},{7,6},{8,9},{9,8},{10,11... | collective-permute-start | bytes 147464 | tf_op jit(solution)/shard_map/ppermute | solution.py:115
  169.7 5.6 %collective-permute-start.5 = (bf16[2,96,128]{2,1,0:T(8,128)(2,1)}, bf16[2,96,128]{2,1,0:T(8,128)(2,1)S(1)}, u32[]{:S(2)}, u32[]{:S(2)}) collective-permute-start(bf16[2,96,128]{2,1,0:T(8,128)(2,1)} %get-tuple-element.9), channel_id=1, source_target_pairs={{0,2},{1,3},{2,0},{3,1},{4,6},{5,7},{6,4},{7,5},{8,10},{9,11},{10,... | collective-permute-start | bytes 147464 | tf_op jit(solution)/shard_map/ppermute | solution.py:115
  169.7 5.6 %collective-permute-start.6 = (bf16[2,96,128]{2,1,0:T(8,128)(2,1)}, bf16[2,96,128]{2,1,0:T(8,128)(2,1)S(1)}, u32[]{:S(2)}, u32[]{:S(2)}) collective-permute-start(bf16[2,96,128]{2,1,0:T(8,128)(2,1)} %get-tuple-element.8), channel_id=1, source_target_pairs={{0,3},{1,2},{2,1},{3,0},{4,7},{5,6},{6,5},{7,4},{8,11},{9,10},{10,... | collective-permute-start | bytes 147464 | tf_op jit(solution)/shard_map/ppermute | solution.py:115
  171.0 6.3 %collective-permute-start.7 = (bf16[2,96,128]{2,1,0:T(8,128)(2,1)}, bf16[2,96,128]{2,1,0:T(8,128)(2,1)S(1)}, u32[]{:S(2)}, u32[]{:S(2)}) collective-permute-start(bf16[2,96,128]{2,1,0:T(8,128)(2,1)} %get-tuple-element.7), channel_id=1, source_target_pairs={{0,4},{1,5},{2,6},{3,7},{4,0},{5,1},{6,2},{7,3},{8,12},{9,13},{10,... | collective-permute-start | bytes 147464 | tf_op jit(solution)/shard_map/ppermute | solution.py:115
  171.7 6.3 %collective-permute-start.8 = (bf16[2,96,128]{2,1,0:T(8,128)(2,1)}, bf16[2,96,128]{2,1,0:T(8,128)(2,1)S(1)}, u32[]{:S(2)}, u32[]{:S(2)}) collective-permute-start(bf16[2,96,128]{2,1,0:T(8,128)(2,1)} %get-tuple-element.6), channel_id=1, source_target_pairs={{0,5},{1,4},{2,7},{3,6},{4,1},{5,0},{6,3},{7,2},{8,13},{9,12},{10,... | collective-permute-start | bytes 147464 | tf_op jit(solution)/shard_map/ppermute | solution.py:115
  174.7 5.5 %collective-permute-start.9 = (bf16[2,96,128]{2,1,0:T(8,128)(2,1)}, bf16[2,96,128]{2,1,0:T(8,128)(2,1)S(1)}, u32[]{:S(2)}, u32[]{:S(2)}) collective-permute-start(bf16[2,96,128]{2,1,0:T(8,128)(2,1)} %get-tuple-element.5), channel_id=1, source_target_pairs={{0,6},{1,7},{2,4},{3,5},{4,2},{5,3},{6,0},{7,1},{8,14},{9,15},{10,... | collective-permute-start | bytes 147464 | tf_op jit(solution)/shard_map/ppermute | solution.py:115
  186.5 12.3 %all-to-all-start.5 = ((bf16[8,2,96,128]{3,2,1,0:T(8,128)(2,1)}), bf16[8,2,96,128]{3,2,1,0:T(8,128)(2,1)S(1)}, u32[]{:S(2)}, u32[]{:S(2)}) async-start(bf16[8,2,96,128]{3,2,1,0:T(8,128)(2,1)} %propagate.1), calls=%async_computation.5 | async-start | bytes 786432 | tf_op jit(solution)/shard_map/all_to_all | solution.py:21

commit v7 on v6

--- a/solution.py
+++ b/solution.py
@@ -84,7 +84,7 @@
 def operator_blocks(core_at, own, other, packed):
     rows, _ = own.shape
     columns, vectors = packed.shape
-    steps = 3
+    steps = 2
     width = columns // steps
     whole = pl.BlockSpec(memory_space=pltpu.VMEM)
     anywhere = pl.BlockSpec(memory_space=pltpu.HBM)
@@ -162,7 +162,7 @@
     f32, bf16 = jnp.float32, jnp.bfloat16
     lane = lax.broadcasted_iota(jnp.int32, (32, 128), 1)
 
-    def assemble(s, carry):
+    def assemble(s):
         def rows_of(t, n):
             at = t * 128
             first = (n & 1) * 128 + (n >> 1) * 8
@@ -202,9 +202,9 @@
                 for k, tile in enumerate(tiles):
                     at = half * 384 + k * 128
                     matrix_ref[s, j * 32 : (j + 1) * 32, at : at + 128] = tile.astype(bf16)
-        return carry
-
-    lax.fori_loop(0, share, assemble, 0)
+
+    for s in range(share):
+        assemble(s)
     narrow, _, rows_each, _ = out_ref.shape
     for k, current_ref in enumerate(current_refs):
         first_row = pl.multiple_of((at_ref[0] ^ k) * rows_each, 8)
@@ -296,11 +296,14 @@
     pairs = pairs.reshape(z_count, x_count, y_count, core_count, share, -1)
     pairs = pairs.transpose(3, 1, 2, 0, 4, 5).reshape(core_count, plane_count * rows_here, -1)
     half_flat = half_cholesky.reshape(-1, vectors)
-    mine = lax.dynamic_index_in_dim(pairs, core_at, 0, keepdims=False)
     theirs = lax.dynamic_index_in_dim(pairs, 1 - core_at, 0, keepdims=False)
     sent = jnp.dot(theirs, half_flat, preferred_element_type=f32).astype(bf16)
+    pairs, sent = lax.optimization_barrier((pairs, sent))
     received = lax.ppermute(sent, "c", swap)
-    partial = jnp.dot(mine, half_flat, preferred_element_type=f32) + received.astype(f32)
+    mine = lax.dynamic_index_in_dim(pairs, core_at, 0, keepdims=False)
+    own = jnp.dot(mine, half_flat, preferred_element_type=f32)
+    own = lax.optimization_barrier(own)
+    partial = own + received.astype(f32)
     partial = partial.astype(bf16).reshape(plane_count, rows_here, vectors)
     partial = exchange(partial, PLANE)
 

time: 200 us -> 200 us (level)
  no operation moved by 1% of the time
where the time goes in v7:
time: 200 us; the launch traced here: 199 us
  waiting for transfers between devices  91.4 us (46%)
  starting transfers between devices  44 us (22%)
  blocking collectives  28.8 us (14%)
  Pallas kernels  18.3 us (9%)
  local copies, waits for them, and re-layouts  9.55 us (5%)
  other arithmetic  3.6 us (2%)
  matrix products  2.39 us (1%)
    ppermute x1, waiting for transfers between devices, slot_walkers(): before = lax.ppermute(walkers, WIDE, up)  51.9 us
    all_to_all x4, waiting for transfers between devices, exchange(): return lax.all_to_all(blocks, axes, split_axis=0, concat_axis=0, tiled=True)  30.2 us
    all_to_all x4, starting transfers between devices, exchange(): return lax.all_to_all(blocks, axes, split_axis=0, concat_axis=0, tiled=True)  29.9 us
    all_to_all x2, blocking collectives, exchange(): return lax.all_to_all(blocks, axes, split_axis=0, concat_axis=0, tiled=True)  28.8 us
    ppermute x7, starting transfers between devices, dealt(): piece = lax.ppermute(piece, axes, [(i, i ^ k) for i in range(count)])  8.12 us
    pallas_call x1, Pallas kernels, packed_cholesky(): pl.pallas_call(pack_kernel, grid=(vectors // width,), in_specs=[pl.BlockS...  6.28 us
    pallas_call x1, Pallas kernels, propagate(): pl.pallas_call(propagate_kernel, in_specs=[pl.BlockSpec(memory_space=pltp...  6.04 us
    pallas_call x1, Pallas kernels, operator_blocks(): pl.pallas_call(operator_kernel, in_specs=[pl.BlockSpec(memory_space=pltpu...  6 us
  transfers between devices with their start and end apart: 15, of which 10 were waited for; matrix products, arithmetic and copies ran while one was open for 4% of the time, Pallas kernels for 3%

profile of v7, /device:TPU:6, one launch (start us, length us, event | category | flops | bytes accessed | tf_op | source)
XLA Modules:
  0.0 199.0 jit_solution(15035858998216440043)
XLA Ops:
  0.6 0.0 copy-start
  0.6 1.5 convolution_convert_fusion.1
  2.2 0.3 copy.15
  2.5 0.4 reshape.60
  2.8 0.9 copy.16
  3.7 11.6 %all-to-all-start = ((bf16[32,16,384]{2,1,0:T(8,128)(2,1)}), bf16[32,16,384]{2,1,0:T(8,128)(2,1)S(1)}, u32[]{:S(2)}, u32[]{:S(2)}) async-start(bf16[32,16,384]{2,1,0:T(8,128)(2,1)} %copy.16), calls=%async_computation | async-start | bytes 786432 | tf_op jit(solution)/shard_map/all_to_all | solution.py:21
  15.3 14.0 %all-to-all-done = bf16[32,16,384]{2,1,0:T(8,128)(2,1)S(1)} async-done(((bf16[32,16,384]{2,1,0:T(8,128)(2,1)}), bf16[32,16,384]{2,1,0:T(8,128)(2,1)S(1)}, u32[]{:S(2)}, u32[]{:S(2)}) %all-to-all-start) | async-done | bytes 393248 | tf_op jit(solution)/shard_map/all_to_all | solution.py:21
  29.3 0.1 reshape.61
  29.4 0.3 copy.17
  29.8 0.4 constant_dynamic-slice_fusion.3
  30.2 0.4 convolution_convert_fusion
  30.6 0.1 collective-permute-start
  30.7 0.4 constant_dynamic-slice_fusion.2
  31.2 0.4 fusion
  31.6 0.0 copy-start.3
  31.6 1.0 collective-permute-done
  32.6 0.9 add_convert_fusion
  33.6 7.5 %all-to-all-start.1 = ((bf16[16,16,1024]{2,1,0:T(8,128)(2,1)}), bf16[16,16,1024]{2,1,0:T(8,128)(2,1)S(1)}, u32[]{:S(2)}, u32[]{:S(2)}) async-start(bf16[16,16,1024]{2,1,0:T(8,128)(2,1)} %bitcast.7), calls=%async_computation.1 | async-start | bytes 1048576 | tf_op jit(solution)/shard_map/all_to_all | solution.py:21
  41.0 0.1 dynamic-slice_convert_fusion
  41.1 0.1 broadcast_in_dim.36
  41.2 0.1 broadcast_in_dim.37
  41.3 0.7 constant_dynamic-slice_fusion.1
  42.0 8.8 %all-to-all-done.1 = bf16[16,16,1024]{2,1,0:T(8,128)(2,1)S(1)} async-done(((bf16[16,16,1024]{2,1,0:T(8,128)(2,1)}), bf16[16,16,1024]{2,1,0:T(8,128)(2,1)S(1)}, u32[]{:S(2)}, u32[]{:S(2)}) %all-to-all-start.1) | async-done | bytes 524320 | tf_op jit(solution)/shard_map/all_to_all | solution.py:21
  50.8 0.1 reduce_sum.21
  50.9 0.1 broadcast_in_dim.38
  51.0 14.8 %all_to_all.30 = bf16[8,16,1280]{2,1,0:T(8,128)(2,1)S(1)} all-to-all(bf16[8,16,1280]{2,1,0:T(8,128)(2,1)S(1)} %broadcast_in_dim.39), channel_id=1, replica_groups=mesh['z'=8,'x'=4,'y'=4,'c'=2] {'z'}, dimensions={0} | all-to-all | bytes 655360 | tf_op jit(solution)/shard_map/all_to_all | solution.py:21
  65.9 0.6 copy-done.2
  66.6 14.0 %all_to_all.31 = bf16[16,16,1152]{2,1,0:T(8,128)(2,1)S(1)} all-to-all(bf16[16,16,1152]{2,1,0:T(8,128)(2,1)S(1)} %broadcast_in_dim.40), channel_id=1, replica_groups=mesh['z'=8,'x'=4,'y'=4,'c'=2] {'x','y'}, dimensions={0} | all-to-all | bytes 1179648 | tf_op jit(solution)/shard_map/all_to_all | solution.py:21
  80.6 0.0 collective-permute-start.1
  80.6 6.3 %pack.1 = bf16[18,128,1024]{2,1,0:T(8,128)(2,1)} custom-call(bf16[96,24,1024]{2,1,0:T(8,128)(2,1)} %chol_ref.1), custom_call_target="tpu_custom_call" | custom-call | tf_op jit(solution)/shard_map/pack/pallas_call | solution.py:147
  86.9 0.0 collective-permute-done.1.other_ref
  86.9 6.0 %operator_blocks.1 = bf16[256,2,2304]{2,1,0:T(2,128)(2,1)} custom-call(s32[1]{0:T(128)} %bitcast.1.at_ref, bf16[256,1152]{1,0:T(8,128)(2,1)S(1)} %bitcast.46, bf16[256,1152]{1,0:T(8,128)(2,1)S(1)} %collective-permute-done.1.other_ref, bf16[2304,1024]{1,0:T(8,128)(2,1)} %bitcast.47), custom_call_target="tpu_custom_call" | custom-call | tf_op jit(solution)/shard_map/operator_blocks/pallas_call | solution.py:91
  92.9 0.0 copy-start.1
  92.9 7.4 %all-to-all-start.4 = ((bf16[256,2,2304]{2,1,0:T(2,128)(2,1)}), bf16[256,2,2304]{2,1,0:T(2,128)(2,1)S(1)}, u32[]{:S(2)}, u32[]{:S(2)}) async-start(bf16[256,2,2304]{2,1,0:T(2,128)(2,1)} %operator_blocks.1), calls=%async_computation.4 | async-start | bytes 4718592 | tf_op jit(solution)/shard_map/all_to_all | solution.py:21
  100.4 3.5 %collective-permute-start.2 = (bf16[16,96,128]{2,1,0:T(8,128)(2,1)S(1)}, bf16[16,96,128]{2,1,0:T(8,128)(2,1)}, u32[]{:S(2)}, u32[]{:S(2)}) collective-permute-start(bf16[16,96,128]{2,1,0:T(8,128)(2,1)S(1)} %copy-done.1), channel_id=1, source_target_pairs={{0,8},{8,16},{16,24},{24,32},{32,40},{40,48},{48,56},{56,64},{64,7... | collective-permute-start | bytes 1179656 | tf_op jit(solution)/shard_map/ppermute | solution.py:123
  103.9 2.3 %collective-permute-start.3 = (bf16[16,96,128]{2,1,0:T(8,128)(2,1)S(1)}, bf16[16,96,128]{2,1,0:T(8,128)(2,1)}, u32[]{:S(2)}, u32[]{:S(2)}) collective-permute-start(bf16[16,96,128]{2,1,0:T(8,128)(2,1)S(1)} %copy-done.1), channel_id=1, source_target_pairs={{8,0},{16,8},{24,16},{32,24},{40,32},{48,40},{56,48},{64,56},{72,6... | collective-permute-start | bytes 1179656 | tf_op jit(solution)/shard_map/ppermute | solution.py:124
  106.3 0.1 broadcast_in_dim.41
  106.4 51.9 %collective-permute-done.2 = bf16[16,96,128]{2,1,0:T(8,128)(2,1)} collective-permute-done((bf16[16,96,128]{2,1,0:T(8,128)(2,1)S(1)}, bf16[16,96,128]{2,1,0:T(8,128)(2,1)}, u32[]{:S(2)}, u32[]{:S(2)}) %collective-permute-start.2) | collective-permute-done | bytes 393248 | tf_op jit(solution)/shard_map/ppermute | solution.py:123
  158.2 3.2 %collective-permute-done.3 = bf16[16,96,128]{2,1,0:T(8,128)(2,1)} collective-permute-done((bf16[16,96,128]{2,1,0:T(8,128)(2,1)S(1)}, bf16[16,96,128]{2,1,0:T(8,128)(2,1)}, u32[]{:S(2)}, u32[]{:S(2)}) %collective-permute-start.3) | collective-permute-done | bytes 393248 | tf_op jit(solution)/shard_map/ppermute | solution.py:124
  161.4 2.3 %pad_maximum_fusion = bf16[48,96,128]{2,1,0:T(8,128)(2,1)} fusion(bf16[16,96,128]{2,1,0:T(8,128)(2,1)} %collective-permute-done.3, bf16[16,96,128]{2,1,0:T(8,128)(2,1)S(1)} %copy-done.1, bf16[16,96,128]{2,1,0:T(8,128)(2,1)} %collective-permute-done.2), kind=kLoop, calls=%fused_computation.4 | loop fusion | flops 1179648 | bytes 2359296 | tf_op jit(solution)/shard_map/concatenate | solution.py:125
  163.7 1.9 gather_fusion
  165.6 0.1 broadcast_select_fusion
  165.7 0.7 dynamic-slice_bitcast_fusion
  166.4 2.0 collective-permute-start.10
  168.4 1.0 collective-permute-start.4
  169.4 0.0 collective-permute-start.5
  169.4 1.4 collective-permute-start.6
  170.8 0.5 collective-permute-start.7
  171.2 0.2 collective-permute-done.10.refs_7_
  171.5 2.9 %collective-permute-start.8 = (bf16[2,96,128]{2,1,0:T(8,128)(2,1)}, bf16[2,96,128]{2,1,0:T(8,128)(2,1)S(1)}, u32[]{:S(2)}, u32[]{:S(2)}) collective-permute-start(bf16[2,96,128]{2,1,0:T(8,128)(2,1)} %get-tuple-element.10), channel_id=1, source_target_pairs={{0,5},{1,4},{2,7},{3,6},{4,1},{5,0},{6,3},{7,2},{8,13},{9,12},{10,... | collective-permute-start | bytes 147464 | tf_op jit(solution)/shard_map/ppermute | solution.py:115
  174.4 0.0 collective-permute-done.4.refs_1_
  174.4 0.4 collective-permute-start.9
  174.8 0.0 all-to-all-done.4
  174.8 0.2 copy.30
  175.0 0.0 collective-permute-done.5.refs_2_
  175.0 0.0 collective-permute-done.6.refs_3_
  175.0 2.0 %collective-permute-done.7.refs_4_ = bf16[2,96,128]{2,1,0:T(8,128)(2,1)S(1)} collective-permute-done((bf16[2,96,128]{2,1,0:T(8,128)(2,1)}, bf16[2,96,128]{2,1,0:T(8,128)(2,1)S(1)}, u32[]{:S(2)}, u32[]{:S(2)}) %collective-permute-start.7) | collective-permute-done | bytes 49184 | tf_op jit(solution)/shard_map/ppermute | solution.py:115
  177.1 0.7 collective-permute-done.8.refs_5_
  177.8 2.1 %collective-permute-done.9.refs_6_ = bf16[2,96,128]{2,1,0:T(8,128)(2,1)S(1)} collective-permute-done((bf16[2,96,128]{2,1,0:T(8,128)(2,1)}, bf16[2,96,128]{2,1,0:T(8,128)(2,1)S(1)}, u32[]{:S(2)}, u32[]{:S(2)}) %collective-permute-start.9) | collective-permute-done | bytes 49184 | tf_op jit(solution)/shard_map/ppermute | solution.py:115
  179.9 6.0 %propagate.1 = bf16[8,2,96,128]{3,2,1,0:T(8,128)(2,1)} custom-call(s32[1]{0:T(128)} %bitcast.at_ref, bf16[2,256,2304]{2,1,0:T(8,128)(2,1)S(1)} %bitcast.44, bf16[2,96,128]{2,1,0:T(8,128)(2,1)S(1)} %get-tuple-element.15.refs_0_, bf16[2,96,128]{2,1,0:T(8,128)(2,1)S(1)} %collective-permute-done.4.refs_1_, ...), custom_call_target="tpu_custom_call" | custom-call | tf_op jit(solution)/shard_map/propagate/pallas_call | solution.py:243
  186.0 3.5 %all-to-all-start.5 = ((bf16[8,2,96,128]{3,2,1,0:T(8,128)(2,1)}), bf16[8,2,96,128]{3,2,1,0:T(8,128)(2,1)S(1)}, u32[]{:S(2)}, u32[]{:S(2)}) async-start(bf16[8,2,96,128]{3,2,1,0:T(8,128)(2,1)} %propagate.1), calls=%async_computation.5 | async-start | bytes 786432 | tf_op jit(solution)/shard_map/all_to_all | solution.py:21
  189.4 1.4 constant_dynamic-slice_fusion
  190.8 7.5 %all-to-all-done.5 = bf16[8,2,96,128]{3,2,1,0:T(8,128)(2,1)S(1)} async-done(((bf16[8,2,96,128]{3,2,1,0:T(8,128)(2,1)}), bf16[8,2,96,128]{3,2,1,0:T(8,128)(2,1)S(1)}, u32[]{:S(2)}, u32[]{:S(2)}) %all-to-all-start.5) | async-done | bytes 393248 | tf_op jit(solution)/shard_map/all_to_all | solution.py:21
  198.3 0.7 copy.32
  (17 shorter events, 0.2 us)
Async XLA Ops:
  0.6 29.6 %copy-start = (bf16[4,96,1024]{2,1,0:T(8,128)(2,1)S(1)}, bf16[4,96,1024]{2,1,0:T(8,128)(2,1)}, u32[]{:S(2)}) copy-start(bf16[4,96,1024]{2,1,0:T(8,128)(2,1)} %param.9) | copy-start | bytes 2359300
  3.7 25.6 %all-to-all-start = ((bf16[32,16,384]{2,1,0:T(8,128)(2,1)}), bf16[32,16,384]{2,1,0:T(8,128)(2,1)S(1)}, u32[]{:S(2)}, u32[]{:S(2)}) async-start(bf16[32,16,384]{2,1,0:T(8,128)(2,1)} %copy.16), calls=%async_computation | async-start | bytes 786432 | tf_op jit(solution)/shard_map/all_to_all | solution.py:21
  30.6 2.0 %collective-permute-start = (bf16[256,1024]{1,0:T(8,128)(2,1)S(1)}, bf16[256,1024]{1,0:T(8,128)(2,1)S(1)}, u32[]{:S(2)}, u32[]{:S(2)}) collective-permute-start(bf16[256,1024]{1,0:T(8,128)(2,1)S(1)} %convolution_convert_fusion), channel_id=1, source_target_pairs={{0,1},{1,0},{2,3},{3,2},{4,5},{5,4},{6,7},{7,6},{8,9},{9,8},{10,11... | collective-permute-start | bytes 1572872 | tf_op jit(solution)/shard_map/ppermute | solution.py:302
  31.6 9.4 %copy-start.3 = (s32[16]{0:T(128)S(1)}, s32[16]{0:T(128)}, u32[]{:S(2)}) copy-start(s32[16]{0:T(128)} %param.11) | copy-start | bytes 196
  33.6 17.2 %all-to-all-start.1 = ((bf16[16,16,1024]{2,1,0:T(8,128)(2,1)}), bf16[16,16,1024]{2,1,0:T(8,128)(2,1)S(1)}, u32[]{:S(2)}, u32[]{:S(2)}) async-start(bf16[16,16,1024]{2,1,0:T(8,128)(2,1)} %bitcast.7), calls=%async_computation.1 | async-start | bytes 1048576 | tf_op jit(solution)/shard_map/all_to_all | solution.py:21
  65.9 0.6 copy-start.2
  80.6 6.3 %collective-permute-start.1 = (bf16[256,1152]{1,0:T(8,128)(2,1)S(1)}, bf16[256,1152]{1,0:T(8,128)(2,1)S(1)}, u32[]{:S(2)}, u32[]{:S(2)}) collective-permute-start(bf16[256,1152]{1,0:T(8,128)(2,1)S(1)} %bitcast.45), channel_id=1, source_target_pairs={{0,1},{1,0},{2,3},{3,2},{4,5},{5,4},{6,7},{7,6},{8,9},{9,8},{10,11... | collective-permute-start | bytes 1769480 | tf_op jit(solution)/shard_map/ppermute | solution.py:322
  92.9 7.5 %copy-start.1 = (bf16[16,96,128]{2,1,0:T(8,128)(2,1)S(1)}, bf16[16,96,128]{2,1,0:T(8,128)(2,1)}, u32[]{:S(2)}) copy-start(bf16[16,96,128]{2,1,0:T(8,128)(2,1)} %param.6) | copy-start | bytes 1179652
  92.9 81.9 %all-to-all-start.4 = ((bf16[256,2,2304]{2,1,0:T(2,128)(2,1)}), bf16[256,2,2304]{2,1,0:T(2,128)(2,1)S(1)}, u32[]{:S(2)}, u32[]{:S(2)}) async-start(bf16[256,2,2304]{2,1,0:T(2,128)(2,1)} %operator_blocks.1), calls=%async_computation.4 | async-start | bytes 4718592 | tf_op jit(solution)/shard_map/all_to_all | solution.py:21
  100.4 57.9 %collective-permute-start.2 = (bf16[16,96,128]{2,1,0:T(8,128)(2,1)S(1)}, bf16[16,96,128]{2,1,0:T(8,128)(2,1)}, u32[]{:S(2)}, u32[]{:S(2)}) collective-permute-start(bf16[16,96,128]{2,1,0:T(8,128)(2,1)S(1)} %copy-done.1), channel_id=1, source_target_pairs={{0,8},{8,16},{16,24},{24,32},{32,40},{40,48},{48,56},{56,64},{64,7... | collective-permute-start | bytes 1179656 | tf_op jit(solution)/shard_map/ppermute | solution.py:123
  103.9 57.5 %collective-permute-start.3 = (bf16[16,96,128]{2,1,0:T(8,128)(2,1)S(1)}, bf16[16,96,128]{2,1,0:T(8,128)(2,1)}, u32[]{:S(2)}, u32[]{:S(2)}) collective-permute-start(bf16[16,96,128]{2,1,0:T(8,128)(2,1)S(1)} %copy-done.1), channel_id=1, source_target_pairs={{8,0},{16,8},{24,16},{32,24},{40,32},{48,40},{56,48},{64,56},{72,6... | collective-permute-start | bytes 1179656 | tf_op jit(solution)/shard_map/ppermute | solution.py:124
  166.4 5.0 %collective-permute-start.10 = (bf16[2,96,128]{2,1,0:T(8,128)(2,1)S(1)}, bf16[2,96,128]{2,1,0:T(8,128)(2,1)S(1)}, u32[]{:S(2)}, u32[]{:S(2)}) collective-permute-start(bf16[2,96,128]{2,1,0:T(8,128)(2,1)S(1)} %get-tuple-element.8), channel_id=1, source_target_pairs={{0,7},{1,6},{2,5},{3,4},{4,3},{5,2},{6,1},{7,0},{8,15},{9,14},{10,... | collective-permute-start | bytes 147464 | tf_op jit(solution)/shard_map/ppermute | solution.py:115
  168.4 6.0 %collective-permute-start.4 = (bf16[2,96,128]{2,1,0:T(8,128)(2,1)S(1)}, bf16[2,96,128]{2,1,0:T(8,128)(2,1)S(1)}, u32[]{:S(2)}, u32[]{:S(2)}) collective-permute-start(bf16[2,96,128]{2,1,0:T(8,128)(2,1)S(1)} %get-tuple-element.14), channel_id=1, source_target_pairs={{0,1},{1,0},{2,3},{3,2},{4,5},{5,4},{6,7},{7,6},{8,9},{9,8},{10,11... | collective-permute-start | bytes 147464 | tf_op jit(solution)/shard_map/ppermute | solution.py:115
  169.4 5.6 %collective-permute-start.5 = (bf16[2,96,128]{2,1,0:T(8,128)(2,1)}, bf16[2,96,128]{2,1,0:T(8,128)(2,1)S(1)}, u32[]{:S(2)}, u32[]{:S(2)}) collective-permute-start(bf16[2,96,128]{2,1,0:T(8,128)(2,1)} %get-tuple-element.13), channel_id=1, source_target_pairs={{0,2},{1,3},{2,0},{3,1},{4,6},{5,7},{6,4},{7,5},{8,10},{9,11},{10,... | collective-permute-start | bytes 147464 | tf_op jit(solution)/shard_map/ppermute | solution.py:115
  169.4 5.6 %collective-permute-start.6 = (bf16[2,96,128]{2,1,0:T(8,128)(2,1)}, bf16[2,96,128]{2,1,0:T(8,128)(2,1)S(1)}, u32[]{:S(2)}, u32[]{:S(2)}) collective-permute-start(bf16[2,96,128]{2,1,0:T(8,128)(2,1)} %get-tuple-element.12), channel_id=1, source_target_pairs={{0,3},{1,2},{2,1},{3,0},{4,7},{5,6},{6,5},{7,4},{8,11},{9,10},{10,... | collective-permute-start | bytes 147464 | tf_op jit(solution)/shard_map/ppermute | solution.py:115
  170.8 6.3 %collective-permute-start.7 = (bf16[2,96,128]{2,1,0:T(8,128)(2,1)}, bf16[2,96,128]{2,1,0:T(8,128)(2,1)S(1)}, u32[]{:S(2)}, u32[]{:S(2)}) collective-permute-start(bf16[2,96,128]{2,1,0:T(8,128)(2,1)} %get-tuple-element.11), channel_id=1, source_target_pairs={{0,4},{1,5},{2,6},{3,7},{4,0},{5,1},{6,2},{7,3},{8,12},{9,13},{10,... | collective-permute-start | bytes 147464 | tf_op jit(solution)/shard_map/ppermute | solution.py:115
  171.5 6.3 %collective-permute-start.8 = (bf16[2,96,128]{2,1,0:T(8,128)(2,1)}, bf16[2,96,128]{2,1,0:T(8,128)(2,1)S(1)}, u32[]{:S(2)}, u32[]{:S(2)}) collective-permute-start(bf16[2,96,128]{2,1,0:T(8,128)(2,1)} %get-tuple-element.10), channel_id=1, source_target_pairs={{0,5},{1,4},{2,7},{3,6},{4,1},{5,0},{6,3},{7,2},{8,13},{9,12},{10,... | collective-permute-start | bytes 147464 | tf_op jit(solution)/shard_map/ppermute | solution.py:115
  174.4 5.5 %collective-permute-start.9 = (bf16[2,96,128]{2,1,0:T(8,128)(2,1)}, bf16[2,96,128]{2,1,0:T(8,128)(2,1)S(1)}, u32[]{:S(2)}, u32[]{:S(2)}) collective-permute-start(bf16[2,96,128]{2,1,0:T(8,128)(2,1)} %get-tuple-element.9), channel_id=1, source_target_pairs={{0,6},{1,7},{2,4},{3,5},{4,2},{5,3},{6,0},{7,1},{8,14},{9,15},{10,... | collective-permute-start | bytes 147464 | tf_op jit(solution)/shard_map/ppermute | solution.py:115
  186.0 12.3 %all-to-all-start.5 = ((bf16[8,2,96,128]{3,2,1,0:T(8,128)(2,1)}), bf16[8,2,96,128]{3,2,1,0:T(8,128)(2,1)S(1)}, u32[]{:S(2)}, u32[]{:S(2)}) async-start(bf16[8,2,96,128]{3,2,1,0:T(8,128)(2,1)} %propagate.1), calls=%async_computation.5 | async-start | bytes 786432 | tf_op jit(solution)/shard_map/all_to_all | solution.py:21
